TPU v7x, 128 devices: a whole 4x4x4 slice. The times are simulated.
128 devices in a mesh: gx: 16 (over z, y), gy: 8 (over x, core).
Axes of the slice: x: 4, y: 4, z: 4, core: 2. Of those that a mesh axis runs over, the one named last changes fastest.
Arguments:
- pumping: float32 [16, 4, 128, 1024], P(None, None, 'gx', 'gy'), may hold values from -1080 to 1080
- conductivity: float32 [4, 128, 1024], P(None, 'gx', 'gy'), may hold values from 0.2 to 5
- capacity: float32 [4, 128, 1024], P(None, 'gx', 'gy'), may hold values from 1 to 10
Outputs:
- solution: float32 [16, 4, 128, 1024], P(None, None, 'gx', 'gy')
- residual: float32 [16, 4, 128, 1024], P(None, None, 'gx', 'gy')
All inputs are finite; a program needn't handle non-finite values.
Results may differ from a plain program's by a relative error of at most 0.0035.
Values sent between devices are 32-bit elements; how exact they have to be, the bound alone decides.
A program may use at most 64 MiB of HBM per device.

v0:
```python
import jax
import jax.numpy as jnp
from jax import lax
from jax.sharding import PartitionSpec as P

RHS = 16
S = 4
CYCLES = 5
BASIS = 80


def padded_2(array, sides, width):
    for axis, dim in sides:
        devices, length = (lax.axis_size(axis), array.shape[dim])
        up = [(i, (i + 1) % devices) for i in range(devices - 1)]
        down = [(j, i) for i, j in up]
        last = lax.slice_in_dim(array, length - width, length, axis=dim)
        leading = lax.slice_in_dim(array, 0, width, axis=dim)
        before = lax.ppermute(last, axis, up)
        after = lax.ppermute(leading, axis, down)
        array = jnp.concatenate([before, array, after], axis=dim)
    return array


def face_terms(padded, storage):
    core = padded[1:-1, 1:-1, 1:-1]
    terms = (
        (core + padded[:-2, 1:-1, 1:-1]) * 0.5,
        (core + padded[2:, 1:-1, 1:-1]) * 0.5,
        (core + padded[1:-1, :-2, 1:-1]) * 0.5,
        (core + padded[1:-1, 2:, 1:-1]) * 0.5,
        (core + padded[1:-1, 1:-1, :-2]) * 0.5,
        (core + padded[1:-1, 1:-1, 2:]) * 0.5,
    )
    diagonal = storage + terms[0] + terms[1] + terms[2] + terms[3] + terms[4] + terms[5]
    return (terms, diagonal)


def apply_off(padded, terms):
    total = terms[0] * padded[:, :-2, 1:-1, 1:-1] + terms[1] * padded[:, 2:, 1:-1, 1:-1]
    total = total + terms[2] * padded[:, 1:-1, :-2, 1:-1] + terms[3] * padded[:, 1:-1, 2:, 1:-1]
    total = total + terms[4] * padded[:, 1:-1, 1:-1, :-2] + terms[5] * padded[:, 1:-1, 1:-1, 2:]
    return total


def small_solve(gram_all):
    shift_matrix = jnp.eye(BASIS, BASIS - RHS, dtype=jnp.float32) + jnp.eye(
        BASIS, BASIS - RHS, k=-RHS, dtype=jnp.float32
    )
    first_block = jnp.eye(BASIS, RHS, dtype=jnp.float32)
    hp = lax.Precision.HIGHEST
    gram_shift = jnp.dot(gram_all, shift_matrix, precision=hp)
    normal = jnp.dot(shift_matrix.T, gram_shift, precision=hp)
    right_side = jnp.dot(gram_shift.T, first_block, precision=hp)
    lower = jnp.linalg.cholesky(normal)
    y = jax.scipy.linalg.cho_solve((lower, True), right_side)
    coeffs = first_block - jnp.dot(shift_matrix, y, precision=hp)
    return (y, coeffs)


def shards(pumping, conductivity, capacity):
    hp = lax.Precision.HIGHEST
    shape = pumping.shape
    cond_halo = padded_2(conductivity, (("gx", 1), ("gy", 2)), 1)
    cond_pad = jnp.pad(cond_halo, ((1, 1), (0, 0), (0, 0)))
    terms, diagonal = face_terms(cond_pad, capacity)
    solution = jnp.zeros(shape, jnp.float32)
    residual = pumping / diagonal
    for restart in range(CYCLES):
        blocks = [residual]
        for k in range(S):
            bordered = padded_2(blocks[-1], (("gx", 2), ("gy", 3)), 1)
            padded = jnp.pad(bordered, ((0, 0), (1, 1), (0, 0), (0, 0)))
            blocks.append(-apply_off(padded, terms) / diagonal)
        stacked = jnp.concatenate(blocks, 0).reshape(BASIS, -1)
        local_gram = jnp.dot(stacked, stacked.T, precision=hp)
        gram_all = lax.psum(local_gram, ("gx", "gy"))
        y, coeffs = small_solve(gram_all)
        solution = solution + jnp.dot(y.T, stacked[: BASIS - RHS], precision=hp).reshape(shape)
        residual = jnp.dot(coeffs.T, stacked, precision=hp).reshape(shape)
    return (solution, residual)


def solution(mesh):
    return jax.shard_map(
        shards,
        mesh=mesh,
        in_specs=(P(None, None, "gx", "gy"), P(None, "gx", "gy"), P(None, "gx", "gy")),
        out_specs=(P(None, None, "gx", "gy"), P(None, None, "gx", "gy")),
        check_vma=False,
    )
```

profile of v0, /device:TPU:1, one launch (start us, length us, event | category | flops | bytes accessed | tf_op | source)
XLA Modules:
  0.0 885.2 jit_solution(18000092713170605420)
XLA Ops:
  1.4 4.0 collective-permute-start
  10.6 5.1 collective-permute-start.2
  39.3 4.4 collective-permute-done.7
  44.5 4.6 collective-permute-start.8
  61.1 4.4 collective-permute-done.11
  66.3 3.7 collective-permute-start.12
  82.1 4.4 collective-permute-done.15
  103.1 4.4 collective-permute-done.19
  109.9 68.0 %psum.35 = f32[80,80]{1,0:T(8,128)S(1)} all-reduce(f32[80,80]{1,0:T(8,128)S(1)} %convolution_bitcast_fusion.4), channel_id=1, replica_groups=mesh['gx'=16,'gy'=8] {'gx','gy'}, use_global_device_ids=true, to_apply=%region_0.1 | all-reduce | flops 6400 | bytes 51200 | tf_op jit(solution)/shard_map/psum | solution.py:77
  179.8 5.8 cholesky.89
  187.0 4.9 custom-call.11
  201.0 4.9 collective-permute-start.22
  210.0 4.4 collective-permute-done.23
  230.1 4.4 collective-permute-done.27
  235.3 4.8 collective-permute-start.28
  252.4 4.4 collective-permute-done.31
  273.4 4.4 collective-permute-done.35
  280.8 66.5 %psum.36 = f32[80,80]{1,0:T(8,128)} all-reduce(f32[80,80]{1,0:T(8,128)} %convolution_bitcast_fusion.3), channel_id=1, replica_groups=mesh['gx'=16,'gy'=8] {'gx','gy'}, use_global_device_ids=true, to_apply=%region_3.6 | all-reduce | flops 6400 | bytes 51200 | tf_op jit(solution)/shard_map/psum | solution.py:77
  352.3 5.8 cholesky.100
  359.5 4.9 custom-call.12
  374.5 4.3 collective-permute-start.38
  382.9 4.4 collective-permute-done.39
  403.0 4.4 collective-permute-done.43
  408.2 5.4 collective-permute-start.44
  425.6 4.4 collective-permute-done.47
  446.6 4.4 collective-permute-done.51
  454.5 66.5 %psum.37 = f32[80,80]{1,0:T(8,128)S(1)} all-reduce(f32[80,80]{1,0:T(8,128)S(1)} %convolution_bitcast_fusion.2), channel_id=1, replica_groups=mesh['gx'=16,'gy'=8] {'gx','gy'}, use_global_device_ids=true, to_apply=%region_4.7 | all-reduce | flops 6400 | bytes 51200 | tf_op jit(solution)/shard_map/psum | solution.py:77
  525.3 5.8 cholesky.111
  532.4 4.9 custom-call.13
  547.1 4.8 collective-permute-start.54
  555.9 4.4 collective-permute-done.55
  575.9 4.4 collective-permute-done.59
  581.1 4.7 collective-permute-start.60
  597.8 4.4 collective-permute-done.63
  619.3 3.9 collective-permute-done.67
  626.7 66.7 %psum.38 = f32[80,80]{1,0:T(8,128)S(1)} all-reduce(f32[80,80]{1,0:T(8,128)S(1)} %convolution_bitcast_fusion.1), channel_id=1, replica_groups=mesh['gx'=16,'gy'=8] {'gx','gy'}, use_global_device_ids=true, to_apply=%region_5.8 | all-reduce | flops 6400 | bytes 51200 | tf_op jit(solution)/shard_map/psum | solution.py:77
  697.7 5.8 cholesky.122
  704.9 4.9 custom-call.14
  719.4 5.7 collective-permute-start.70
  729.1 4.4 collective-permute-done.71
  748.7 4.4 collective-permute-done.75
  753.9 5.0 collective-permute-start.76
  771.0 4.4 collective-permute-done.79
  776.2 4.5 collective-permute-start.80
  792.7 4.4 collective-permute-done.83
  799.5 66.5 %psum.39 = f32[80,80]{1,0:T(8,128)S(1)} all-reduce(f32[80,80]{1,0:T(8,128)S(1)} %convolution_bitcast_fusion), channel_id=1, replica_groups=mesh['gx'=16,'gy'=8] {'gx','gy'}, use_global_device_ids=true, to_apply=%region_6.9 | all-reduce | flops 6400 | bytes 51200 | tf_op jit(solution)/shard_map/psum | solution.py:77
  867.9 5.8 cholesky.133
  875.1 4.9 custom-call.15
  (373 shorter events, 345.4 us)
Async XLA Ops:
  1.4 5.3 collective-permute-start
  10.6 7.0 collective-permute-start.2
  32.0 7.3 collective-permute-start.6
  35.3 8.4 collective-permute-start.7
  44.5 5.9 collective-permute-start.8
  54.2 6.9 collective-permute-start.10
  57.1 8.4 collective-permute-start.11
  75.2 6.9 collective-permute-start.14
  78.1 8.4 collective-permute-start.15
  96.2 6.9 collective-permute-start.18
  99.1 8.4 collective-permute-start.19
  201.0 8.9 %collective-permute-start.22 = (f32[16,4,10,1]{3,0,2,1:T(8,128)S(1)}, f32[16,4,10,1]{3,0,2,1:T(8,128)S(1)}, u32[]{:S(2)}, u32[]{:S(2)}) collective-permute-start(f32[16,4,10,1]{3,0,2,1:T(8,128)S(1)} %get-tuple-element.77), channel_id=1, source_target_pairs={{0,1},{1,2},{2,3},{3,4},{4,5},{5,6},{6,7},{8,9},{9,10},{10,11},{11... | collective-permute-start | bytes 7688 | tf_op jit(solution)/shard_map/ppermute | solution.py:19
  206.0 8.4 collective-permute-start.23
  222.8 7.3 collective-permute-start.26
  226.1 8.4 collective-permute-start.27
  235.3 6.1 collective-permute-start.28
  245.2 7.2 collective-permute-start.30
  248.4 8.4 collective-permute-start.31
  266.2 7.2 collective-permute-start.34
  269.4 8.4 collective-permute-start.35
  374.5 8.4 collective-permute-start.38
  378.9 8.4 collective-permute-start.39
  396.1 6.9 collective-permute-start.42
  399.0 8.4 collective-permute-start.43
  408.2 6.7 collective-permute-start.44
  418.5 7.2 collective-permute-start.46
  421.6 8.4 collective-permute-start.47
  439.7 6.9 collective-permute-start.50
  442.6 8.4 collective-permute-start.51
  547.1 8.8 collective-permute-start.54
  551.9 8.4 collective-permute-start.55
  568.8 7.1 collective-permute-start.58
  571.9 8.4 collective-permute-start.59
  581.1 6.0 collective-permute-start.60
  590.9 6.9 collective-permute-start.62
  593.8 8.4 collective-permute-start.63
  611.9 7.4 collective-permute-start.66
  614.8 8.4 collective-permute-start.67
  719.4 9.7 %collective-permute-start.70 = (f32[16,4,10,1]{3,0,2,1:T(8,128)S(1)}, f32[16,4,10,1]{3,0,2,1:T(8,128)S(1)}, u32[]{:S(2)}, u32[]{:S(2)}) collective-permute-start(f32[16,4,10,1]{3,0,2,1:T(8,128)S(1)} %get-tuple-element.53), channel_id=1, source_target_pairs={{0,1},{1,2},{2,3},{3,4},{4,5},{5,6},{6,7},{8,9},{9,10},{10,11},{11... | collective-permute-start | bytes 7688 | tf_op jit(solution)/shard_map/ppermute | solution.py:19
  725.1 8.4 collective-permute-start.71
  741.5 7.2 collective-permute-start.74
  744.7 8.4 collective-permute-start.75
  753.9 7.6 collective-permute-start.76
  764.1 6.9 collective-permute-start.78
  767.0 8.4 collective-permute-start.79
  776.2 7.2 collective-permute-start.80
  785.8 6.9 collective-permute-start.82
  788.7 8.4 collective-permute-start.83
  (48 other events, 613.6 us)
where the time goes:
time: 894 us; the launch traced here: 885 us
  blocking collectives  334 us (37%)
  starting transfers between devices  214 us (24%)
  waiting for transfers between devices  190 us (21%)
  other arithmetic  80.5 us (9%)
  matrix products  34 us (4%)
  local copies, waits for them, and re-layouts  30.1 us (3%)
    psum x5, blocking collectives, shards(): gram_all = lax.psum(local_gram, ('gx', 'gy'))  334 us
    ppermute x42, waiting for transfers between devices, padded_2(): after = lax.ppermute(leading, axis, down)  157 us
    ppermute x42, starting transfers between devices, padded_2(): before = lax.ppermute(last, axis, up)  145 us
    ppermute x42, starting transfers between devices, padded_2(): after = lax.ppermute(leading, axis, down)  68.6 us
    another operation x15, other arithmetic, small_solve(): lower = jnp.linalg.cholesky(normal)  32.6 us
    ppermute x42, waiting for transfers between devices, padded_2(): before = lax.ppermute(last, axis, up)  32.5 us
    another operation x10, other arithmetic, small_solve(): y = jax.scipy.linalg.cho_solve((lower, True), right_side)  27.7 us
    unnamed x46, local copies, waits for them, and re-layouts  18.2 us
  transfers between devices with their start and end apart: 84, of which 61 were waited for; matrix products, arithmetic and copies ran while one was open for 2% of the time, Pallas kernels for 0%

commit v1 on v0

--- a/solution.py
+++ b/solution.py
@@ -20,6 +20,22 @@
         after = lax.ppermute(leading, axis, down)
         array = jnp.concatenate([before, array, after], axis=dim)
     return array
+
+
+def halo_4(array):
+    out = {}
+    for axis, dim in (("gx", 2), ("gy", 3)):
+        devices, length = (lax.axis_size(axis), array.shape[dim])
+        up = [(i, (i + 1) % devices) for i in range(devices - 1)]
+        down = [(j, i) for i, j in up]
+        last = lax.slice_in_dim(array, length - 1, length, axis=dim)
+        leading = lax.slice_in_dim(array, 0, 1, axis=dim)
+        out[axis] = (lax.ppermute(last, axis, up), lax.ppermute(leading, axis, down))
+    xb, xa = out["gx"]
+    yb, ya = out["gy"]
+    rows = jnp.concatenate([xb, array, xa], axis=2)
+    zero_pad = ((0, 0), (0, 0), (1, 1), (0, 0))
+    return jnp.concatenate([jnp.pad(yb, zero_pad), rows, jnp.pad(ya, zero_pad)], axis=3)
 
 
 def face_terms(padded, storage):
@@ -69,7 +85,7 @@
     for restart in range(CYCLES):
         blocks = [residual]
         for k in range(S):
-            bordered = padded_2(blocks[-1], (("gx", 2), ("gy", 3)), 1)
+            bordered = halo_4(blocks[-1])
             padded = jnp.pad(bordered, ((0, 0), (1, 1), (0, 0), (0, 0)))
             blocks.append(-apply_off(padded, terms) / diagonal)
         stacked = jnp.concatenate(blocks, 0).reshape(BASIS, -1)

time: 894 us -> 827 us (0.925)
  waiting for transfers between devices: 190 us -> 99.7 us
  blocking collectives: 334 us -> 371 us
    ppermute x0 -> x80, starting transfers between devices: none -> 194 us  [the longest x40 123 us: halo_4(): lax.ppermute(last, axis, up)]
    ppermute x42 -> x2, waiting for transfers between devices: 157 us -> 6.31 us  [padded_2(): after = lax.ppermute(leading, axis, down)]
    ppermute x42 -> x2, starting transfers between devices: 145 us -> 9.12 us  [padded_2(): before = lax.ppermute(last, axis, up)]
    ppermute x0 -> x80, waiting for transfers between devices: none -> 93.4 us  [the longest x40 81.7 us: halo_4(): lax.ppermute(leading, axis, down)]
    ppermute x42 -> x2, starting transfers between devices: 68.6 us -> 3.21 us  [padded_2(): after = lax.ppermute(leading, axis, down)]
    psum x5, blocking collectives: 334 us -> 371 us  [shards(): gram_all = lax.psum(local_gram, ('gx', 'gy'))]
    ppermute x42 -> x2, waiting for transfers between devices: 32.5 us -> 0.01 us  [padded_2(): before = lax.ppermute(last, axis, up)]
    unnamed x46 -> x26, local copies, waits for them, and re-layouts: 18.2 us -> 17.6 us
  transfers between devices with their start and end apart: 84 -> 84, of which waited for: 61 -> 34; matrix products, arithmetic and copies ran while one was open for 2% -> 2% of each run, Pallas kernels for 0% -> 0%
where the time goes in v1:
time: 827 us; the launch traced here: 819 us
  blocking collectives  371 us (45%)
  starting transfers between devices  206 us (25%)
  waiting for transfers between devices  99.7 us (12%)
  other arithmetic  80.1 us (10%)
  local copies, waits for them, and re-layouts  29.8 us (4%)
  matrix products  28.9 us (3%)
    psum x5, blocking collectives, shards(): gram_all = lax.psum(local_gram, ('gx', 'gy'))  371 us
    ppermute x40, starting transfers between devices, halo_4(): lax.ppermute(last, axis, up)  123 us
    ppermute x40, waiting for transfers between devices, halo_4(): lax.ppermute(leading, axis, down)  81.7 us
    ppermute x40, starting transfers between devices, halo_4(): lax.ppermute(leading, axis, down)  71.1 us
    another operation x15, other arithmetic, small_solve(): lower = jnp.linalg.cholesky(normal)  32.6 us
    another operation x10, other arithmetic, small_solve(): y = jax.scipy.linalg.cho_solve((lower, True), right_side)  27.7 us
    unnamed x26, local copies, waits for them, and re-layouts  17.6 us
  transfers between devices with their start and end apart: 84, of which 34 were waited for; matrix products, arithmetic and copies ran while one was open for 2% of the time, Pallas kernels for 0%

profile of v1, /device:TPU:1, one launch (start us, length us, event | category | flops | bytes accessed | tf_op | source)
XLA Modules:
  0.0 819.0 jit_solution(14355877820562168291)
XLA Ops:
  1.4 4.0 collective-permute-start
  10.6 5.1 collective-permute-start.2
  34.1 4.4 collective-permute-done.7
  39.3 4.3 collective-permute-start.9
  50.4 4.4 collective-permute-done.11
  55.6 5.2 collective-permute-start.13
  67.6 4.4 collective-permute-done.15
  72.9 4.3 collective-permute-start.17
  83.9 4.4 collective-permute-done.19
  90.7 75.5 %psum.35 = f32[80,80]{1,0:T(8,128)S(1)} all-reduce(f32[80,80]{1,0:T(8,128)S(1)} %convolution_bitcast_fusion.4), channel_id=1, replica_groups=mesh['gx'=16,'gy'=8] {'gx','gy'}, use_global_device_ids=true, to_apply=%region_0.1 | all-reduce | flops 6400 | bytes 51200 | tf_op jit(solution)/shard_map/psum | solution.py:93
  168.1 5.8 cholesky.89
  175.3 4.9 custom-call.11
  192.7 4.4 collective-permute-done.23
  197.9 4.3 collective-permute-start.25
  209.0 4.4 collective-permute-done.27
  214.2 4.3 collective-permute-start.29
  225.2 4.4 collective-permute-done.31
  230.5 4.3 collective-permute-start.33
  241.5 4.4 collective-permute-done.35
  249.4 73.8 %psum.36 = f32[80,80]{1,0:T(8,128)S(1)} all-reduce(f32[80,80]{1,0:T(8,128)S(1)} %convolution_bitcast_fusion.3), channel_id=1, replica_groups=mesh['gx'=16,'gy'=8] {'gx','gy'}, use_global_device_ids=true, to_apply=%region_3.6 | all-reduce | flops 6400 | bytes 51200 | tf_op jit(solution)/shard_map/psum | solution.py:93
  327.5 5.8 cholesky.100
  334.7 4.9 custom-call.12
  352.9 4.4 collective-permute-done.39
  358.2 4.3 collective-permute-start.41
  369.2 4.4 collective-permute-done.43
  374.4 4.3 collective-permute-start.45
  385.5 4.4 collective-permute-done.47
  390.9 4.5 collective-permute-start.49
  409.9 73.9 %psum.37 = f32[80,80]{1,0:T(8,128)S(1)} all-reduce(f32[80,80]{1,0:T(8,128)S(1)} %convolution_bitcast_fusion.2), channel_id=1, replica_groups=mesh['gx'=16,'gy'=8] {'gx','gy'}, use_global_device_ids=true, to_apply=%region_4.7 | all-reduce | flops 6400 | bytes 51200 | tf_op jit(solution)/shard_map/psum | solution.py:93
  488.1 5.8 cholesky.111
  495.3 4.9 custom-call.13
  506.5 4.3 collective-permute-start.52
  514.4 4.1 collective-permute-done.55
  519.5 4.3 collective-permute-start.57
  535.8 4.3 collective-permute-start.61
  546.9 4.2 collective-permute-done.63
  552.1 4.3 collective-permute-start.65
  569.8 73.8 %psum.38 = f32[80,80]{1,0:T(8,128)S(1)} all-reduce(f32[80,80]{1,0:T(8,128)S(1)} %convolution_bitcast_fusion.1), channel_id=1, replica_groups=mesh['gx'=16,'gy'=8] {'gx','gy'}, use_global_device_ids=true, to_apply=%region_5.8 | all-reduce | flops 6400 | bytes 51200 | tf_op jit(solution)/shard_map/psum | solution.py:93
  645.5 5.8 cholesky.122
  652.7 4.9 custom-call.14
  662.6 4.1 collective-permute-start.68
  670.0 4.4 collective-permute-done.71
  675.4 4.3 collective-permute-start.73
  691.6 4.3 collective-permute-start.77
  707.9 4.3 collective-permute-start.81
  725.7 74.1 %psum.39 = f32[80,80]{1,0:T(8,128)S(1)} all-reduce(f32[80,80]{1,0:T(8,128)S(1)} %convolution_bitcast_fusion), channel_id=1, replica_groups=mesh['gx'=16,'gy'=8] {'gx','gy'}, use_global_device_ids=true, to_apply=%region_6.9 | all-reduce | flops 6400 | bytes 51200 | tf_op jit(solution)/shard_map/psum | solution.py:93
  801.7 5.8 cholesky.133
  808.9 4.9 custom-call.15
  (373 shorter events, 247.4 us)
Async XLA Ops:
  23.9 14.6 %collective-permute-start.5 = (f32[16,4,1,128]{3,0,2,1:T(8,128)S(1)}, f32[16,4,1,128]{3,0,2,1:T(8,128)S(1)}, u32[]{:S(2)}, u32[]{:S(2)}) collective-permute-start(f32[16,4,1,128]{3,0,2,1:T(8,128)S(1)} %get-tuple-element.125), channel_id=1, source_target_pairs={{0,8},{8,16},{16,24},{24,32},{32,40},{40,48},{48,56},{56,64},{64,7... | collective-permute-start | bytes 98312 | tf_op jit(solution)/shard_map/ppermute | solution.py:33
  27.1 11.4 %collective-permute-start.6 = (f32[16,4,1,128]{3,0,2,1:T(8,128)S(1)}, f32[16,4,1,128]{3,0,2,1:T(8,128)S(1)}, u32[]{:S(2)}, u32[]{:S(2)}) collective-permute-start(f32[16,4,1,128]{3,0,2,1:T(8,128)S(1)} %get-tuple-element.126), channel_id=1, source_target_pairs={{8,0},{16,8},{24,16},{32,24},{40,32},{48,40},{56,48},{64,56},{72,6... | collective-permute-start | bytes 98312 | tf_op jit(solution)/shard_map/ppermute | solution.py:33
  39.3 15.5 %collective-permute-start.9 = (f32[16,4,1,128]{3,0,2,1:T(8,128)S(1)}, f32[16,4,1,128]{3,0,2,1:T(8,128)S(1)}, u32[]{:S(2)}, u32[]{:S(2)}) collective-permute-start(f32[16,4,1,128]{3,0,2,1:T(8,128)S(1)} %get-tuple-element.121), channel_id=1, source_target_pairs={{0,8},{8,16},{16,24},{24,32},{32,40},{40,48},{48,56},{56,64},{64,7... | collective-permute-start | bytes 98312 | tf_op jit(solution)/shard_map/ppermute | solution.py:33
  43.6 11.2 %collective-permute-start.10 = (f32[16,4,1,128]{3,0,2,1:T(8,128)S(1)}, f32[16,4,1,128]{3,0,2,1:T(8,128)S(1)}, u32[]{:S(2)}, u32[]{:S(2)}) collective-permute-start(f32[16,4,1,128]{3,0,2,1:T(8,128)S(1)} %get-tuple-element.122), channel_id=1, source_target_pairs={{8,0},{16,8},{24,16},{32,24},{40,32},{48,40},{56,48},{64,56},{72,6... | collective-permute-start | bytes 98312 | tf_op jit(solution)/shard_map/ppermute | solution.py:33
  55.6 16.4 %collective-permute-start.13 = (f32[16,4,1,128]{3,0,2,1:T(8,128)S(1)}, f32[16,4,1,128]{3,0,2,1:T(8,128)S(1)}, u32[]{:S(2)}, u32[]{:S(2)}) collective-permute-start(f32[16,4,1,128]{3,0,2,1:T(8,128)S(1)} %get-tuple-element.117), channel_id=1, source_target_pairs={{0,8},{8,16},{16,24},{24,32},{32,40},{40,48},{48,56},{56,64},{64,7... | collective-permute-start | bytes 98312 | tf_op jit(solution)/shard_map/ppermute | solution.py:33
  60.8 11.2 %collective-permute-start.14 = (f32[16,4,1,128]{3,0,2,1:T(8,128)S(1)}, f32[16,4,1,128]{3,0,2,1:T(8,128)S(1)}, u32[]{:S(2)}, u32[]{:S(2)}) collective-permute-start(f32[16,4,1,128]{3,0,2,1:T(8,128)S(1)} %get-tuple-element.118), channel_id=1, source_target_pairs={{8,0},{16,8},{24,16},{32,24},{40,32},{48,40},{56,48},{64,56},{72,6... | collective-permute-start | bytes 98312 | tf_op jit(solution)/shard_map/ppermute | solution.py:33
  72.9 15.3 %collective-permute-start.17 = (f32[16,4,1,128]{3,0,2,1:T(8,128)S(1)}, f32[16,4,1,128]{3,0,2,1:T(8,128)S(1)}, u32[]{:S(2)}, u32[]{:S(2)}) collective-permute-start(f32[16,4,1,128]{3,0,2,1:T(8,128)S(1)} %get-tuple-element.113), channel_id=1, source_target_pairs={{0,8},{8,16},{16,24},{24,32},{32,40},{40,48},{48,56},{56,64},{64,7... | collective-permute-start | bytes 98312 | tf_op jit(solution)/shard_map/ppermute | solution.py:33
  77.2 11.1 %collective-permute-start.18 = (f32[16,4,1,128]{3,0,2,1:T(8,128)S(1)}, f32[16,4,1,128]{3,0,2,1:T(8,128)S(1)}, u32[]{:S(2)}, u32[]{:S(2)}) collective-permute-start(f32[16,4,1,128]{3,0,2,1:T(8,128)S(1)} %get-tuple-element.114), channel_id=1, source_target_pairs={{8,0},{16,8},{24,16},{32,24},{40,32},{48,40},{56,48},{64,56},{72,6... | collective-permute-start | bytes 98312 | tf_op jit(solution)/shard_map/ppermute | solution.py:33
  182.4 14.7 %collective-permute-start.21 = (f32[16,4,1,128]{3,0,2,1:T(8,128)S(1)}, f32[16,4,1,128]{3,0,2,1:T(8,128)S(1)}, u32[]{:S(2)}, u32[]{:S(2)}) collective-permute-start(f32[16,4,1,128]{3,0,2,1:T(8,128)S(1)} %get-tuple-element.109), channel_id=1, source_target_pairs={{0,8},{8,16},{16,24},{24,32},{32,40},{40,48},{48,56},{56,64},{64,7... | collective-permute-start | bytes 98312 | tf_op jit(solution)/shard_map/ppermute | solution.py:33
  184.1 13.0 %collective-permute-start.22 = (f32[16,4,1,128]{3,0,2,1:T(8,128)S(1)}, f32[16,4,1,128]{3,0,2,1:T(8,128)S(1)}, u32[]{:S(2)}, u32[]{:S(2)}) collective-permute-start(f32[16,4,1,128]{3,0,2,1:T(8,128)S(1)} %get-tuple-element.110), channel_id=1, source_target_pairs={{8,0},{16,8},{24,16},{32,24},{40,32},{48,40},{56,48},{64,56},{72,6... | collective-permute-start | bytes 98312 | tf_op jit(solution)/shard_map/ppermute | solution.py:33
  197.9 15.5 %collective-permute-start.25 = (f32[16,4,1,128]{3,0,2,1:T(8,128)S(1)}, f32[16,4,1,128]{3,0,2,1:T(8,128)S(1)}, u32[]{:S(2)}, u32[]{:S(2)}) collective-permute-start(f32[16,4,1,128]{3,0,2,1:T(8,128)S(1)} %get-tuple-element.105), channel_id=1, source_target_pairs={{0,8},{8,16},{16,24},{24,32},{32,40},{40,48},{48,56},{56,64},{64,7... | collective-permute-start | bytes 98312 | tf_op jit(solution)/shard_map/ppermute | solution.py:33
  202.2 11.2 %collective-permute-start.26 = (f32[16,4,1,128]{3,0,2,1:T(8,128)S(1)}, f32[16,4,1,128]{3,0,2,1:T(8,128)S(1)}, u32[]{:S(2)}, u32[]{:S(2)}) collective-permute-start(f32[16,4,1,128]{3,0,2,1:T(8,128)S(1)} %get-tuple-element.106), channel_id=1, source_target_pairs={{8,0},{16,8},{24,16},{32,24},{40,32},{48,40},{56,48},{64,56},{72,6... | collective-permute-start | bytes 98312 | tf_op jit(solution)/shard_map/ppermute | solution.py:33
  205.6 7.7 collective-permute-start.27
  214.2 15.5 %collective-permute-start.29 = (f32[16,4,1,128]{3,0,2,1:T(8,128)S(1)}, f32[16,4,1,128]{3,0,2,1:T(8,128)S(1)}, u32[]{:S(2)}, u32[]{:S(2)}) collective-permute-start(f32[16,4,1,128]{3,0,2,1:T(8,128)S(1)} %get-tuple-element.101), channel_id=1, source_target_pairs={{0,8},{8,16},{16,24},{24,32},{32,40},{40,48},{48,56},{56,64},{64,7... | collective-permute-start | bytes 98312 | tf_op jit(solution)/shard_map/ppermute | solution.py:33
  218.4 11.2 %collective-permute-start.30 = (f32[16,4,1,128]{3,0,2,1:T(8,128)S(1)}, f32[16,4,1,128]{3,0,2,1:T(8,128)S(1)}, u32[]{:S(2)}, u32[]{:S(2)}) collective-permute-start(f32[16,4,1,128]{3,0,2,1:T(8,128)S(1)} %get-tuple-element.102), channel_id=1, source_target_pairs={{8,0},{16,8},{24,16},{32,24},{40,32},{48,40},{56,48},{64,56},{72,6... | collective-permute-start | bytes 98312 | tf_op jit(solution)/shard_map/ppermute | solution.py:33
  221.9 7.7 collective-permute-start.31
  230.5 15.5 %collective-permute-start.33 = (f32[16,4,1,128]{3,0,2,1:T(8,128)S(1)}, f32[16,4,1,128]{3,0,2,1:T(8,128)S(1)}, u32[]{:S(2)}, u32[]{:S(2)}) collective-permute-start(f32[16,4,1,128]{3,0,2,1:T(8,128)S(1)} %get-tuple-element.97), channel_id=1, source_target_pairs={{0,8},{8,16},{16,24},{24,32},{32,40},{40,48},{48,56},{56,64},{64,7... | collective-permute-start | bytes 98312 | tf_op jit(solution)/shard_map/ppermute | solution.py:33
  234.7 11.2 %collective-permute-start.34 = (f32[16,4,1,128]{3,0,2,1:T(8,128)S(1)}, f32[16,4,1,128]{3,0,2,1:T(8,128)S(1)}, u32[]{:S(2)}, u32[]{:S(2)}) collective-permute-start(f32[16,4,1,128]{3,0,2,1:T(8,128)S(1)} %get-tuple-element.98), channel_id=1, source_target_pairs={{8,0},{16,8},{24,16},{32,24},{40,32},{48,40},{56,48},{64,56},{72,6... | collective-permute-start | bytes 98312 | tf_op jit(solution)/shard_map/ppermute | solution.py:33
  238.2 7.7 collective-permute-start.35
  343.1 14.3 %collective-permute-start.37 = (f32[16,4,1,128]{3,0,2,1:T(8,128)S(1)}, f32[16,4,1,128]{3,0,2,1:T(8,128)S(1)}, u32[]{:S(2)}, u32[]{:S(2)}) collective-permute-start(f32[16,4,1,128]{3,0,2,1:T(8,128)S(1)} %get-tuple-element.93), channel_id=1, source_target_pairs={{0,8},{8,16},{16,24},{24,32},{32,40},{40,48},{48,56},{56,64},{64,7... | collective-permute-start | bytes 98312 | tf_op jit(solution)/shard_map/ppermute | solution.py:33
  344.4 13.0 %collective-permute-start.38 = (f32[16,4,1,128]{3,0,2,1:T(8,128)S(1)}, f32[16,4,1,128]{3,0,2,1:T(8,128)S(1)}, u32[]{:S(2)}, u32[]{:S(2)}) collective-permute-start(f32[16,4,1,128]{3,0,2,1:T(8,128)S(1)} %get-tuple-element.94), channel_id=1, source_target_pairs={{8,0},{16,8},{24,16},{32,24},{40,32},{48,40},{56,48},{64,56},{72,6... | collective-permute-start | bytes 98312 | tf_op jit(solution)/shard_map/ppermute | solution.py:33
  349.6 7.7 collective-permute-start.39
  358.2 15.5 %collective-permute-start.41 = (f32[16,4,1,128]{3,0,2,1:T(8,128)S(1)}, f32[16,4,1,128]{3,0,2,1:T(8,128)S(1)}, u32[]{:S(2)}, u32[]{:S(2)}) collective-permute-start(f32[16,4,1,128]{3,0,2,1:T(8,128)S(1)} %get-tuple-element.89), channel_id=1, source_target_pairs={{0,8},{8,16},{16,24},{24,32},{32,40},{40,48},{48,56},{56,64},{64,7... | collective-permute-start | bytes 98312 | tf_op jit(solution)/shard_map/ppermute | solution.py:33
  362.4 11.2 %collective-permute-start.42 = (f32[16,4,1,128]{3,0,2,1:T(8,128)S(1)}, f32[16,4,1,128]{3,0,2,1:T(8,128)S(1)}, u32[]{:S(2)}, u32[]{:S(2)}) collective-permute-start(f32[16,4,1,128]{3,0,2,1:T(8,128)S(1)} %get-tuple-element.90), channel_id=1, source_target_pairs={{8,0},{16,8},{24,16},{32,24},{40,32},{48,40},{56,48},{64,56},{72,6... | collective-permute-start | bytes 98312 | tf_op jit(solution)/shard_map/ppermute | solution.py:33
  365.9 7.7 collective-permute-start.43
  374.4 15.5 %collective-permute-start.45 = (f32[16,4,1,128]{3,0,2,1:T(8,128)S(1)}, f32[16,4,1,128]{3,0,2,1:T(8,128)S(1)}, u32[]{:S(2)}, u32[]{:S(2)}) collective-permute-start(f32[16,4,1,128]{3,0,2,1:T(8,128)S(1)} %get-tuple-element.85), channel_id=1, source_target_pairs={{0,8},{8,16},{16,24},{24,32},{32,40},{40,48},{48,56},{56,64},{64,7... | collective-permute-start | bytes 98312 | tf_op jit(solution)/shard_map/ppermute | solution.py:33
  378.7 11.2 %collective-permute-start.46 = (f32[16,4,1,128]{3,0,2,1:T(8,128)S(1)}, f32[16,4,1,128]{3,0,2,1:T(8,128)S(1)}, u32[]{:S(2)}, u32[]{:S(2)}) collective-permute-start(f32[16,4,1,128]{3,0,2,1:T(8,128)S(1)} %get-tuple-element.86), channel_id=1, source_target_pairs={{8,0},{16,8},{24,16},{32,24},{40,32},{48,40},{56,48},{64,56},{72,6... | collective-permute-start | bytes 98312 | tf_op jit(solution)/shard_map/ppermute | solution.py:33
  390.9 15.5 %collective-permute-start.49 = (f32[16,4,1,128]{3,0,2,1:T(8,128)S(1)}, f32[16,4,1,128]{3,0,2,1:T(8,128)S(1)}, u32[]{:S(2)}, u32[]{:S(2)}) collective-permute-start(f32[16,4,1,128]{3,0,2,1:T(8,128)S(1)} %get-tuple-element.81), channel_id=1, source_target_pairs={{0,8},{8,16},{16,24},{24,32},{32,40},{40,48},{48,56},{56,64},{64,7... | collective-permute-start | bytes 98312 | tf_op jit(solution)/shard_map/ppermute | solution.py:33
  395.3 11.1 %collective-permute-start.50 = (f32[16,4,1,128]{3,0,2,1:T(8,128)S(1)}, f32[16,4,1,128]{3,0,2,1:T(8,128)S(1)}, u32[]{:S(2)}, u32[]{:S(2)}) collective-permute-start(f32[16,4,1,128]{3,0,2,1:T(8,128)S(1)} %get-tuple-element.82), channel_id=1, source_target_pairs={{8,0},{16,8},{24,16},{32,24},{40,32},{48,40},{56,48},{64,56},{72,6... | collective-permute-start | bytes 98312 | tf_op jit(solution)/shard_map/ppermute | solution.py:33
  398.7 7.7 collective-permute-start.51
  503.9 14.7 %collective-permute-start.53 = (f32[16,4,1,128]{3,0,2,1:T(8,128)S(1)}, f32[16,4,1,128]{3,0,2,1:T(8,128)S(1)}, u32[]{:S(2)}, u32[]{:S(2)}) collective-permute-start(f32[16,4,1,128]{3,0,2,1:T(8,128)S(1)} %get-tuple-element.77), channel_id=1, source_target_pairs={{0,8},{8,16},{16,24},{24,32},{32,40},{40,48},{48,56},{56,64},{64,7... | collective-permute-start | bytes 98312 | tf_op jit(solution)/shard_map/ppermute | solution.py:33
  505.2 13.4 %collective-permute-start.54 = (f32[16,4,1,128]{3,0,2,1:T(8,128)S(1)}, f32[16,4,1,128]{3,0,2,1:T(8,128)S(1)}, u32[]{:S(2)}, u32[]{:S(2)}) collective-permute-start(f32[16,4,1,128]{3,0,2,1:T(8,128)S(1)} %get-tuple-element.78), channel_id=1, source_target_pairs={{8,0},{16,8},{24,16},{32,24},{40,32},{48,40},{56,48},{64,56},{72,6... | collective-permute-start | bytes 98312 | tf_op jit(solution)/shard_map/ppermute | solution.py:33
  506.5 7.9 collective-permute-start.52
  510.8 7.7 collective-permute-start.55
  519.5 15.3 %collective-permute-start.57 = (f32[16,4,1,128]{3,0,2,1:T(8,128)S(1)}, f32[16,4,1,128]{3,0,2,1:T(8,128)S(1)}, u32[]{:S(2)}, u32[]{:S(2)}) collective-permute-start(f32[16,4,1,128]{3,0,2,1:T(8,128)S(1)} %get-tuple-element.73), channel_id=1, source_target_pairs={{0,8},{8,16},{16,24},{24,32},{32,40},{40,48},{48,56},{56,64},{64,7... | collective-permute-start | bytes 98312 | tf_op jit(solution)/shard_map/ppermute | solution.py:33
  523.8 11.1 %collective-permute-start.58 = (f32[16,4,1,128]{3,0,2,1:T(8,128)S(1)}, f32[16,4,1,128]{3,0,2,1:T(8,128)S(1)}, u32[]{:S(2)}, u32[]{:S(2)}) collective-permute-start(f32[16,4,1,128]{3,0,2,1:T(8,128)S(1)} %get-tuple-element.74), channel_id=1, source_target_pairs={{8,0},{16,8},{24,16},{32,24},{40,32},{48,40},{56,48},{64,56},{72,6... | collective-permute-start | bytes 98312 | tf_op jit(solution)/shard_map/ppermute | solution.py:33
  535.8 15.3 %collective-permute-start.61 = (f32[16,4,1,128]{3,0,2,1:T(8,128)S(1)}, f32[16,4,1,128]{3,0,2,1:T(8,128)S(1)}, u32[]{:S(2)}, u32[]{:S(2)}) collective-permute-start(f32[16,4,1,128]{3,0,2,1:T(8,128)S(1)} %get-tuple-element.69), channel_id=1, source_target_pairs={{0,8},{8,16},{16,24},{24,32},{32,40},{40,48},{48,56},{56,64},{64,7... | collective-permute-start | bytes 98312 | tf_op jit(solution)/shard_map/ppermute | solution.py:33
  540.0 11.1 %collective-permute-start.62 = (f32[16,4,1,128]{3,0,2,1:T(8,128)S(1)}, f32[16,4,1,128]{3,0,2,1:T(8,128)S(1)}, u32[]{:S(2)}, u32[]{:S(2)}) collective-permute-start(f32[16,4,1,128]{3,0,2,1:T(8,128)S(1)} %get-tuple-element.70), channel_id=1, source_target_pairs={{8,0},{16,8},{24,16},{32,24},{40,32},{48,40},{56,48},{64,56},{72,6... | collective-permute-start | bytes 98312 | tf_op jit(solution)/shard_map/ppermute | solution.py:33
  552.1 15.3 %collective-permute-start.65 = (f32[16,4,1,128]{3,0,2,1:T(8,128)S(1)}, f32[16,4,1,128]{3,0,2,1:T(8,128)S(1)}, u32[]{:S(2)}, u32[]{:S(2)}) collective-permute-start(f32[16,4,1,128]{3,0,2,1:T(8,128)S(1)} %get-tuple-element.65), channel_id=1, source_target_pairs={{0,8},{8,16},{16,24},{24,32},{32,40},{40,48},{48,56},{56,64},{64,7... | collective-permute-start | bytes 98312 | tf_op jit(solution)/shard_map/ppermute | solution.py:33
  556.3 11.1 %collective-permute-start.66 = (f32[16,4,1,128]{3,0,2,1:T(8,128)S(1)}, f32[16,4,1,128]{3,0,2,1:T(8,128)S(1)}, u32[]{:S(2)}, u32[]{:S(2)}) collective-permute-start(f32[16,4,1,128]{3,0,2,1:T(8,128)S(1)} %get-tuple-element.66), channel_id=1, source_target_pairs={{8,0},{16,8},{24,16},{32,24},{40,32},{48,40},{56,48},{64,56},{72,6... | collective-permute-start | bytes 98312 | tf_op jit(solution)/shard_map/ppermute | solution.py:33
  660.0 14.4 %collective-permute-start.69 = (f32[16,4,1,128]{3,0,2,1:T(8,128)S(1)}, f32[16,4,1,128]{3,0,2,1:T(8,128)S(1)}, u32[]{:S(2)}, u32[]{:S(2)}) collective-permute-start(f32[16,4,1,128]{3,0,2,1:T(8,128)S(1)} %get-tuple-element.61), channel_id=1, source_target_pairs={{0,8},{8,16},{16,24},{24,32},{32,40},{40,48},{48,56},{56,64},{64,7... | collective-permute-start | bytes 98312 | tf_op jit(solution)/shard_map/ppermute | solution.py:33
  661.3 13.2 %collective-permute-start.70 = (f32[16,4,1,128]{3,0,2,1:T(8,128)S(1)}, f32[16,4,1,128]{3,0,2,1:T(8,128)S(1)}, u32[]{:S(2)}, u32[]{:S(2)}) collective-permute-start(f32[16,4,1,128]{3,0,2,1:T(8,128)S(1)} %get-tuple-element.62), channel_id=1, source_target_pairs={{8,0},{16,8},{24,16},{32,24},{40,32},{48,40},{56,48},{64,56},{72,6... | collective-permute-start | bytes 98312 | tf_op jit(solution)/shard_map/ppermute | solution.py:33
  675.4 15.3 %collective-permute-start.73 = (f32[16,4,1,128]{3,0,2,1:T(8,128)S(1)}, f32[16,4,1,128]{3,0,2,1:T(8,128)S(1)}, u32[]{:S(2)}, u32[]{:S(2)}) collective-permute-start(f32[16,4,1,128]{3,0,2,1:T(8,128)S(1)} %get-tuple-element.57), channel_id=1, source_target_pairs={{0,8},{8,16},{16,24},{24,32},{32,40},{40,48},{48,56},{56,64},{64,7... | collective-permute-start | bytes 98312 | tf_op jit(solution)/shard_map/ppermute | solution.py:33
  679.6 11.1 %collective-permute-start.74 = (f32[16,4,1,128]{3,0,2,1:T(8,128)S(1)}, f32[16,4,1,128]{3,0,2,1:T(8,128)S(1)}, u32[]{:S(2)}, u32[]{:S(2)}) collective-permute-start(f32[16,4,1,128]{3,0,2,1:T(8,128)S(1)} %get-tuple-element.58), channel_id=1, source_target_pairs={{8,0},{16,8},{24,16},{32,24},{40,32},{48,40},{56,48},{64,56},{72,6... | collective-permute-start | bytes 98312 | tf_op jit(solution)/shard_map/ppermute | solution.py:33
  691.6 15.3 %collective-permute-start.77 = (f32[16,4,1,128]{3,0,2,1:T(8,128)S(1)}, f32[16,4,1,128]{3,0,2,1:T(8,128)S(1)}, u32[]{:S(2)}, u32[]{:S(2)}) collective-permute-start(f32[16,4,1,128]{3,0,2,1:T(8,128)S(1)} %get-tuple-element.53), channel_id=1, source_target_pairs={{0,8},{8,16},{16,24},{24,32},{32,40},{40,48},{48,56},{56,64},{64,7... | collective-permute-start | bytes 98312 | tf_op jit(solution)/shard_map/ppermute | solution.py:33
  695.9 11.1 %collective-permute-start.78 = (f32[16,4,1,128]{3,0,2,1:T(8,128)S(1)}, f32[16,4,1,128]{3,0,2,1:T(8,128)S(1)}, u32[]{:S(2)}, u32[]{:S(2)}) collective-permute-start(f32[16,4,1,128]{3,0,2,1:T(8,128)S(1)} %get-tuple-element.54), channel_id=1, source_target_pairs={{8,0},{16,8},{24,16},{32,24},{40,32},{48,40},{56,48},{64,56},{72,6... | collective-permute-start | bytes 98312 | tf_op jit(solution)/shard_map/ppermute | solution.py:33
  707.9 15.3 %collective-permute-start.81 = (f32[16,4,1,128]{3,0,2,1:T(8,128)S(1)}, f32[16,4,1,128]{3,0,2,1:T(8,128)S(1)}, u32[]{:S(2)}, u32[]{:S(2)}) collective-permute-start(f32[16,4,1,128]{3,0,2,1:T(8,128)S(1)} %get-tuple-element.49), channel_id=1, source_target_pairs={{0,8},{8,16},{16,24},{24,32},{32,40},{40,48},{48,56},{56,64},{64,7... | collective-permute-start | bytes 98312 | tf_op jit(solution)/shard_map/ppermute | solution.py:33
  712.2 11.1 %collective-permute-start.82 = (f32[16,4,1,128]{3,0,2,1:T(8,128)S(1)}, f32[16,4,1,128]{3,0,2,1:T(8,128)S(1)}, u32[]{:S(2)}, u32[]{:S(2)}) collective-permute-start(f32[16,4,1,128]{3,0,2,1:T(8,128)S(1)} %get-tuple-element.50), channel_id=1, source_target_pairs={{8,0},{16,8},{24,16},{32,24},{40,32},{48,40},{56,48},{64,56},{72,6... | collective-permute-start | bytes 98312 | tf_op jit(solution)/shard_map/ppermute | solution.py:33
  (38 other events, 257.0 us)

commit v2 on v1

--- a/solution.py
+++ b/solution.py
@@ -2,6 +2,8 @@
 import jax.numpy as jnp
 from jax import lax
 from jax.sharding import PartitionSpec as P
+from jax.experimental import pallas as pl
+from jax.experimental.pallas import tpu as pltpu
 
 RHS = 16
 S = 4
@@ -59,6 +61,83 @@
     return total
 
 
+def _device(axis, index, other_axis, other_index):
+    return {axis: index, other_axis: other_index}
+
+
+def allreduce_kernel(axis, other_axis, n, x_ref, o_ref, slots, send_sem, recv_sem):
+    me = lax.axis_index(axis)
+    other = lax.axis_index(other_axis)
+    barrier = pltpu.get_barrier_semaphore()
+    for j in range(n):
+        @pl.when(j != me)
+        def _():
+            pl.semaphore_signal(
+                barrier, inc=1, device_id=_device(axis, j, other_axis, other),
+                device_id_type=pl.DeviceIdType.MESH,
+            )
+    pl.semaphore_wait(barrier, n - 1)
+
+    def copy_to(j):
+        return pltpu.make_async_remote_copy(
+            src_ref=x_ref,
+            dst_ref=slots.at[me],
+            send_sem=send_sem.at[j],
+            recv_sem=recv_sem.at[me],
+            device_id=_device(axis, j, other_axis, other),
+            device_id_type=pl.DeviceIdType.MESH,
+        )
+
+    def copy_from(j):
+        return pltpu.make_async_remote_copy(
+            src_ref=x_ref,
+            dst_ref=slots.at[j],
+            send_sem=send_sem.at[j],
+            recv_sem=recv_sem.at[j],
+            device_id=_device(axis, j, other_axis, other),
+            device_id_type=pl.DeviceIdType.MESH,
+        )
+
+    for j in range(n):
+        @pl.when(j != me)
+        def _():
+            copy_to(j).start()
+
+    slots[me] = x_ref[...]
+    for j in range(n):
+        @pl.when(j != me)
+        def _():
+            copy_to(j).wait_send()
+            copy_from(j).wait_recv()
+
+    acc = slots[0]
+    for j in range(1, n):
+        acc = acc + slots[j]
+    o_ref[...] = acc
+
+
+def allreduce_axis(x, axis, other_axis, collective_id):
+    n = lax.axis_size(axis)
+    return pl.pallas_call(
+        lambda *refs: allreduce_kernel(axis, other_axis, n, *refs),
+        out_shape=jax.ShapeDtypeStruct(x.shape, x.dtype),
+        in_specs=[pl.BlockSpec(memory_space=pltpu.VMEM)],
+        out_specs=pl.BlockSpec(memory_space=pltpu.VMEM),
+        scratch_shapes=[
+            pltpu.VMEM((n,) + x.shape, x.dtype),
+            pltpu.SemaphoreType.DMA((n,)),
+            pltpu.SemaphoreType.DMA((n,)),
+        ],
+        compiler_params=pltpu.CompilerParams(collective_id=collective_id, has_side_effects=True),
+        name=f"allreduce_{axis}",
+    )(x)
+
+
+def gram_sum(local_gram):
+    partial = allreduce_axis(local_gram, "gy", "gx", 0)
+    return allreduce_axis(partial, "gx", "gy", 1)
+
+
 def small_solve(gram_all):
     shift_matrix = jnp.eye(BASIS, BASIS - RHS, dtype=jnp.float32) + jnp.eye(
         BASIS, BASIS - RHS, k=-RHS, dtype=jnp.float32
@@ -90,7 +169,7 @@
             blocks.append(-apply_off(padded, terms) / diagonal)
         stacked = jnp.concatenate(blocks, 0).reshape(BASIS, -1)
         local_gram = jnp.dot(stacked, stacked.T, precision=hp)
-        gram_all = lax.psum(local_gram, ("gx", "gy"))
+        gram_all = gram_sum(local_gram)
         y, coeffs = small_solve(gram_all)
         solution = solution + jnp.dot(y.T, stacked[: BASIS - RHS], precision=hp).reshape(shape)
         residual = jnp.dot(coeffs.T, stacked, precision=hp).reshape(shape)

time: 827 us -> 644 us (0.78)
  blocking collectives: 371 us -> 0 us
  Pallas kernels: 0 us -> 166 us
    psum x5 -> x0, blocking collectives: 371 us -> none  [shards(): gram_all = lax.psum(local_gram, ('gx', 'gy'))]
    pallas_call x0 -> x10, Pallas kernels: none -> 166 us  [allreduce_axis(): pl.pallas_call(lambda *refs: allreduce_kernel(axis, other_axis, n, *refs)...]
  transfers between devices with their start and end apart: 84 -> 84, of which waited for: 34 -> 35; matrix products, arithmetic and copies ran while one was open for 2% -> 3% of each run, Pallas kernels for 0% -> 0%
where the time goes in v2:
time: 644 us; the launch traced here: 633 us
  starting transfers between devices  212 us (33%)
  Pallas kernels  166 us (26%)
  waiting for transfers between devices  105 us (16%)
  other arithmetic  80.1 us (12%)
  matrix products  35.9 us (6%)
  local copies, waits for them, and re-layouts  29.8 us (5%)
    pallas_call x10, Pallas kernels, allreduce_axis(): pl.pallas_call(lambda *refs: allreduce_kernel(axis, other_axis, n, *refs)...  166 us
    ppermute x40, starting transfers between devices, halo_4(): lax.ppermute(last, axis, up)  129 us
    ppermute x40, waiting for transfers between devices, halo_4(): lax.ppermute(leading, axis, down)  87.1 us
    ppermute x40, starting transfers between devices, halo_4(): lax.ppermute(leading, axis, down)  71.2 us
    another operation x15, other arithmetic, small_solve(): lower = jnp.linalg.cholesky(normal)  32.6 us
    another operation x10, other arithmetic, small_solve(): y = jax.scipy.linalg.cho_solve((lower, True), right_side)  27.7 us
    unnamed x26, local copies, waits for them, and re-layouts  17.6 us
  transfers between devices with their start and end apart: 84, of which 35 were waited for; matrix products, arithmetic and copies ran while one was open for 3% of the time, Pallas kernels for 0%

profile of v2, /device:TPU:1, one launch (start us, length us, event | category | flops | bytes accessed | tf_op | source)
XLA Modules:
  0.0 632.9 jit_solution(5189427867202452876)
XLA Ops:
  10.6 5.1 collective-permute-start.2
  34.1 4.4 collective-permute-done.7
  39.3 4.3 collective-permute-start.9
  50.4 4.4 collective-permute-done.11
  55.6 5.2 collective-permute-start.13
  67.6 4.4 collective-permute-done.15
  72.9 4.3 collective-permute-start.17
  83.9 4.4 collective-permute-done.19
  91.3 9.1 %allreduce_gy.5.refs_0_ = f32[80,80]{1,0:T(8,128)} custom-call(f32[80,80]{1,0:T(8,128)} %convolution_bitcast_fusion.4.refs_0_), custom_call_target="tpu_custom_call" | custom-call | tf_op jit(solution)/shard_map/allreduce_gy/pallas_call | solution.py:121
  100.4 23.2 %allreduce_gx.5 = f32[80,80]{1,0:T(8,128)} custom-call(f32[80,80]{1,0:T(8,128)} %allreduce_gy.5.refs_0_), custom_call_target="tpu_custom_call" | custom-call | tf_op jit(solution)/shard_map/allreduce_gx/pallas_call | solution.py:121
  126.3 5.8 cholesky.89
  133.5 4.9 custom-call.11
  140.6 5.0 collective-permute-start.21
  152.9 4.4 collective-permute-done.23
  158.1 4.3 collective-permute-start.25
  169.2 5.1 collective-permute-done.27
  185.9 4.6 collective-permute-done.31
  202.2 4.6 collective-permute-done.35
  210.9 9.3 %allreduce_gy.6.refs_0_ = f32[80,80]{1,0:T(8,128)} custom-call(f32[80,80]{1,0:T(8,128)} %convolution_bitcast_fusion.3.refs_0_), custom_call_target="tpu_custom_call" | custom-call | tf_op jit(solution)/shard_map/allreduce_gy/pallas_call | solution.py:121
  220.2 23.8 %allreduce_gx.6 = f32[80,80]{1,0:T(8,128)} custom-call(f32[80,80]{1,0:T(8,128)} %allreduce_gy.6.refs_0_), custom_call_target="tpu_custom_call" | custom-call | tf_op jit(solution)/shard_map/allreduce_gx/pallas_call | solution.py:121
  249.1 5.8 cholesky.100
  256.3 4.9 custom-call.12
  275.6 4.4 collective-permute-done.39
  280.8 5.7 collective-permute-start.41
  293.2 5.4 collective-permute-done.43
  310.3 4.6 collective-permute-done.47
  335.3 9.3 %allreduce_gy.7.refs_0_ = f32[80,80]{1,0:T(8,128)} custom-call(f32[80,80]{1,0:T(8,128)} %convolution_bitcast_fusion.2.refs_0_), custom_call_target="tpu_custom_call" | custom-call | tf_op jit(solution)/shard_map/allreduce_gy/pallas_call | solution.py:121
  344.6 24.2 %allreduce_gx.7 = f32[80,80]{1,0:T(8,128)} custom-call(f32[80,80]{1,0:T(8,128)} %allreduce_gy.7.refs_0_), custom_call_target="tpu_custom_call" | custom-call | tf_op jit(solution)/shard_map/allreduce_gx/pallas_call | solution.py:121
  373.9 5.8 cholesky.111
  381.1 4.9 custom-call.13
  400.3 4.4 collective-permute-done.55
  405.7 5.8 collective-permute-start.57
  419.1 4.3 collective-permute-done.59
  424.4 4.1 collective-permute-start.61
  435.3 4.4 collective-permute-done.63
  440.7 4.1 collective-permute-start.65
  459.0 9.3 %allreduce_gy.8.refs_0_ = f32[80,80]{1,0:T(8,128)} custom-call(f32[80,80]{1,0:T(8,128)} %convolution_bitcast_fusion.1.refs_0_), custom_call_target="tpu_custom_call" | custom-call | tf_op jit(solution)/shard_map/allreduce_gy/pallas_call | solution.py:121
  468.3 24.4 %allreduce_gx.8 = f32[80,80]{1,0:T(8,128)} custom-call(f32[80,80]{1,0:T(8,128)} %allreduce_gy.8.refs_0_), custom_call_target="tpu_custom_call" | custom-call | tf_op jit(solution)/shard_map/allreduce_gx/pallas_call | solution.py:121
  495.4 5.8 cholesky.122
  502.6 4.9 custom-call.14
  520.6 4.4 collective-permute-done.71
  525.9 5.7 collective-permute-start.73
  538.9 4.8 collective-permute-done.75
  555.8 4.2 collective-permute-done.79
  579.3 9.3 %allreduce_gy.9.refs_0_ = f32[80,80]{1,0:T(8,128)} custom-call(f32[80,80]{1,0:T(8,128)} %convolution_bitcast_fusion.refs_0_), custom_call_target="tpu_custom_call" | custom-call | tf_op jit(solution)/shard_map/allreduce_gy/pallas_call | solution.py:121
  588.6 24.2 %allreduce_gx.9 = f32[80,80]{1,0:T(8,128)} custom-call(f32[80,80]{1,0:T(8,128)} %allreduce_gy.9.refs_0_), custom_call_target="tpu_custom_call" | custom-call | tf_op jit(solution)/shard_map/allreduce_gx/pallas_call | solution.py:121
  615.6 5.8 cholesky.133
  622.8 4.9 custom-call.15
  (378 shorter events, 279.2 us)
Async XLA Ops:
  23.9 14.6 %collective-permute-start.5 = (f32[16,4,1,128]{3,0,2,1:T(8,128)S(1)}, f32[16,4,1,128]{3,0,2,1:T(8,128)S(1)}, u32[]{:S(2)}, u32[]{:S(2)}) collective-permute-start(f32[16,4,1,128]{3,0,2,1:T(8,128)S(1)} %get-tuple-element.125), channel_id=1, source_target_pairs={{0,8},{8,16},{16,24},{24,32},{32,40},{40,48},{48,56},{56,64},{64,7... | collective-permute-start | bytes 98312 | tf_op jit(solution)/shard_map/ppermute | solution.py:35
  27.1 11.4 %collective-permute-start.6 = (f32[16,4,1,128]{3,0,2,1:T(8,128)S(1)}, f32[16,4,1,128]{3,0,2,1:T(8,128)S(1)}, u32[]{:S(2)}, u32[]{:S(2)}) collective-permute-start(f32[16,4,1,128]{3,0,2,1:T(8,128)S(1)} %get-tuple-element.126), channel_id=1, source_target_pairs={{8,0},{16,8},{24,16},{32,24},{40,32},{48,40},{56,48},{64,56},{72,6... | collective-permute-start | bytes 98312 | tf_op jit(solution)/shard_map/ppermute | solution.py:35
  39.3 15.5 %collective-permute-start.9 = (f32[16,4,1,128]{3,0,2,1:T(8,128)S(1)}, f32[16,4,1,128]{3,0,2,1:T(8,128)S(1)}, u32[]{:S(2)}, u32[]{:S(2)}) collective-permute-start(f32[16,4,1,128]{3,0,2,1:T(8,128)S(1)} %get-tuple-element.121), channel_id=1, source_target_pairs={{0,8},{8,16},{16,24},{24,32},{32,40},{40,48},{48,56},{56,64},{64,7... | collective-permute-start | bytes 98312 | tf_op jit(solution)/shard_map/ppermute | solution.py:35
  43.6 11.2 %collective-permute-start.10 = (f32[16,4,1,128]{3,0,2,1:T(8,128)S(1)}, f32[16,4,1,128]{3,0,2,1:T(8,128)S(1)}, u32[]{:S(2)}, u32[]{:S(2)}) collective-permute-start(f32[16,4,1,128]{3,0,2,1:T(8,128)S(1)} %get-tuple-element.122), channel_id=1, source_target_pairs={{8,0},{16,8},{24,16},{32,24},{40,32},{48,40},{56,48},{64,56},{72,6... | collective-permute-start | bytes 98312 | tf_op jit(solution)/shard_map/ppermute | solution.py:35
  55.6 16.4 %collective-permute-start.13 = (f32[16,4,1,128]{3,0,2,1:T(8,128)S(1)}, f32[16,4,1,128]{3,0,2,1:T(8,128)S(1)}, u32[]{:S(2)}, u32[]{:S(2)}) collective-permute-start(f32[16,4,1,128]{3,0,2,1:T(8,128)S(1)} %get-tuple-element.117), channel_id=1, source_target_pairs={{0,8},{8,16},{16,24},{24,32},{32,40},{40,48},{48,56},{56,64},{64,7... | collective-permute-start | bytes 98312 | tf_op jit(solution)/shard_map/ppermute | solution.py:35
  60.8 11.2 %collective-permute-start.14 = (f32[16,4,1,128]{3,0,2,1:T(8,128)S(1)}, f32[16,4,1,128]{3,0,2,1:T(8,128)S(1)}, u32[]{:S(2)}, u32[]{:S(2)}) collective-permute-start(f32[16,4,1,128]{3,0,2,1:T(8,128)S(1)} %get-tuple-element.118), channel_id=1, source_target_pairs={{8,0},{16,8},{24,16},{32,24},{40,32},{48,40},{56,48},{64,56},{72,6... | collective-permute-start | bytes 98312 | tf_op jit(solution)/shard_map/ppermute | solution.py:35
  72.9 15.3 %collective-permute-start.17 = (f32[16,4,1,128]{3,0,2,1:T(8,128)S(1)}, f32[16,4,1,128]{3,0,2,1:T(8,128)S(1)}, u32[]{:S(2)}, u32[]{:S(2)}) collective-permute-start(f32[16,4,1,128]{3,0,2,1:T(8,128)S(1)} %get-tuple-element.113), channel_id=1, source_target_pairs={{0,8},{8,16},{16,24},{24,32},{32,40},{40,48},{48,56},{56,64},{64,7... | collective-permute-start | bytes 98312 | tf_op jit(solution)/shard_map/ppermute | solution.py:35
  77.2 11.1 %collective-permute-start.18 = (f32[16,4,1,128]{3,0,2,1:T(8,128)S(1)}, f32[16,4,1,128]{3,0,2,1:T(8,128)S(1)}, u32[]{:S(2)}, u32[]{:S(2)}) collective-permute-start(f32[16,4,1,128]{3,0,2,1:T(8,128)S(1)} %get-tuple-element.114), channel_id=1, source_target_pairs={{8,0},{16,8},{24,16},{32,24},{40,32},{48,40},{56,48},{64,56},{72,6... | collective-permute-start | bytes 98312 | tf_op jit(solution)/shard_map/ppermute | solution.py:35
  140.6 16.7 %collective-permute-start.21 = (f32[16,4,1,128]{3,0,2,1:T(8,128)S(1)}, f32[16,4,1,128]{3,0,2,1:T(8,128)S(1)}, u32[]{:S(2)}, u32[]{:S(2)}) collective-permute-start(f32[16,4,1,128]{3,0,2,1:T(8,128)S(1)} %get-tuple-element.109), channel_id=1, source_target_pairs={{0,8},{8,16},{16,24},{24,32},{32,40},{40,48},{48,56},{56,64},{64,7... | collective-permute-start | bytes 98312 | tf_op jit(solution)/shard_map/ppermute | solution.py:35
  145.6 11.6 %collective-permute-start.22 = (f32[16,4,1,128]{3,0,2,1:T(8,128)S(1)}, f32[16,4,1,128]{3,0,2,1:T(8,128)S(1)}, u32[]{:S(2)}, u32[]{:S(2)}) collective-permute-start(f32[16,4,1,128]{3,0,2,1:T(8,128)S(1)} %get-tuple-element.110), channel_id=1, source_target_pairs={{8,0},{16,8},{24,16},{32,24},{40,32},{48,40},{56,48},{64,56},{72,6... | collective-permute-start | bytes 98312 | tf_op jit(solution)/shard_map/ppermute | solution.py:35
  158.1 16.2 %collective-permute-start.25 = (f32[16,4,1,128]{3,0,2,1:T(8,128)S(1)}, f32[16,4,1,128]{3,0,2,1:T(8,128)S(1)}, u32[]{:S(2)}, u32[]{:S(2)}) collective-permute-start(f32[16,4,1,128]{3,0,2,1:T(8,128)S(1)} %get-tuple-element.105), channel_id=1, source_target_pairs={{0,8},{8,16},{16,24},{24,32},{32,40},{40,48},{48,56},{56,64},{64,7... | collective-permute-start | bytes 98312 | tf_op jit(solution)/shard_map/ppermute | solution.py:35
  162.4 11.9 %collective-permute-start.26 = (f32[16,4,1,128]{3,0,2,1:T(8,128)S(1)}, f32[16,4,1,128]{3,0,2,1:T(8,128)S(1)}, u32[]{:S(2)}, u32[]{:S(2)}) collective-permute-start(f32[16,4,1,128]{3,0,2,1:T(8,128)S(1)} %get-tuple-element.106), channel_id=1, source_target_pairs={{8,0},{16,8},{24,16},{32,24},{40,32},{48,40},{56,48},{64,56},{72,6... | collective-permute-start | bytes 98312 | tf_op jit(solution)/shard_map/ppermute | solution.py:35
  165.8 8.4 %collective-permute-start.27 = (f32[16,4,8,1]{3,0,2,1:T(8,128)S(1)}, f32[16,4,8,1]{3,0,2,1:T(8,128)S(1)}, u32[]{:S(2)}, u32[]{:S(2)}) collective-permute-start(f32[16,4,8,1]{3,0,2,1:T(8,128)S(1)} %get-tuple-element.104), channel_id=1, source_target_pairs={{1,0},{2,1},{3,2},{4,3},{5,4},{6,5},{7,6},{9,8},{10,9},{11,10},{12... | collective-permute-start | bytes 6152 | tf_op jit(solution)/shard_map/ppermute | solution.py:35
  175.1 15.5 %collective-permute-start.29 = (f32[16,4,1,128]{3,0,2,1:T(8,128)S(1)}, f32[16,4,1,128]{3,0,2,1:T(8,128)S(1)}, u32[]{:S(2)}, u32[]{:S(2)}) collective-permute-start(f32[16,4,1,128]{3,0,2,1:T(8,128)S(1)} %get-tuple-element.101), channel_id=1, source_target_pairs={{0,8},{8,16},{16,24},{24,32},{32,40},{40,48},{48,56},{56,64},{64,7... | collective-permute-start | bytes 98312 | tf_op jit(solution)/shard_map/ppermute | solution.py:35
  179.1 11.5 %collective-permute-start.30 = (f32[16,4,1,128]{3,0,2,1:T(8,128)S(1)}, f32[16,4,1,128]{3,0,2,1:T(8,128)S(1)}, u32[]{:S(2)}, u32[]{:S(2)}) collective-permute-start(f32[16,4,1,128]{3,0,2,1:T(8,128)S(1)} %get-tuple-element.102), channel_id=1, source_target_pairs={{8,0},{16,8},{24,16},{32,24},{40,32},{48,40},{56,48},{64,56},{72,6... | collective-permute-start | bytes 98312 | tf_op jit(solution)/shard_map/ppermute | solution.py:35
  182.6 8.0 %collective-permute-start.31 = (f32[16,4,8,1]{3,0,2,1:T(8,128)S(1)}, f32[16,4,8,1]{3,0,2,1:T(8,128)S(1)}, u32[]{:S(2)}, u32[]{:S(2)}) collective-permute-start(f32[16,4,8,1]{3,0,2,1:T(8,128)S(1)} %get-tuple-element.100), channel_id=1, source_target_pairs={{1,0},{2,1},{3,2},{4,3},{5,4},{6,5},{7,6},{9,8},{10,9},{11,10},{12... | collective-permute-start | bytes 6152 | tf_op jit(solution)/shard_map/ppermute | solution.py:35
  191.4 15.5 %collective-permute-start.33 = (f32[16,4,1,128]{3,0,2,1:T(8,128)S(1)}, f32[16,4,1,128]{3,0,2,1:T(8,128)S(1)}, u32[]{:S(2)}, u32[]{:S(2)}) collective-permute-start(f32[16,4,1,128]{3,0,2,1:T(8,128)S(1)} %get-tuple-element.97), channel_id=1, source_target_pairs={{0,8},{8,16},{16,24},{24,32},{32,40},{40,48},{48,56},{56,64},{64,7... | collective-permute-start | bytes 98312 | tf_op jit(solution)/shard_map/ppermute | solution.py:35
  195.4 11.5 %collective-permute-start.34 = (f32[16,4,1,128]{3,0,2,1:T(8,128)S(1)}, f32[16,4,1,128]{3,0,2,1:T(8,128)S(1)}, u32[]{:S(2)}, u32[]{:S(2)}) collective-permute-start(f32[16,4,1,128]{3,0,2,1:T(8,128)S(1)} %get-tuple-element.98), channel_id=1, source_target_pairs={{8,0},{16,8},{24,16},{32,24},{40,32},{48,40},{56,48},{64,56},{72,6... | collective-permute-start | bytes 98312 | tf_op jit(solution)/shard_map/ppermute | solution.py:35
  198.9 8.0 %collective-permute-start.35 = (f32[16,4,8,1]{3,0,2,1:T(8,128)S(1)}, f32[16,4,8,1]{3,0,2,1:T(8,128)S(1)}, u32[]{:S(2)}, u32[]{:S(2)}) collective-permute-start(f32[16,4,8,1]{3,0,2,1:T(8,128)S(1)} %get-tuple-element.96), channel_id=1, source_target_pairs={{1,0},{2,1},{3,2},{4,3},{5,4},{6,5},{7,6},{9,8},{10,9},{11,10},{12... | collective-permute-start | bytes 6152 | tf_op jit(solution)/shard_map/ppermute | solution.py:35
  264.7 15.3 %collective-permute-start.37 = (f32[16,4,1,128]{3,0,2,1:T(8,128)S(1)}, f32[16,4,1,128]{3,0,2,1:T(8,128)S(1)}, u32[]{:S(2)}, u32[]{:S(2)}) collective-permute-start(f32[16,4,1,128]{3,0,2,1:T(8,128)S(1)} %get-tuple-element.93), channel_id=1, source_target_pairs={{0,8},{8,16},{16,24},{24,32},{32,40},{40,48},{48,56},{56,64},{64,7... | collective-permute-start | bytes 98312 | tf_op jit(solution)/shard_map/ppermute | solution.py:35
  268.3 11.6 %collective-permute-start.38 = (f32[16,4,1,128]{3,0,2,1:T(8,128)S(1)}, f32[16,4,1,128]{3,0,2,1:T(8,128)S(1)}, u32[]{:S(2)}, u32[]{:S(2)}) collective-permute-start(f32[16,4,1,128]{3,0,2,1:T(8,128)S(1)} %get-tuple-element.94), channel_id=1, source_target_pairs={{8,0},{16,8},{24,16},{32,24},{40,32},{48,40},{56,48},{64,56},{72,6... | collective-permute-start | bytes 98312 | tf_op jit(solution)/shard_map/ppermute | solution.py:35
  280.8 17.9 %collective-permute-start.41 = (f32[16,4,1,128]{3,0,2,1:T(8,128)S(1)}, f32[16,4,1,128]{3,0,2,1:T(8,128)S(1)}, u32[]{:S(2)}, u32[]{:S(2)}) collective-permute-start(f32[16,4,1,128]{3,0,2,1:T(8,128)S(1)} %get-tuple-element.89), channel_id=1, source_target_pairs={{0,8},{8,16},{16,24},{24,32},{32,40},{40,48},{48,56},{56,64},{64,7... | collective-permute-start | bytes 98312 | tf_op jit(solution)/shard_map/ppermute | solution.py:35
  286.5 12.2 %collective-permute-start.42 = (f32[16,4,1,128]{3,0,2,1:T(8,128)S(1)}, f32[16,4,1,128]{3,0,2,1:T(8,128)S(1)}, u32[]{:S(2)}, u32[]{:S(2)}) collective-permute-start(f32[16,4,1,128]{3,0,2,1:T(8,128)S(1)} %get-tuple-element.90), channel_id=1, source_target_pairs={{8,0},{16,8},{24,16},{32,24},{40,32},{48,40},{56,48},{64,56},{72,6... | collective-permute-start | bytes 98312 | tf_op jit(solution)/shard_map/ppermute | solution.py:35
  289.9 8.7 %collective-permute-start.43 = (f32[16,4,8,1]{3,0,2,1:T(8,128)S(1)}, f32[16,4,8,1]{3,0,2,1:T(8,128)S(1)}, u32[]{:S(2)}, u32[]{:S(2)}) collective-permute-start(f32[16,4,8,1]{3,0,2,1:T(8,128)S(1)} %get-tuple-element.88), channel_id=1, source_target_pairs={{1,0},{2,1},{3,2},{4,3},{5,4},{6,5},{7,6},{9,8},{10,9},{11,10},{12... | collective-permute-start | bytes 6152 | tf_op jit(solution)/shard_map/ppermute | solution.py:35
  299.5 15.5 %collective-permute-start.45 = (f32[16,4,1,128]{3,0,2,1:T(8,128)S(1)}, f32[16,4,1,128]{3,0,2,1:T(8,128)S(1)}, u32[]{:S(2)}, u32[]{:S(2)}) collective-permute-start(f32[16,4,1,128]{3,0,2,1:T(8,128)S(1)} %get-tuple-element.85), channel_id=1, source_target_pairs={{0,8},{8,16},{16,24},{24,32},{32,40},{40,48},{48,56},{56,64},{64,7... | collective-permute-start | bytes 98312 | tf_op jit(solution)/shard_map/ppermute | solution.py:35
  303.5 11.5 %collective-permute-start.46 = (f32[16,4,1,128]{3,0,2,1:T(8,128)S(1)}, f32[16,4,1,128]{3,0,2,1:T(8,128)S(1)}, u32[]{:S(2)}, u32[]{:S(2)}) collective-permute-start(f32[16,4,1,128]{3,0,2,1:T(8,128)S(1)} %get-tuple-element.86), channel_id=1, source_target_pairs={{8,0},{16,8},{24,16},{32,24},{40,32},{48,40},{56,48},{64,56},{72,6... | collective-permute-start | bytes 98312 | tf_op jit(solution)/shard_map/ppermute | solution.py:35
  307.0 8.0 %collective-permute-start.47 = (f32[16,4,8,1]{3,0,2,1:T(8,128)S(1)}, f32[16,4,8,1]{3,0,2,1:T(8,128)S(1)}, u32[]{:S(2)}, u32[]{:S(2)}) collective-permute-start(f32[16,4,8,1]{3,0,2,1:T(8,128)S(1)} %get-tuple-element.84), channel_id=1, source_target_pairs={{1,0},{2,1},{3,2},{4,3},{5,4},{6,5},{7,6},{9,8},{10,9},{11,10},{12... | collective-permute-start | bytes 6152 | tf_op jit(solution)/shard_map/ppermute | solution.py:35
  315.9 15.3 %collective-permute-start.49 = (f32[16,4,1,128]{3,0,2,1:T(8,128)S(1)}, f32[16,4,1,128]{3,0,2,1:T(8,128)S(1)}, u32[]{:S(2)}, u32[]{:S(2)}) collective-permute-start(f32[16,4,1,128]{3,0,2,1:T(8,128)S(1)} %get-tuple-element.81), channel_id=1, source_target_pairs={{0,8},{8,16},{16,24},{24,32},{32,40},{40,48},{48,56},{56,64},{64,7... | collective-permute-start | bytes 98312 | tf_op jit(solution)/shard_map/ppermute | solution.py:35
  319.9 11.3 %collective-permute-start.50 = (f32[16,4,1,128]{3,0,2,1:T(8,128)S(1)}, f32[16,4,1,128]{3,0,2,1:T(8,128)S(1)}, u32[]{:S(2)}, u32[]{:S(2)}) collective-permute-start(f32[16,4,1,128]{3,0,2,1:T(8,128)S(1)} %get-tuple-element.82), channel_id=1, source_target_pairs={{8,0},{16,8},{24,16},{32,24},{40,32},{48,40},{56,48},{64,56},{72,6... | collective-permute-start | bytes 98312 | tf_op jit(solution)/shard_map/ppermute | solution.py:35
  323.2 8.0 %collective-permute-start.51 = (f32[16,4,8,1]{3,0,2,1:T(8,128)S(1)}, f32[16,4,8,1]{3,0,2,1:T(8,128)S(1)}, u32[]{:S(2)}, u32[]{:S(2)}) collective-permute-start(f32[16,4,8,1]{3,0,2,1:T(8,128)S(1)} %get-tuple-element.80), channel_id=1, source_target_pairs={{1,0},{2,1},{3,2},{4,3},{5,4},{6,5},{7,6},{9,8},{10,9},{11,10},{12... | collective-permute-start | bytes 6152 | tf_op jit(solution)/shard_map/ppermute | solution.py:35
  389.7 15.0 %collective-permute-start.53 = (f32[16,4,1,128]{3,0,2,1:T(8,128)S(1)}, f32[16,4,1,128]{3,0,2,1:T(8,128)S(1)}, u32[]{:S(2)}, u32[]{:S(2)}) collective-permute-start(f32[16,4,1,128]{3,0,2,1:T(8,128)S(1)} %get-tuple-element.77), channel_id=1, source_target_pairs={{0,8},{8,16},{16,24},{24,32},{32,40},{40,48},{48,56},{56,64},{64,7... | collective-permute-start | bytes 98312 | tf_op jit(solution)/shard_map/ppermute | solution.py:35
  393.2 11.5 %collective-permute-start.54 = (f32[16,4,1,128]{3,0,2,1:T(8,128)S(1)}, f32[16,4,1,128]{3,0,2,1:T(8,128)S(1)}, u32[]{:S(2)}, u32[]{:S(2)}) collective-permute-start(f32[16,4,1,128]{3,0,2,1:T(8,128)S(1)} %get-tuple-element.78), channel_id=1, source_target_pairs={{8,0},{16,8},{24,16},{32,24},{40,32},{48,40},{56,48},{64,56},{72,6... | collective-permute-start | bytes 98312 | tf_op jit(solution)/shard_map/ppermute | solution.py:35
  405.7 17.8 %collective-permute-start.57 = (f32[16,4,1,128]{3,0,2,1:T(8,128)S(1)}, f32[16,4,1,128]{3,0,2,1:T(8,128)S(1)}, u32[]{:S(2)}, u32[]{:S(2)}) collective-permute-start(f32[16,4,1,128]{3,0,2,1:T(8,128)S(1)} %get-tuple-element.73), channel_id=1, source_target_pairs={{0,8},{8,16},{16,24},{24,32},{32,40},{40,48},{48,56},{56,64},{64,7... | collective-permute-start | bytes 98312 | tf_op jit(solution)/shard_map/ppermute | solution.py:35
  411.5 12.0 %collective-permute-start.58 = (f32[16,4,1,128]{3,0,2,1:T(8,128)S(1)}, f32[16,4,1,128]{3,0,2,1:T(8,128)S(1)}, u32[]{:S(2)}, u32[]{:S(2)}) collective-permute-start(f32[16,4,1,128]{3,0,2,1:T(8,128)S(1)} %get-tuple-element.74), channel_id=1, source_target_pairs={{8,0},{16,8},{24,16},{32,24},{40,32},{48,40},{56,48},{64,56},{72,6... | collective-permute-start | bytes 98312 | tf_op jit(solution)/shard_map/ppermute | solution.py:35
  414.8 8.6 %collective-permute-start.59 = (f32[16,4,8,1]{3,0,2,1:T(8,128)S(1)}, f32[16,4,8,1]{3,0,2,1:T(8,128)S(1)}, u32[]{:S(2)}, u32[]{:S(2)}) collective-permute-start(f32[16,4,8,1]{3,0,2,1:T(8,128)S(1)} %get-tuple-element.72), channel_id=1, source_target_pairs={{1,0},{2,1},{3,2},{4,3},{5,4},{6,5},{7,6},{9,8},{10,9},{11,10},{12... | collective-permute-start | bytes 6152 | tf_op jit(solution)/shard_map/ppermute | solution.py:35
  424.4 15.3 %collective-permute-start.61 = (f32[16,4,1,128]{3,0,2,1:T(8,128)S(1)}, f32[16,4,1,128]{3,0,2,1:T(8,128)S(1)}, u32[]{:S(2)}, u32[]{:S(2)}) collective-permute-start(f32[16,4,1,128]{3,0,2,1:T(8,128)S(1)} %get-tuple-element.69), channel_id=1, source_target_pairs={{0,8},{8,16},{16,24},{24,32},{32,40},{40,48},{48,56},{56,64},{64,7... | collective-permute-start | bytes 98312 | tf_op jit(solution)/shard_map/ppermute | solution.py:35
  428.5 11.3 %collective-permute-start.62 = (f32[16,4,1,128]{3,0,2,1:T(8,128)S(1)}, f32[16,4,1,128]{3,0,2,1:T(8,128)S(1)}, u32[]{:S(2)}, u32[]{:S(2)}) collective-permute-start(f32[16,4,1,128]{3,0,2,1:T(8,128)S(1)} %get-tuple-element.70), channel_id=1, source_target_pairs={{8,0},{16,8},{24,16},{32,24},{40,32},{48,40},{56,48},{64,56},{72,6... | collective-permute-start | bytes 98312 | tf_op jit(solution)/shard_map/ppermute | solution.py:35
  440.7 15.3 %collective-permute-start.65 = (f32[16,4,1,128]{3,0,2,1:T(8,128)S(1)}, f32[16,4,1,128]{3,0,2,1:T(8,128)S(1)}, u32[]{:S(2)}, u32[]{:S(2)}) collective-permute-start(f32[16,4,1,128]{3,0,2,1:T(8,128)S(1)} %get-tuple-element.65), channel_id=1, source_target_pairs={{0,8},{8,16},{16,24},{24,32},{32,40},{40,48},{48,56},{56,64},{64,7... | collective-permute-start | bytes 98312 | tf_op jit(solution)/shard_map/ppermute | solution.py:35
  444.7 11.3 %collective-permute-start.66 = (f32[16,4,1,128]{3,0,2,1:T(8,128)S(1)}, f32[16,4,1,128]{3,0,2,1:T(8,128)S(1)}, u32[]{:S(2)}, u32[]{:S(2)}) collective-permute-start(f32[16,4,1,128]{3,0,2,1:T(8,128)S(1)} %get-tuple-element.66), channel_id=1, source_target_pairs={{8,0},{16,8},{24,16},{32,24},{40,32},{48,40},{56,48},{64,56},{72,6... | collective-permute-start | bytes 98312 | tf_op jit(solution)/shard_map/ppermute | solution.py:35
  509.9 15.1 %collective-permute-start.69 = (f32[16,4,1,128]{3,0,2,1:T(8,128)S(1)}, f32[16,4,1,128]{3,0,2,1:T(8,128)S(1)}, u32[]{:S(2)}, u32[]{:S(2)}) collective-permute-start(f32[16,4,1,128]{3,0,2,1:T(8,128)S(1)} %get-tuple-element.61), channel_id=1, source_target_pairs={{0,8},{8,16},{16,24},{24,32},{32,40},{40,48},{48,56},{56,64},{64,7... | collective-permute-start | bytes 98312 | tf_op jit(solution)/shard_map/ppermute | solution.py:35
  513.5 11.5 %collective-permute-start.70 = (f32[16,4,1,128]{3,0,2,1:T(8,128)S(1)}, f32[16,4,1,128]{3,0,2,1:T(8,128)S(1)}, u32[]{:S(2)}, u32[]{:S(2)}) collective-permute-start(f32[16,4,1,128]{3,0,2,1:T(8,128)S(1)} %get-tuple-element.62), channel_id=1, source_target_pairs={{8,0},{16,8},{24,16},{32,24},{40,32},{48,40},{56,48},{64,56},{72,6... | collective-permute-start | bytes 98312 | tf_op jit(solution)/shard_map/ppermute | solution.py:35
  525.9 17.8 %collective-permute-start.73 = (f32[16,4,1,128]{3,0,2,1:T(8,128)S(1)}, f32[16,4,1,128]{3,0,2,1:T(8,128)S(1)}, u32[]{:S(2)}, u32[]{:S(2)}) collective-permute-start(f32[16,4,1,128]{3,0,2,1:T(8,128)S(1)} %get-tuple-element.57), channel_id=1, source_target_pairs={{0,8},{8,16},{16,24},{24,32},{32,40},{40,48},{48,56},{56,64},{64,7... | collective-permute-start | bytes 98312 | tf_op jit(solution)/shard_map/ppermute | solution.py:35
  531.6 12.1 %collective-permute-start.74 = (f32[16,4,1,128]{3,0,2,1:T(8,128)S(1)}, f32[16,4,1,128]{3,0,2,1:T(8,128)S(1)}, u32[]{:S(2)}, u32[]{:S(2)}) collective-permute-start(f32[16,4,1,128]{3,0,2,1:T(8,128)S(1)} %get-tuple-element.58), channel_id=1, source_target_pairs={{8,0},{16,8},{24,16},{32,24},{40,32},{48,40},{56,48},{64,56},{72,6... | collective-permute-start | bytes 98312 | tf_op jit(solution)/shard_map/ppermute | solution.py:35
  535.0 8.7 %collective-permute-start.75 = (f32[16,4,8,1]{3,0,2,1:T(8,128)S(1)}, f32[16,4,8,1]{3,0,2,1:T(8,128)S(1)}, u32[]{:S(2)}, u32[]{:S(2)}) collective-permute-start(f32[16,4,8,1]{3,0,2,1:T(8,128)S(1)} %get-tuple-element.56), channel_id=1, source_target_pairs={{1,0},{2,1},{3,2},{4,3},{5,4},{6,5},{7,6},{9,8},{10,9},{11,10},{12... | collective-permute-start | bytes 6152 | tf_op jit(solution)/shard_map/ppermute | solution.py:35
  544.7 15.3 %collective-permute-start.77 = (f32[16,4,1,128]{3,0,2,1:T(8,128)S(1)}, f32[16,4,1,128]{3,0,2,1:T(8,128)S(1)}, u32[]{:S(2)}, u32[]{:S(2)}) collective-permute-start(f32[16,4,1,128]{3,0,2,1:T(8,128)S(1)} %get-tuple-element.53), channel_id=1, source_target_pairs={{0,8},{8,16},{16,24},{24,32},{32,40},{40,48},{48,56},{56,64},{64,7... | collective-permute-start | bytes 98312 | tf_op jit(solution)/shard_map/ppermute | solution.py:35
  548.7 11.3 %collective-permute-start.78 = (f32[16,4,1,128]{3,0,2,1:T(8,128)S(1)}, f32[16,4,1,128]{3,0,2,1:T(8,128)S(1)}, u32[]{:S(2)}, u32[]{:S(2)}) collective-permute-start(f32[16,4,1,128]{3,0,2,1:T(8,128)S(1)} %get-tuple-element.54), channel_id=1, source_target_pairs={{8,0},{16,8},{24,16},{32,24},{40,32},{48,40},{56,48},{64,56},{72,6... | collective-permute-start | bytes 98312 | tf_op jit(solution)/shard_map/ppermute | solution.py:35
  561.0 15.3 %collective-permute-start.81 = (f32[16,4,1,128]{3,0,2,1:T(8,128)S(1)}, f32[16,4,1,128]{3,0,2,1:T(8,128)S(1)}, u32[]{:S(2)}, u32[]{:S(2)}) collective-permute-start(f32[16,4,1,128]{3,0,2,1:T(8,128)S(1)} %get-tuple-element.49), channel_id=1, source_target_pairs={{0,8},{8,16},{16,24},{24,32},{32,40},{40,48},{48,56},{56,64},{64,7... | collective-permute-start | bytes 98312 | tf_op jit(solution)/shard_map/ppermute | solution.py:35
  565.0 11.3 %collective-permute-start.82 = (f32[16,4,1,128]{3,0,2,1:T(8,128)S(1)}, f32[16,4,1,128]{3,0,2,1:T(8,128)S(1)}, u32[]{:S(2)}, u32[]{:S(2)}) collective-permute-start(f32[16,4,1,128]{3,0,2,1:T(8,128)S(1)} %get-tuple-element.50), channel_id=1, source_target_pairs={{8,0},{16,8},{24,16},{32,24},{40,32},{48,40},{56,48},{64,56},{72,6... | collective-permute-start | bytes 98312 | tf_op jit(solution)/shard_map/ppermute | solution.py:35
  (38 other events, 252.9 us)

commit v3 on v0

--- a/solution.py
+++ b/solution.py
@@ -2,6 +2,8 @@
 import jax.numpy as jnp
 from jax import lax
 from jax.sharding import PartitionSpec as P
+from jax.experimental import pallas as pl
+from jax.experimental.pallas import tpu as pltpu
 
 RHS = 16
 S = 4
@@ -20,6 +22,222 @@
         after = lax.ppermute(leading, axis, down)
         array = jnp.concatenate([before, array, after], axis=dim)
     return array
+
+
+def exchange_reduce(axis, other_axis, n, src, mine, rs, ag, full, send_sem, rs_sem, ag_sem):
+    me = lax.axis_index(axis)
+    other = lax.axis_index(other_axis)
+    part = src.shape[0] // n
+
+    def scatter(j, slot):
+        return pltpu.make_async_remote_copy(
+            src_ref=src.at[pl.ds(j * part, part)], dst_ref=rs.at[slot], send_sem=send_sem.at[j],
+            recv_sem=rs_sem.at[slot], device_id=_device(axis, j, other_axis, other),
+            device_id_type=pl.DeviceIdType.MESH,
+        )
+
+    def gather(j, slot):
+        return pltpu.make_async_remote_copy(
+            src_ref=mine, dst_ref=ag.at[slot], send_sem=send_sem.at[j],
+            recv_sem=ag_sem.at[slot], device_id=_device(axis, j, other_axis, other),
+            device_id_type=pl.DeviceIdType.MESH,
+        )
+
+    for j in range(n):
+        @pl.when(j != me)
+        def _():
+            scatter(j, me).start()
+    rs[me] = src[pl.ds(pl.multiple_of(me * part, part), part)]
+    for j in range(n):
+        @pl.when(j != me)
+        def _():
+            scatter(j, me).wait_send()
+            scatter(j, j).wait_recv()
+    acc = rs[0]
+    for j in range(1, n):
+        acc = acc + rs[j]
+    mine[...] = acc
+    for j in range(n):
+        @pl.when(j != me)
+        def _():
+            gather(j, me).start()
+    ag[me] = acc
+    for j in range(n):
+        @pl.when(j != me)
+        def _():
+            gather(j, me).wait_send()
+            gather(j, j).wait_recv()
+    for j in range(n):
+        full[pl.ds(j * part, part)] = ag[j]
+
+
+def reduce_kernel(nx, ny, x_ref, o_ref, gy_full, mine_y, rs_y, ag_y, mine_x, rs_x, ag_x,
+                  y_send, y_rs, y_ag, x_send, x_rs, x_ag):
+    gx = lax.axis_index("gx")
+    gy = lax.axis_index("gy")
+    barrier = pltpu.get_barrier_semaphore()
+    for j in range(nx):
+        @pl.when(j != gx)
+        def _():
+            pl.semaphore_signal(barrier, inc=1, device_id={"gx": j, "gy": gy},
+                                device_id_type=pl.DeviceIdType.MESH)
+    for j in range(ny):
+        @pl.when(j != gy)
+        def _():
+            pl.semaphore_signal(barrier, inc=1, device_id={"gx": gx, "gy": j},
+                                device_id_type=pl.DeviceIdType.MESH)
+    pl.semaphore_wait(barrier, nx + ny - 2)
+    exchange_reduce("gy", "gx", ny, x_ref, mine_y, rs_y, ag_y, gy_full, y_send, y_rs, y_ag)
+    exchange_reduce("gx", "gy", nx, gy_full, mine_x, rs_x, ag_x, o_ref, x_send, x_rs, x_ag)
+
+
+def gram_sum(local_gram):
+    size = local_gram.shape[0]
+    nx, ny = lax.axis_size("gx"), lax.axis_size("gy")
+    pad = 128
+    py, px = pad // ny, pad // nx
+    f32 = jnp.float32
+    wide = jnp.pad(local_gram, ((0, pad - size), (0, pad - size)))
+    vmem = pl.BlockSpec(memory_space=pltpu.VMEM)
+    total = pl.pallas_call(
+        lambda *refs: reduce_kernel(nx, ny, *refs),
+        out_shape=jax.ShapeDtypeStruct((pad, pad), f32),
+        in_specs=[vmem],
+        out_specs=vmem,
+        scratch_shapes=[
+            pltpu.VMEM((pad, pad), f32),
+            pltpu.VMEM((py, pad), f32),
+            pltpu.VMEM((ny, py, pad), f32),
+            pltpu.VMEM((ny, py, pad), f32),
+            pltpu.VMEM((px, pad), f32),
+            pltpu.VMEM((nx, px, pad), f32),
+            pltpu.VMEM((nx, px, pad), f32),
+            pltpu.SemaphoreType.DMA((ny,)),
+            pltpu.SemaphoreType.DMA((ny,)),
+            pltpu.SemaphoreType.DMA((ny,)),
+            pltpu.SemaphoreType.DMA((nx,)),
+            pltpu.SemaphoreType.DMA((nx,)),
+            pltpu.SemaphoreType.DMA((nx,)),
+        ],
+        compiler_params=pltpu.CompilerParams(collective_id=4, has_side_effects=True),
+        name="gram_allreduce",
+    )(wide)
+    return total[:size, :size]
+
+
+def krylov_kernel(nx, ny, bx, v0_ref, terms_ref, diag_ref, out_ref,
+                  halo_x, xsend, ysend, xr, yr, send_sem, recv_sem):
+    gx = lax.axis_index("gx")
+    gy = lax.axis_index("gy")
+    rhs = out_ref.shape[1] // terms_ref.shape[1]
+    rows, lanes = terms_ref.shape[1], terms_ref.shape[2]
+    cells = out_ref.shape[1]
+    zero_x = jnp.zeros(xr.shape[2:], jnp.float32)
+    zero_y = jnp.zeros(yr.shape[2:], jnp.float32)
+    for k in range(xr.shape[0]):
+        for d in range(2):
+            xr[k, d] = zero_x
+            yr[k, d] = zero_y
+    targets = (
+        (gx < nx - 1, {"gx": gx + 1, "gy": gy}, gx > 0),
+        (gx > 0, {"gx": gx - 1, "gy": gy}, gx < nx - 1),
+        (gy < ny - 1, {"gx": gx, "gy": gy + 1}, gy > 0),
+        (gy > 0, {"gx": gx, "gy": gy - 1}, gy < ny - 1),
+    )
+    barrier = pltpu.get_barrier_semaphore()
+    for has_target, target, _ in targets:
+        @pl.when(has_target)
+        def _():
+            pl.semaphore_signal(barrier, inc=1, device_id=target, device_id_type=pl.DeviceIdType.MESH)
+    peers = (gx + nx - 1) // nx + (2 * nx - 2 - gx) // nx + (gy + ny - 1) // ny + (2 * ny - 2 - gy) // ny
+    pl.semaphore_wait(barrier, peers)
+
+    row = lax.broadcasted_iota(jnp.int32, (rhs, rows, lanes), 1)
+    lane = lax.broadcasted_iota(jnp.int32, (rhs, rows, lanes), 2)
+    xpos = row % bx
+    zpos = row // bx
+    nzp = rows // bx
+    t = [terms_ref[i][None] for i in range(6)]
+    diag = diag_ref[...][None]
+    trow = lax.broadcasted_iota(jnp.int32, (lanes, cells), 0)
+
+    out_ref[0] = v0_ref[...]
+    for k in range(xr.shape[0]):
+        flat = out_ref[k]
+        xsend[0] = out_ref[k, pl.ds(0, cells // bx, stride=bx), :]
+        xsend[1] = out_ref[k, pl.ds(bx - 1, cells // bx, stride=bx), :]
+        tr = flat.T
+        ysend[...] = jnp.where(trow[:8] == 0, tr[0:1], jnp.where(trow[:8] == 1, tr[lanes - 1:lanes], 0.0))
+        plan = (
+            (xsend.at[1], xr.at[k, 0]),
+            (xsend.at[0], xr.at[k, 1]),
+            (ysend, yr.at[k, 0]),
+            (ysend, yr.at[k, 1]),
+        )
+
+        def copy(d):
+            return pltpu.make_async_remote_copy(
+                src_ref=plan[d][0], dst_ref=plan[d][1], send_sem=send_sem.at[d],
+                recv_sem=recv_sem.at[k, d], device_id=targets[d][1],
+                device_id_type=pl.DeviceIdType.MESH,
+            )
+
+        for d in range(4):
+            @pl.when(targets[d][0])
+            def _():
+                copy(d).start()
+        for d in range(4):
+            @pl.when(targets[d][0])
+            def _():
+                copy(d).wait_send()
+
+            @pl.when(targets[d][2])
+            def _():
+                copy(d).wait_recv()
+
+        halo_x[pl.ds(0, cells // bx, stride=bx), :] = xr[k, 0]
+        halo_x[pl.ds(bx - 1, cells // bx, stride=bx), :] = xr[k, 1]
+        before = yr[k, 0][1:2]
+        after = yr[k, 1][0:1]
+        ycols = jnp.where(trow == 0, before, jnp.where(trow == lanes - 1, after, 0.0)).T
+        v = flat.reshape(rhs, rows, lanes)
+        hx = halo_x[...].reshape(rhs, rows, lanes)
+        hy = ycols.reshape(rhs, rows, lanes)
+        zm = jnp.where(zpos == 0, 0.0, pltpu.roll(v, bx, 1))
+        zp = jnp.where(zpos == nzp - 1, 0.0, pltpu.roll(v, rows - bx, 1))
+        xm = jnp.where(xpos == 0, hx, pltpu.roll(v, 1, 1))
+        xp = jnp.where(xpos == bx - 1, hx, pltpu.roll(v, rows - 1, 1))
+        ym = jnp.where(lane == 0, hy, pltpu.roll(v, 1, 2))
+        yp = jnp.where(lane == lanes - 1, hy, pltpu.roll(v, lanes - 1, 2))
+        total = t[0] * zm + t[1] * zp
+        total = total + t[2] * xm + t[3] * xp
+        total = total + t[4] * ym + t[5] * yp
+        out_ref[k + 1] = (-total / diag).reshape(cells, lanes)
+
+
+def krylov_basis(v0, terms, diagonal):
+    rhs, nz, bx, by = v0.shape
+    nx, ny = lax.axis_size("gx"), lax.axis_size("gy")
+    cells = rhs * nz * bx
+    vmem = pl.BlockSpec(memory_space=pltpu.VMEM)
+    out = pl.pallas_call(
+        lambda *refs: krylov_kernel(nx, ny, bx, *refs),
+        out_shape=jax.ShapeDtypeStruct((S + 1, cells, by), jnp.float32),
+        in_specs=[vmem] * 3,
+        out_specs=vmem,
+        scratch_shapes=[
+            pltpu.VMEM((cells, by), jnp.float32),
+            pltpu.VMEM((2, cells // bx, by), jnp.float32),
+            pltpu.VMEM((8, cells), jnp.float32),
+            pltpu.VMEM((S, 2, cells // bx, by), jnp.float32),
+            pltpu.VMEM((S, 2, 8, cells), jnp.float32),
+            pltpu.SemaphoreType.DMA((4,)),
+            pltpu.SemaphoreType.DMA((S, 4)),
+        ],
+        compiler_params=pltpu.CompilerParams(collective_id=3, has_side_effects=True),
+        name="krylov_basis",
+    )(v0.reshape(cells, by), jnp.stack(terms).reshape(6, nz * bx, by), diagonal.reshape(nz * bx, by))
+    return out.reshape(S + 1, rhs, nz, bx, by)
 
 
 def face_terms(padded, storage):
@@ -36,11 +254,8 @@
     return (terms, diagonal)
 
 
-def apply_off(padded, terms):
-    total = terms[0] * padded[:, :-2, 1:-1, 1:-1] + terms[1] * padded[:, 2:, 1:-1, 1:-1]
-    total = total + terms[2] * padded[:, 1:-1, :-2, 1:-1] + terms[3] * padded[:, 1:-1, 2:, 1:-1]
-    total = total + terms[4] * padded[:, 1:-1, 1:-1, :-2] + terms[5] * padded[:, 1:-1, 1:-1, 2:]
-    return total
+def _device(axis, index, other_axis, other_index):
+    return {axis: index, other_axis: other_index}
 
 
 def small_solve(gram_all):
@@ -67,17 +282,14 @@
     solution = jnp.zeros(shape, jnp.float32)
     residual = pumping / diagonal
     for restart in range(CYCLES):
-        blocks = [residual]
-        for k in range(S):
-            bordered = padded_2(blocks[-1], (("gx", 2), ("gy", 3)), 1)
-            padded = jnp.pad(bordered, ((0, 0), (1, 1), (0, 0), (0, 0)))
-            blocks.append(-apply_off(padded, terms) / diagonal)
-        stacked = jnp.concatenate(blocks, 0).reshape(BASIS, -1)
+        stacked = krylov_basis(residual, terms, diagonal).reshape(BASIS, -1)
         local_gram = jnp.dot(stacked, stacked.T, precision=hp)
-        gram_all = lax.psum(local_gram, ("gx", "gy"))
+        gram_all = gram_sum(local_gram)
         y, coeffs = small_solve(gram_all)
-        solution = solution + jnp.dot(y.T, stacked[: BASIS - RHS], precision=hp).reshape(shape)
-        residual = jnp.dot(coeffs.T, stacked, precision=hp).reshape(shape)
+        y_full = jnp.concatenate([y, jnp.zeros((RHS, RHS), jnp.float32)], axis=0)
+        both = jnp.dot(jnp.concatenate([y_full, coeffs], axis=1).T, stacked, precision=hp)
+        solution = solution + both[:RHS].reshape(shape)
+        residual = both[RHS:].reshape(shape)
     return (solution, residual)
 
 

time: 894 us -> 350 us (0.39)
  blocking collectives: 334 us -> 0 us
  Pallas kernels: 0 us -> 222 us
  starting transfers between devices: 214 us -> 12.8 us
  waiting for transfers between devices: 190 us -> 4 us
  matrix products: 34 us -> 21 us
  local copies, waits for them, and re-layouts: 30.1 us -> 17.2 us
  other arithmetic: 80.5 us -> 68.9 us
    psum x5 -> x0, blocking collectives: 334 us -> none  [shards(): gram_all = lax.psum(local_gram, ('gx', 'gy'))]
    pallas_call x0 -> x10, Pallas kernels: none -> 222 us  [the longest x5 127 us: gram_sum(): pl.pallas_call(lambda *refs: reduce_kernel(nx, ny, *refs), out_shape=jax....]
    ppermute x42 -> x2, waiting for transfers between devices: 157 us -> 3.29 us  [padded_2(): after = lax.ppermute(leading, axis, down)]
    ppermute x42 -> x2, starting transfers between devices: 145 us -> 9.62 us  [padded_2(): before = lax.ppermute(last, axis, up)]
    ppermute x42 -> x2, starting transfers between devices: 68.6 us -> 3.2 us  [padded_2(): after = lax.ppermute(leading, axis, down)]
    ppermute x42 -> x2, waiting for transfers between devices: 32.5 us -> 0.71 us  [padded_2(): before = lax.ppermute(last, axis, up)]
    unnamed x46 -> x8, local copies, waits for them, and re-layouts: 18.2 us -> 2.15 us
    dot_general x10 -> x5, matrix products: 18.2 us -> 3.94 us  [shards(): jnp.dot(jnp.concatenate([y_full, coeffs], axis=1).T, stacked, precision=hp)]
  transfers between devices with their start and end apart: 84 -> 4, of which waited for: 61 -> 2; matrix products, arithmetic and copies ran while one was open for 2% -> 0% of each run, Pallas kernels for 0% -> 0%
where the time goes in v3:
time: 350 us; the launch traced here: 347 us
  Pallas kernels  222 us (63%)
  other arithmetic  68.9 us (20%)
  matrix products  21 us (6%)
  local copies, waits for them, and re-layouts  17.2 us (5%)
  starting transfers between devices  12.8 us (4%)
  waiting for transfers between devices  4 us (1%)
    pallas_call x5, Pallas kernels, gram_sum(): pl.pallas_call(lambda *refs: reduce_kernel(nx, ny, *refs), out_shape=jax....  127 us
    pallas_call x5, Pallas kernels, krylov_basis(): pl.pallas_call(lambda *refs: krylov_kernel(nx, ny, bx, *refs), out_shape=...  95.5 us
    another operation x15, other arithmetic, small_solve(): lower = jnp.linalg.cholesky(normal)  32.6 us
    another operation x10, other arithmetic, small_solve(): y = jax.scipy.linalg.cho_solve((lower, True), right_side)  27.7 us
    ppermute x2, starting transfers between devices, padded_2(): before = lax.ppermute(last, axis, up)  9.62 us
    another operation x5, local copies, waits for them, and re-layouts, shards(): stacked = krylov_basis(residual, terms, diagonal).reshape(BASIS, -1)  7.57 us
  transfers between devices with their start and end apart: 4, of which 2 were waited for; matrix products, arithmetic and copies ran while one was open for 0% of the time, Pallas kernels for 0%

profile of v3, /device:TPU:1, one launch (start us, length us, event | category | flops | bytes accessed | tf_op | source)
XLA Modules:
  0.0 347.5 jit_solution(13712520910885608188)
XLA Ops:
  0.6 0.8 fusion.118
  1.5 1.3 collective-permute-start.1
  2.8 4.7 %collective-permute-start = (f32[4,1,128]{2,1,0:T(1,128)S(1)}, f32[4,1,128]{2,1,0:T(1,128)S(1)}, u32[]{:S(2)}, u32[]{:S(2)}) collective-permute-start(f32[4,1,128]{2,1,0:T(1,128)S(1)} %get-tuple-element.9), channel_id=1, source_target_pairs={{0,8},{8,16},{16,24},{24,32},{32,40},{40,48},{48,56},{56,64},{64,7... | collective-permute-start | bytes 6152 | tf_op jit(solution)/shard_map/ppermute | solution.py:21
  8.9 5.0 %collective-permute-start.2 = (f32[4,10,1]{2,1,0:T(8,128)S(1)}, f32[4,10,1]{2,1,0:T(8,128)S(1)}, u32[]{:S(2)}, u32[]{:S(2)}) collective-permute-start(f32[4,10,1]{2,1,0:T(8,128)S(1)} %get-tuple-element.6), channel_id=1, source_target_pairs={{0,1},{1,2},{2,3},{3,4},{4,5},{5,6},{6,7},{8,9},{9,10},{10,11},{11... | collective-permute-start | bytes 488 | tf_op jit(solution)/shard_map/ppermute | solution.py:21
  13.9 1.9 collective-permute-start.3
  15.9 3.3 collective-permute-done.3
  19.1 0.8 select_maximum_fusion
  20.0 0.8 bitcast_dynamic-update-slice_fusion.5
  21.6 1.0 add_add_fusion
  22.6 1.7 broadcast_divide_fusion
  24.3 0.8 bitcast_dynamic-update-slice_fusion.3
  25.1 0.8 bitcast_dynamic-update-slice_fusion.2
  25.9 0.9 bitcast_dynamic-update-slice_fusion.1
  27.5 22.5 %krylov_basis.5 = f32[5,512,128]{2,1,0:T(8,128)} custom-call(f32[512,128]{1,0:T(8,128)} %bitcast.117, f32[6,32,128]{2,1,0:T(8,128)} %copy-done, f32[32,128]{1,0:T(8,128)} %bitcast.118), custom_call_target="tpu_custom_call" | custom-call | tf_op jit(solution)/shard_map/krylov_basis/pallas_call | solution.py:223
  49.9 1.5 reshape_reshape.27
  51.5 1.2 fusion.119
  53.3 26.5 %gram_allreduce.5 = f32[128,128]{1,0:T(8,128)} custom-call(f32[128,128]{1,0:T(8,128)} %pad.26.refs_0_), custom_call_target="tpu_custom_call" | custom-call | tf_op jit(solution)/shard_map/gram_allreduce/pallas_call | solution.py:102
  79.8 1.1 fusion.10
  81.5 5.8 %cholesky.89 = f32[64,64]{1,0:T(8,128)S(1)} custom-call(f32[64,64]{1,0:T(8,128)S(1)} %fusion.46), custom_call_target="Cholesky" | custom-call | tf_op jit(solution)/shard_map/jit(cholesky)/cholesky | solution.py:270
  88.6 4.9 %custom-call.11 = f32[1,64,64]{1,2,0:T(8,128)S(1)} custom-call(f32[1,64,64]{2,1,0:T(8,128)S(1)} %fusion.17), custom_call_target="InvertDiagBlocksLowerTriangular" | custom-call | tf_op jit(solution)/shard_map/jit(_cho_solve)/triangular_solve | solution.py:271
  95.8 18.3 %krylov_basis.6 = f32[5,512,128]{2,1,0:T(8,128)} custom-call(f32[512,128]{1,0:T(8,128)} %reshape_reshape.28.refs_0_, f32[6,32,128]{2,1,0:T(8,128)} %copy-done, f32[32,128]{1,0:T(8,128)} %bitcast.119), custom_call_target="tpu_custom_call" | custom-call | tf_op jit(solution)/shard_map/krylov_basis/pallas_call | solution.py:223
  114.1 1.5 reshape_reshape.29
  115.6 1.2 fusion.120
  117.4 25.0 %gram_allreduce.6 = f32[128,128]{1,0:T(8,128)} custom-call(f32[128,128]{1,0:T(8,128)} %pad.27.refs_0_), custom_call_target="tpu_custom_call" | custom-call | tf_op jit(solution)/shard_map/gram_allreduce/pallas_call | solution.py:102
  142.5 1.1 fusion.8
  144.2 5.8 %cholesky.100 = f32[64,64]{1,0:T(8,128)S(1)} custom-call(f32[64,64]{1,0:T(8,128)S(1)} %fusion.41), custom_call_target="Cholesky" | custom-call | tf_op jit(solution)/shard_map/jit(cholesky)/cholesky | solution.py:270
  151.3 4.9 %custom-call.12 = f32[1,64,64]{1,2,0:T(8,128)S(1)} custom-call(f32[1,64,64]{2,1,0:T(8,128)S(1)} %fusion.18), custom_call_target="InvertDiagBlocksLowerTriangular" | custom-call | tf_op jit(solution)/shard_map/jit(_cho_solve)/triangular_solve | solution.py:271
  158.5 18.3 %krylov_basis.7 = f32[5,512,128]{2,1,0:T(8,128)} custom-call(f32[512,128]{1,0:T(8,128)} %reshape_reshape.30.refs_0_, f32[6,32,128]{2,1,0:T(8,128)} %copy-done, f32[32,128]{1,0:T(8,128)} %bitcast.120), custom_call_target="tpu_custom_call" | custom-call | tf_op jit(solution)/shard_map/krylov_basis/pallas_call | solution.py:223
  176.8 1.5 reshape_reshape.31
  178.3 1.2 fusion.121
  180.1 25.1 %gram_allreduce.7 = f32[128,128]{1,0:T(8,128)} custom-call(f32[128,128]{1,0:T(8,128)} %pad.28.refs_0_), custom_call_target="tpu_custom_call" | custom-call | tf_op jit(solution)/shard_map/gram_allreduce/pallas_call | solution.py:102
  205.2 1.1 fusion.6
  206.9 5.8 %cholesky.111 = f32[64,64]{1,0:T(8,128)S(1)} custom-call(f32[64,64]{1,0:T(8,128)S(1)} %fusion.36), custom_call_target="Cholesky" | custom-call | tf_op jit(solution)/shard_map/jit(cholesky)/cholesky | solution.py:270
  214.1 4.9 %custom-call.13 = f32[1,64,64]{1,2,0:T(8,128)S(1)} custom-call(f32[1,64,64]{2,1,0:T(8,128)S(1)} %fusion.19), custom_call_target="InvertDiagBlocksLowerTriangular" | custom-call | tf_op jit(solution)/shard_map/jit(_cho_solve)/triangular_solve | solution.py:271
  221.2 18.3 %krylov_basis.8 = f32[5,512,128]{2,1,0:T(8,128)} custom-call(f32[512,128]{1,0:T(8,128)} %reshape_reshape.32.refs_0_, f32[6,32,128]{2,1,0:T(8,128)} %copy-done, f32[32,128]{1,0:T(8,128)} %bitcast.121), custom_call_target="tpu_custom_call" | custom-call | tf_op jit(solution)/shard_map/krylov_basis/pallas_call | solution.py:223
  239.5 1.5 reshape_reshape.33
  241.0 1.2 fusion.122
  242.8 25.1 %gram_allreduce.8 = f32[128,128]{1,0:T(8,128)} custom-call(f32[128,128]{1,0:T(8,128)} %pad.29.refs_0_), custom_call_target="tpu_custom_call" | custom-call | tf_op jit(solution)/shard_map/gram_allreduce/pallas_call | solution.py:102
  267.9 1.1 fusion.4
  269.6 5.8 %cholesky.122 = f32[64,64]{1,0:T(8,128)S(1)} custom-call(f32[64,64]{1,0:T(8,128)S(1)} %fusion.31), custom_call_target="Cholesky" | custom-call | tf_op jit(solution)/shard_map/jit(cholesky)/cholesky | solution.py:270
  276.8 4.9 %custom-call.14 = f32[1,64,64]{1,2,0:T(8,128)S(1)} custom-call(f32[1,64,64]{2,1,0:T(8,128)S(1)} %fusion.20), custom_call_target="InvertDiagBlocksLowerTriangular" | custom-call | tf_op jit(solution)/shard_map/jit(_cho_solve)/triangular_solve | solution.py:271
  284.0 18.2 %krylov_basis.9 = f32[5,512,128]{2,1,0:T(8,128)} custom-call(f32[512,128]{1,0:T(8,128)} %reshape_reshape.34.refs_0_, f32[6,32,128]{2,1,0:T(8,128)} %copy-done, f32[32,128]{1,0:T(8,128)} %bitcast.122), custom_call_target="tpu_custom_call" | custom-call | tf_op jit(solution)/shard_map/krylov_basis/pallas_call | solution.py:223
  302.2 1.5 reshape_reshape.35
  303.7 1.2 fusion.123
  305.5 25.1 %gram_allreduce.9 = f32[128,128]{1,0:T(8,128)} custom-call(f32[128,128]{1,0:T(8,128)} %pad.30.refs_0_), custom_call_target="tpu_custom_call" | custom-call | tf_op jit(solution)/shard_map/gram_allreduce/pallas_call | solution.py:102
  330.6 1.1 fusion.2
  332.3 5.8 %cholesky.133 = f32[64,64]{1,0:T(8,128)S(1)} custom-call(f32[64,64]{1,0:T(8,128)S(1)} %fusion.26), custom_call_target="Cholesky" | custom-call | tf_op jit(solution)/shard_map/jit(cholesky)/cholesky | solution.py:270
  339.5 4.9 %custom-call.15 = f32[1,64,64]{1,2,0:T(8,128)S(1)} custom-call(f32[1,64,64]{2,1,0:T(8,128)S(1)} %fusion.21), custom_call_target="InvertDiagBlocksLowerTriangular" | custom-call | tf_op jit(solution)/shard_map/jit(_cho_solve)/triangular_solve | solution.py:271
  (85 shorter events, 27.6 us)
Async XLA Ops:
  0.6 26.1 %copy-start.1 = (f32[4,8,128]{2,1,0:T(8,128)S(1)}, f32[4,8,128]{2,1,0:T(8,128)}, u32[]{:S(2)}) copy-start(f32[4,8,128]{2,1,0:T(8,128)} %param.7) | copy-start | bytes 49156
  1.5 6.0 %collective-permute-start.1 = (f32[4,1,128]{2,1,0:T(1,128)S(1)}, f32[4,1,128]{2,1,0:T(1,128)S(1)}, u32[]{:S(2)}, u32[]{:S(2)}) collective-permute-start(f32[4,1,128]{2,1,0:T(1,128)S(1)} %get-tuple-element.8), channel_id=1, source_target_pairs={{8,0},{16,8},{24,16},{32,24},{40,32},{48,40},{56,48},{64,56},{72,6... | collective-permute-start | bytes 6152 | tf_op jit(solution)/shard_map/ppermute | solution.py:22
  2.8 5.4 %collective-permute-start = (f32[4,1,128]{2,1,0:T(1,128)S(1)}, f32[4,1,128]{2,1,0:T(1,128)S(1)}, u32[]{:S(2)}, u32[]{:S(2)}) collective-permute-start(f32[4,1,128]{2,1,0:T(1,128)S(1)} %get-tuple-element.9), channel_id=1, source_target_pairs={{0,8},{8,16},{16,24},{24,32},{32,40},{40,48},{48,56},{56,64},{64,7... | collective-permute-start | bytes 6152 | tf_op jit(solution)/shard_map/ppermute | solution.py:21
  8.9 6.9 %collective-permute-start.2 = (f32[4,10,1]{2,1,0:T(8,128)S(1)}, f32[4,10,1]{2,1,0:T(8,128)S(1)}, u32[]{:S(2)}, u32[]{:S(2)}) collective-permute-start(f32[4,10,1]{2,1,0:T(8,128)S(1)} %get-tuple-element.6), channel_id=1, source_target_pairs={{0,1},{1,2},{2,3},{3,4},{4,5},{5,6},{6,7},{8,9},{9,10},{10,11},{11... | collective-permute-start | bytes 488 | tf_op jit(solution)/shard_map/ppermute | solution.py:21
  13.9 5.2 %collective-permute-start.3 = (f32[4,10,1]{2,1,0:T(8,128)S(1)}, f32[4,10,1]{2,1,0:T(8,128)S(1)}, u32[]{:S(2)}, u32[]{:S(2)}) collective-permute-start(f32[4,10,1]{2,1,0:T(8,128)S(1)} %get-tuple-element.7), channel_id=1, source_target_pairs={{1,0},{2,1},{3,2},{4,3},{5,4},{6,5},{7,6},{9,8},{10,9},{11,10},{12... | collective-permute-start | bytes 488 | tf_op jit(solution)/shard_map/ppermute | solution.py:22
  22.6 4.3 %copy-start.2 = (f32[4,8,128]{2,1,0:T(8,128)}, f32[4,8,128]{2,1,0:T(8,128)S(1)}, u32[]{:S(2)}) copy-start(f32[4,8,128]{2,1,0:T(8,128)S(1)} %add_add_fusion) | copy-start | bytes 49156
  26.8 0.6 copy-start

commit v4 on v3

--- a/solution.py
+++ b/solution.py
@@ -122,7 +122,52 @@
         compiler_params=pltpu.CompilerParams(collective_id=4, has_side_effects=True),
         name="gram_allreduce",
     )(wide)
-    return total[:size, :size]
+    return total
+
+
+def solve_kernel(g_ref, y_ref):
+    n, r = BASIS - RHS, RHS
+    g = g_ref[...]
+    lanes = g.shape[1]
+    a1 = g[0:n] + g[r:r + n]
+    lane = lax.broadcasted_iota(jnp.int32, (n, lanes), 1)
+    row = lax.broadcasted_iota(jnp.int32, (n, lanes), 0)
+    normal = a1 + pltpu.roll(a1, lanes - r, 1)
+    m = jnp.where(lane < n, normal, jnp.where(lane < n + r, pltpu.roll(a1, n, 1), 0.0))
+    upper = []
+    for j in range(n):
+        rowj = m[j:j + 1, :]
+        d = jnp.sqrt(rowj[:, j:j + 1])
+        urow = rowj / d
+        upper.append(urow)
+        col = jnp.where(row > j, m[:, j:j + 1] / d, 0.0)
+        m = m - col * urow
+    w = jnp.concatenate(upper, axis=0)
+    rhs_lane = jnp.logical_and(lane >= n, lane < n + r)
+    ys = [None] * n
+    for j in reversed(range(n)):
+        yj = jnp.where(rhs_lane[0:1], w[j:j + 1, :] / w[j:j + 1, j:j + 1], 0.0)
+        ys[j] = yj
+        col = jnp.where(row < j, w[:, j:j + 1], 0.0)
+        w = w - col * yj
+    y = jnp.concatenate(ys, axis=0)
+    y_ref[...] = pltpu.roll(y, lanes - n, 1)[:, 0:r]
+
+
+def small_solve_fast(gram_pad):
+    y = pl.pallas_call(
+        solve_kernel,
+        out_shape=jax.ShapeDtypeStruct((BASIS - RHS, RHS), jnp.float32),
+        in_specs=[pl.BlockSpec(memory_space=pltpu.VMEM)],
+        out_specs=pl.BlockSpec(memory_space=pltpu.VMEM),
+        name="small_solve",
+    )(gram_pad)
+    shift_matrix = jnp.eye(BASIS, BASIS - RHS, dtype=jnp.float32) + jnp.eye(
+        BASIS, BASIS - RHS, k=-RHS, dtype=jnp.float32
+    )
+    first_block = jnp.eye(BASIS, RHS, dtype=jnp.float32)
+    coeffs = first_block - jnp.dot(shift_matrix, y, precision=lax.Precision.HIGHEST)
+    return (y, coeffs)
 
 
 def krylov_kernel(nx, ny, bx, v0_ref, terms_ref, diag_ref, out_ref,
@@ -284,8 +329,7 @@
     for restart in range(CYCLES):
         stacked = krylov_basis(residual, terms, diagonal).reshape(BASIS, -1)
         local_gram = jnp.dot(stacked, stacked.T, precision=hp)
-        gram_all = gram_sum(local_gram)
-        y, coeffs = small_solve(gram_all)
+        y, coeffs = small_solve_fast(gram_sum(local_gram))
         y_full = jnp.concatenate([y, jnp.zeros((RHS, RHS), jnp.float32)], axis=0)
         both = jnp.dot(jnp.concatenate([y_full, coeffs], axis=1).T, stacked, precision=hp)
         solution = solution + both[:RHS].reshape(shape)

time: 350 us -> 353 us (level)
  Pallas kernels: 222 us -> 288 us
  other arithmetic: 68.9 us -> 8.46 us
  matrix products: 21 us -> 14.6 us
  local copies, waits for them, and re-layouts: 17.2 us -> 21.1 us
    pallas_call x0 -> x5, Pallas kernels: none -> 65.6 us  [small_solve_fast(): pl.pallas_call(solve_kernel, out_shape=jax.ShapeDtypeStruct((BASIS - RHS,...]
    another operation x25 -> x0, other arithmetic: 60.3 us -> none  [the longest x15 32.6 us: small_solve(): lower = jnp.linalg.cholesky(normal)]
    unnamed x8 -> x13, local copies, waits for them, and re-layouts: 2.15 us -> 6.36 us
    dot_general x20 -> x5, matrix products: 8.92 us -> 4.94 us  [small_solve_fast(): jnp.dot(shift_matrix, y, precision=lax.Precision.HIGHEST)]
where the time goes in v4:
time: 353 us; the launch traced here: 350 us
  Pallas kernels  288 us (82%)
  local copies, waits for them, and re-layouts  21.1 us (6%)
  matrix products  14.6 us (4%)
  starting transfers between devices  12.8 us (4%)
  other arithmetic  8.46 us (2%)
  waiting for transfers between devices  4 us (1%)
    pallas_call x5, Pallas kernels, gram_sum(): pl.pallas_call(lambda *refs: reduce_kernel(nx, ny, *refs), out_shape=jax....  127 us
    pallas_call x5, Pallas kernels, krylov_basis(): pl.pallas_call(lambda *refs: krylov_kernel(nx, ny, bx, *refs), out_shape=...  95.6 us
    pallas_call x5, Pallas kernels, small_solve_fast(): pl.pallas_call(solve_kernel, out_shape=jax.ShapeDtypeStruct((BASIS - RHS,...  65.6 us
    ppermute x2, starting transfers between devices, padded_2(): before = lax.ppermute(last, axis, up)  9.62 us
    another operation x5, local copies, waits for them, and re-layouts, shards(): stacked = krylov_basis(residual, terms, diagonal).reshape(BASIS, -1)  7.57 us
  transfers between devices with their start and end apart: 4, of which 2 were waited for; matrix products, arithmetic and copies ran while one was open for 0% of the time, Pallas kernels for 0%

profile of v4, /device:TPU:1, one launch (start us, length us, event | category | flops | bytes accessed | tf_op | source)
XLA Modules:
  0.0 350.0 jit_solution(3767404437577478979)
XLA Ops:
  0.6 0.8 fusion.58
  1.5 1.3 collective-permute-start.1
  2.8 4.7 %collective-permute-start = (f32[4,1,128]{2,1,0:T(1,128)S(1)}, f32[4,1,128]{2,1,0:T(1,128)S(1)}, u32[]{:S(2)}, u32[]{:S(2)}) collective-permute-start(f32[4,1,128]{2,1,0:T(1,128)S(1)} %get-tuple-element.7), channel_id=1, source_target_pairs={{0,8},{8,16},{16,24},{24,32},{32,40},{40,48},{48,56},{56,64},{64,7... | collective-permute-start | bytes 6152 | tf_op jit(solution)/shard_map/ppermute | solution.py:21
  8.9 5.0 %collective-permute-start.2 = (f32[4,10,1]{2,1,0:T(8,128)S(1)}, f32[4,10,1]{2,1,0:T(8,128)S(1)}, u32[]{:S(2)}, u32[]{:S(2)}) collective-permute-start(f32[4,10,1]{2,1,0:T(8,128)S(1)} %get-tuple-element.4), channel_id=1, source_target_pairs={{0,1},{1,2},{2,3},{3,4},{4,5},{5,6},{6,7},{8,9},{9,10},{10,11},{11... | collective-permute-start | bytes 488 | tf_op jit(solution)/shard_map/ppermute | solution.py:21
  13.9 1.9 collective-permute-start.3
  15.9 3.3 collective-permute-done.3
  19.1 0.8 select_maximum_fusion
  20.0 0.8 bitcast_dynamic-update-slice_fusion.5
  21.6 1.0 add_add_fusion
  22.6 1.7 broadcast_divide_fusion
  24.3 0.8 bitcast_dynamic-update-slice_fusion.3
  25.1 0.8 bitcast_dynamic-update-slice_fusion.2
  25.9 0.9 bitcast_dynamic-update-slice_fusion.1
  27.5 22.5 %krylov_basis.5 = f32[5,512,128]{2,1,0:T(8,128)} custom-call(f32[512,128]{1,0:T(8,128)} %bitcast.42, f32[6,32,128]{2,1,0:T(8,128)} %copy-done, f32[32,128]{1,0:T(8,128)} %bitcast.43), custom_call_target="tpu_custom_call" | custom-call | tf_op jit(solution)/shard_map/krylov_basis/pallas_call | solution.py:268
  50.0 1.5 reshape_reshape.27
  51.5 1.2 fusion.59
  53.3 26.5 %gram_allreduce.5.g_ref = f32[128,128]{1,0:T(8,128)} custom-call(f32[128,128]{1,0:T(8,128)} %pad.26.refs_0_), custom_call_target="tpu_custom_call" | custom-call | tf_op jit(solution)/shard_map/gram_allreduce/pallas_call | solution.py:102
  79.8 13.1 %small_solve.5 = f32[64,16]{1,0:T(8,128)} custom-call(f32[128,128]{1,0:T(8,128)} %gram_allreduce.5.g_ref), custom_call_target="tpu_custom_call" | custom-call | tf_op jit(solution)/shard_map/small_solve/pallas_call | solution.py:158
  93.0 0.8 copy.10
  93.8 1.0 convolution_subtract_fusion.4
  96.3 18.3 %krylov_basis.6 = f32[5,512,128]{2,1,0:T(8,128)} custom-call(f32[512,128]{1,0:T(8,128)} %reshape_reshape.28.refs_0_, f32[6,32,128]{2,1,0:T(8,128)} %copy-done, f32[32,128]{1,0:T(8,128)} %bitcast.44), custom_call_target="tpu_custom_call" | custom-call | tf_op jit(solution)/shard_map/krylov_basis/pallas_call | solution.py:268
  114.6 1.5 reshape_reshape.29
  116.2 1.2 fusion.60
  118.0 25.0 %gram_allreduce.6.g_ref = f32[128,128]{1,0:T(8,128)} custom-call(f32[128,128]{1,0:T(8,128)} %pad.27.refs_0_), custom_call_target="tpu_custom_call" | custom-call | tf_op jit(solution)/shard_map/gram_allreduce/pallas_call | solution.py:102
  143.0 13.1 %small_solve.6 = f32[64,16]{1,0:T(8,128)} custom-call(f32[128,128]{1,0:T(8,128)} %gram_allreduce.6.g_ref), custom_call_target="tpu_custom_call" | custom-call | tf_op jit(solution)/shard_map/small_solve/pallas_call | solution.py:158
  156.2 1.0 convolution_subtract_fusion.3
  157.1 0.8 copy.11
  159.5 18.3 %krylov_basis.7 = f32[5,512,128]{2,1,0:T(8,128)} custom-call(f32[512,128]{1,0:T(8,128)} %reshape_reshape.30.refs_0_, f32[6,32,128]{2,1,0:T(8,128)} %copy-done, f32[32,128]{1,0:T(8,128)} %bitcast.45), custom_call_target="tpu_custom_call" | custom-call | tf_op jit(solution)/shard_map/krylov_basis/pallas_call | solution.py:268
  177.8 1.5 reshape_reshape.31
  179.3 1.2 fusion.61
  181.2 25.1 %gram_allreduce.7.g_ref = f32[128,128]{1,0:T(8,128)} custom-call(f32[128,128]{1,0:T(8,128)} %pad.28.refs_0_), custom_call_target="tpu_custom_call" | custom-call | tf_op jit(solution)/shard_map/gram_allreduce/pallas_call | solution.py:102
  206.2 13.1 %small_solve.7 = f32[64,16]{1,0:T(8,128)} custom-call(f32[128,128]{1,0:T(8,128)} %gram_allreduce.7.g_ref), custom_call_target="tpu_custom_call" | custom-call | tf_op jit(solution)/shard_map/small_solve/pallas_call | solution.py:158
  219.4 1.0 convolution_subtract_fusion.2
  220.4 0.8 copy.12
  222.7 18.3 %krylov_basis.8 = f32[5,512,128]{2,1,0:T(8,128)} custom-call(f32[512,128]{1,0:T(8,128)} %reshape_reshape.32.refs_0_, f32[6,32,128]{2,1,0:T(8,128)} %copy-done, f32[32,128]{1,0:T(8,128)} %bitcast.46), custom_call_target="tpu_custom_call" | custom-call | tf_op jit(solution)/shard_map/krylov_basis/pallas_call | solution.py:268
  241.0 1.5 reshape_reshape.33
  242.5 1.2 fusion.62
  244.4 25.1 %gram_allreduce.8.g_ref = f32[128,128]{1,0:T(8,128)} custom-call(f32[128,128]{1,0:T(8,128)} %pad.29.refs_0_), custom_call_target="tpu_custom_call" | custom-call | tf_op jit(solution)/shard_map/gram_allreduce/pallas_call | solution.py:102
  269.5 13.1 %small_solve.8 = f32[64,16]{1,0:T(8,128)} custom-call(f32[128,128]{1,0:T(8,128)} %gram_allreduce.8.g_ref), custom_call_target="tpu_custom_call" | custom-call | tf_op jit(solution)/shard_map/small_solve/pallas_call | solution.py:158
  282.6 1.0 convolution_subtract_fusion.1
  283.6 0.8 copy.13
  286.0 18.2 %krylov_basis.9 = f32[5,512,128]{2,1,0:T(8,128)} custom-call(f32[512,128]{1,0:T(8,128)} %reshape_reshape.34.refs_0_, f32[6,32,128]{2,1,0:T(8,128)} %copy-done, f32[32,128]{1,0:T(8,128)} %bitcast.47), custom_call_target="tpu_custom_call" | custom-call | tf_op jit(solution)/shard_map/krylov_basis/pallas_call | solution.py:268
  304.2 1.5 reshape_reshape.35
  305.8 1.2 fusion.63
  307.6 25.1 %gram_allreduce.9.g_ref = f32[128,128]{1,0:T(8,128)} custom-call(f32[128,128]{1,0:T(8,128)} %pad.30.refs_0_), custom_call_target="tpu_custom_call" | custom-call | tf_op jit(solution)/shard_map/gram_allreduce/pallas_call | solution.py:102
  332.7 13.1 %small_solve.9 = f32[64,16]{1,0:T(8,128)} custom-call(f32[128,128]{1,0:T(8,128)} %gram_allreduce.9.g_ref), custom_call_target="tpu_custom_call" | custom-call | tf_op jit(solution)/shard_map/small_solve/pallas_call | solution.py:158
  345.8 1.0 convolution_subtract_fusion
  346.8 0.8 copy.14
  (35 shorter events, 14.7 us)
Async XLA Ops:
  0.6 26.1 %copy-start.1 = (f32[4,8,128]{2,1,0:T(8,128)S(1)}, f32[4,8,128]{2,1,0:T(8,128)}, u32[]{:S(2)}) copy-start(f32[4,8,128]{2,1,0:T(8,128)} %param.4) | copy-start | bytes 49156
  1.5 6.0 %collective-permute-start.1 = (f32[4,1,128]{2,1,0:T(1,128)S(1)}, f32[4,1,128]{2,1,0:T(1,128)S(1)}, u32[]{:S(2)}, u32[]{:S(2)}) collective-permute-start(f32[4,1,128]{2,1,0:T(1,128)S(1)} %get-tuple-element.6), channel_id=1, source_target_pairs={{8,0},{16,8},{24,16},{32,24},{40,32},{48,40},{56,48},{64,56},{72,6... | collective-permute-start | bytes 6152 | tf_op jit(solution)/shard_map/ppermute | solution.py:22
  2.8 5.4 %collective-permute-start = (f32[4,1,128]{2,1,0:T(1,128)S(1)}, f32[4,1,128]{2,1,0:T(1,128)S(1)}, u32[]{:S(2)}, u32[]{:S(2)}) collective-permute-start(f32[4,1,128]{2,1,0:T(1,128)S(1)} %get-tuple-element.7), channel_id=1, source_target_pairs={{0,8},{8,16},{16,24},{24,32},{32,40},{40,48},{48,56},{56,64},{64,7... | collective-permute-start | bytes 6152 | tf_op jit(solution)/shard_map/ppermute | solution.py:21
  8.9 6.9 %collective-permute-start.2 = (f32[4,10,1]{2,1,0:T(8,128)S(1)}, f32[4,10,1]{2,1,0:T(8,128)S(1)}, u32[]{:S(2)}, u32[]{:S(2)}) collective-permute-start(f32[4,10,1]{2,1,0:T(8,128)S(1)} %get-tuple-element.4), channel_id=1, source_target_pairs={{0,1},{1,2},{2,3},{3,4},{4,5},{5,6},{6,7},{8,9},{9,10},{10,11},{11... | collective-permute-start | bytes 488 | tf_op jit(solution)/shard_map/ppermute | solution.py:21
  13.9 5.2 %collective-permute-start.3 = (f32[4,10,1]{2,1,0:T(8,128)S(1)}, f32[4,10,1]{2,1,0:T(8,128)S(1)}, u32[]{:S(2)}, u32[]{:S(2)}) collective-permute-start(f32[4,10,1]{2,1,0:T(8,128)S(1)} %get-tuple-element.5), channel_id=1, source_target_pairs={{1,0},{2,1},{3,2},{4,3},{5,4},{6,5},{7,6},{9,8},{10,9},{11,10},{12... | collective-permute-start | bytes 488 | tf_op jit(solution)/shard_map/ppermute | solution.py:22
  22.6 4.3 %copy-start.2 = (f32[4,8,128]{2,1,0:T(8,128)}, f32[4,8,128]{2,1,0:T(8,128)S(1)}, u32[]{:S(2)}) copy-start(f32[4,8,128]{2,1,0:T(8,128)S(1)} %add_add_fusion) | copy-start | bytes 49156
  26.8 0.6 copy-start

commit v5 on v3

--- a/solution.py
+++ b/solution.py
@@ -87,8 +87,60 @@
             pl.semaphore_signal(barrier, inc=1, device_id={"gx": gx, "gy": j},
                                 device_id_type=pl.DeviceIdType.MESH)
     pl.semaphore_wait(barrier, nx + ny - 2)
-    exchange_reduce("gy", "gx", ny, x_ref, mine_y, rs_y, ag_y, gy_full, y_send, y_rs, y_ag)
-    exchange_reduce("gx", "gy", nx, gy_full, mine_x, rs_x, ag_x, o_ref, x_send, x_rs, x_ag)
+    part = x_ref.shape[0] // ny
+
+    def to_y(j, src, dst, slot, sem):
+        return pltpu.make_async_remote_copy(
+            src_ref=src, dst_ref=dst.at[slot], send_sem=y_send.at[j], recv_sem=sem.at[slot],
+            device_id={"gx": gx, "gy": j}, device_id_type=pl.DeviceIdType.MESH,
+        )
+
+    def to_x(j, slot):
+        return pltpu.make_async_remote_copy(
+            src_ref=mine_y, dst_ref=rs_x.at[slot], send_sem=x_send.at[j], recv_sem=x_rs.at[slot],
+            device_id={"gx": j, "gy": gy}, device_id_type=pl.DeviceIdType.MESH,
+        )
+
+    for j in range(ny):
+        @pl.when(j != gy)
+        def _():
+            to_y(j, x_ref.at[pl.ds(j * part, part)], rs_y, gy, y_rs).start()
+    rs_y[gy] = x_ref[pl.ds(pl.multiple_of(gy * part, part), part)]
+    for j in range(ny):
+        @pl.when(j != gy)
+        def _():
+            to_y(j, x_ref.at[pl.ds(j * part, part)], rs_y, gy, y_rs).wait_send()
+            to_y(j, x_ref.at[pl.ds(j * part, part)], rs_y, j, y_rs).wait_recv()
+    acc = rs_y[0]
+    for j in range(1, ny):
+        acc = acc + rs_y[j]
+    mine_y[...] = acc
+    for j in range(nx):
+        @pl.when(j != gx)
+        def _():
+            to_x(j, gx).start()
+    rs_x[gx] = acc
+    for j in range(nx):
+        @pl.when(j != gx)
+        def _():
+            to_x(j, gx).wait_send()
+            to_x(j, j).wait_recv()
+    acc = rs_x[0]
+    for j in range(1, nx):
+        acc = acc + rs_x[j]
+    mine_x[...] = acc
+    for j in range(ny):
+        @pl.when(j != gy)
+        def _():
+            to_y(j, mine_x, ag_y, gy, y_ag).start()
+    ag_y[gy] = acc
+    for j in range(ny):
+        @pl.when(j != gy)
+        def _():
+            to_y(j, mine_x, ag_y, gy, y_ag).wait_send()
+            to_y(j, mine_x, ag_y, j, y_ag).wait_recv()
+    for j in range(ny):
+        o_ref[pl.ds(j * part, part)] = ag_y[j]
 
 
 def gram_sum(local_gram):
@@ -109,9 +161,9 @@
             pltpu.VMEM((py, pad), f32),
             pltpu.VMEM((ny, py, pad), f32),
             pltpu.VMEM((ny, py, pad), f32),
-            pltpu.VMEM((px, pad), f32),
-            pltpu.VMEM((nx, px, pad), f32),
-            pltpu.VMEM((nx, px, pad), f32),
+            pltpu.VMEM((py, pad), f32),
+            pltpu.VMEM((nx, py, pad), f32),
+            pltpu.VMEM((nx, py, pad), f32),
             pltpu.SemaphoreType.DMA((ny,)),
             pltpu.SemaphoreType.DMA((ny,)),
             pltpu.SemaphoreType.DMA((ny,)),

time: 350 us -> 329 us (0.940)
  Pallas kernels: 222 us -> 202 us
    pallas_call x5, Pallas kernels: 127 us -> 112 us  [gram_sum(): pl.pallas_call(lambda *refs: reduce_kernel(nx, ny, *refs), out_shape=jax....]
    pallas_call x5, Pallas kernels: 95.5 us -> 89.7 us  [krylov_basis(): pl.pallas_call(lambda *refs: krylov_kernel(nx, ny, bx, *refs), out_shape=...]
where the time goes in v5:
time: 329 us; the launch traced here: 327 us
  Pallas kernels  202 us (61%)
  other arithmetic  68.9 us (21%)
  matrix products  21 us (6%)
  local copies, waits for them, and re-layouts  17.2 us (5%)
  starting transfers between devices  12.8 us (4%)
  waiting for transfers between devices  4 us (1%)
    pallas_call x5, Pallas kernels, gram_sum(): pl.pallas_call(lambda *refs: reduce_kernel(nx, ny, *refs), out_shape=jax....  112 us
    pallas_call x5, Pallas kernels, krylov_basis(): pl.pallas_call(lambda *refs: krylov_kernel(nx, ny, bx, *refs), out_shape=...  89.7 us
    another operation x15, other arithmetic, small_solve(): lower = jnp.linalg.cholesky(normal)  32.6 us
    another operation x10, other arithmetic, small_solve(): y = jax.scipy.linalg.cho_solve((lower, True), right_side)  27.7 us
    ppermute x2, starting transfers between devices, padded_2(): before = lax.ppermute(last, axis, up)  9.62 us
    another operation x5, local copies, waits for them, and re-layouts, shards(): stacked = krylov_basis(residual, terms, diagonal).reshape(BASIS, -1)  7.57 us
  transfers between devices with their start and end apart: 4, of which 2 were waited for; matrix products, arithmetic and copies ran while one was open for 0% of the time, Pallas kernels for 0%

profile of v5, /device:TPU:1, one launch (start us, length us, event | category | flops | bytes accessed | tf_op | source)
XLA Modules:
  0.0 327.3 jit_solution(11804090222352714837)
XLA Ops:
  0.6 0.8 fusion.118
  1.5 1.3 collective-permute-start.1
  2.8 4.7 %collective-permute-start = (f32[4,1,128]{2,1,0:T(1,128)S(1)}, f32[4,1,128]{2,1,0:T(1,128)S(1)}, u32[]{:S(2)}, u32[]{:S(2)}) collective-permute-start(f32[4,1,128]{2,1,0:T(1,128)S(1)} %get-tuple-element.9), channel_id=1, source_target_pairs={{0,8},{8,16},{16,24},{24,32},{32,40},{40,48},{48,56},{56,64},{64,7... | collective-permute-start | bytes 6152 | tf_op jit(solution)/shard_map/ppermute | solution.py:21
  8.9 5.0 %collective-permute-start.2 = (f32[4,10,1]{2,1,0:T(8,128)S(1)}, f32[4,10,1]{2,1,0:T(8,128)S(1)}, u32[]{:S(2)}, u32[]{:S(2)}) collective-permute-start(f32[4,10,1]{2,1,0:T(8,128)S(1)} %get-tuple-element.6), channel_id=1, source_target_pairs={{0,1},{1,2},{2,3},{3,4},{4,5},{5,6},{6,7},{8,9},{9,10},{10,11},{11... | collective-permute-start | bytes 488 | tf_op jit(solution)/shard_map/ppermute | solution.py:21
  13.9 1.9 collective-permute-start.3
  15.9 3.3 %collective-permute-done.3 = f32[4,10,1]{2,1,0:T(8,128)S(1)} collective-permute-done((f32[4,10,1]{2,1,0:T(8,128)S(1)}, f32[4,10,1]{2,1,0:T(8,128)S(1)}, u32[]{:S(2)}, u32[]{:S(2)}) %collective-permute-start.3) | collective-permute-done | bytes 192 | tf_op jit(solution)/shard_map/ppermute | solution.py:22
  19.1 0.8 select_maximum_fusion
  20.0 0.8 bitcast_dynamic-update-slice_fusion.5
  21.6 1.0 add_add_fusion
  22.6 1.7 broadcast_divide_fusion
  24.3 0.8 bitcast_dynamic-update-slice_fusion.3
  25.1 0.8 bitcast_dynamic-update-slice_fusion.2
  25.9 0.9 bitcast_dynamic-update-slice_fusion.1
  27.5 22.5 %krylov_basis.5 = f32[5,512,128]{2,1,0:T(8,128)} custom-call(f32[512,128]{1,0:T(8,128)} %bitcast.117, f32[6,32,128]{2,1,0:T(8,128)} %copy-done, f32[32,128]{1,0:T(8,128)} %bitcast.118), custom_call_target="tpu_custom_call" | custom-call | tf_op jit(solution)/shard_map/krylov_basis/pallas_call | solution.py:275
  49.9 1.5 reshape_reshape.27
  51.5 1.2 fusion.119
  53.3 22.8 %gram_allreduce.5 = f32[128,128]{1,0:T(8,128)} custom-call(f32[128,128]{1,0:T(8,128)} %pad.26.refs_0_), custom_call_target="tpu_custom_call" | custom-call | tf_op jit(solution)/shard_map/gram_allreduce/pallas_call | solution.py:154
  76.0 1.1 fusion.10
  77.7 5.8 %cholesky.89 = f32[64,64]{1,0:T(8,128)S(1)} custom-call(f32[64,64]{1,0:T(8,128)S(1)} %fusion.46), custom_call_target="Cholesky" | custom-call | tf_op jit(solution)/shard_map/jit(cholesky)/cholesky | solution.py:322
  84.9 4.9 %custom-call.11 = f32[1,64,64]{1,2,0:T(8,128)S(1)} custom-call(f32[1,64,64]{2,1,0:T(8,128)S(1)} %fusion.17), custom_call_target="InvertDiagBlocksLowerTriangular" | custom-call | tf_op jit(solution)/shard_map/jit(_cho_solve)/triangular_solve | solution.py:323
  92.1 16.8 %krylov_basis.6 = f32[5,512,128]{2,1,0:T(8,128)} custom-call(f32[512,128]{1,0:T(8,128)} %reshape_reshape.28.refs_0_, f32[6,32,128]{2,1,0:T(8,128)} %copy-done, f32[32,128]{1,0:T(8,128)} %bitcast.119), custom_call_target="tpu_custom_call" | custom-call | tf_op jit(solution)/shard_map/krylov_basis/pallas_call | solution.py:275
  108.9 1.5 reshape_reshape.29
  110.4 1.2 fusion.120
  112.2 22.4 %gram_allreduce.6 = f32[128,128]{1,0:T(8,128)} custom-call(f32[128,128]{1,0:T(8,128)} %pad.27.refs_0_), custom_call_target="tpu_custom_call" | custom-call | tf_op jit(solution)/shard_map/gram_allreduce/pallas_call | solution.py:154
  134.6 1.1 fusion.8
  136.2 5.8 %cholesky.100 = f32[64,64]{1,0:T(8,128)S(1)} custom-call(f32[64,64]{1,0:T(8,128)S(1)} %fusion.41), custom_call_target="Cholesky" | custom-call | tf_op jit(solution)/shard_map/jit(cholesky)/cholesky | solution.py:322
  143.4 4.9 %custom-call.12 = f32[1,64,64]{1,2,0:T(8,128)S(1)} custom-call(f32[1,64,64]{2,1,0:T(8,128)S(1)} %fusion.18), custom_call_target="InvertDiagBlocksLowerTriangular" | custom-call | tf_op jit(solution)/shard_map/jit(_cho_solve)/triangular_solve | solution.py:323
  150.6 16.8 %krylov_basis.7 = f32[5,512,128]{2,1,0:T(8,128)} custom-call(f32[512,128]{1,0:T(8,128)} %reshape_reshape.30.refs_0_, f32[6,32,128]{2,1,0:T(8,128)} %copy-done, f32[32,128]{1,0:T(8,128)} %bitcast.120), custom_call_target="tpu_custom_call" | custom-call | tf_op jit(solution)/shard_map/krylov_basis/pallas_call | solution.py:275
  167.4 1.5 reshape_reshape.31
  168.9 1.2 fusion.121
  170.8 22.4 %gram_allreduce.7 = f32[128,128]{1,0:T(8,128)} custom-call(f32[128,128]{1,0:T(8,128)} %pad.28.refs_0_), custom_call_target="tpu_custom_call" | custom-call | tf_op jit(solution)/shard_map/gram_allreduce/pallas_call | solution.py:154
  193.2 1.1 fusion.6
  194.9 5.8 %cholesky.111 = f32[64,64]{1,0:T(8,128)S(1)} custom-call(f32[64,64]{1,0:T(8,128)S(1)} %fusion.36), custom_call_target="Cholesky" | custom-call | tf_op jit(solution)/shard_map/jit(cholesky)/cholesky | solution.py:322
  202.0 4.9 %custom-call.13 = f32[1,64,64]{1,2,0:T(8,128)S(1)} custom-call(f32[1,64,64]{2,1,0:T(8,128)S(1)} %fusion.19), custom_call_target="InvertDiagBlocksLowerTriangular" | custom-call | tf_op jit(solution)/shard_map/jit(_cho_solve)/triangular_solve | solution.py:323
  209.2 16.9 %krylov_basis.8 = f32[5,512,128]{2,1,0:T(8,128)} custom-call(f32[512,128]{1,0:T(8,128)} %reshape_reshape.32.refs_0_, f32[6,32,128]{2,1,0:T(8,128)} %copy-done, f32[32,128]{1,0:T(8,128)} %bitcast.121), custom_call_target="tpu_custom_call" | custom-call | tf_op jit(solution)/shard_map/krylov_basis/pallas_call | solution.py:275
  226.1 1.5 reshape_reshape.33
  227.6 1.2 fusion.122
  229.4 22.4 %gram_allreduce.8 = f32[128,128]{1,0:T(8,128)} custom-call(f32[128,128]{1,0:T(8,128)} %pad.29.refs_0_), custom_call_target="tpu_custom_call" | custom-call | tf_op jit(solution)/shard_map/gram_allreduce/pallas_call | solution.py:154
  251.9 1.1 fusion.4
  253.5 5.8 %cholesky.122 = f32[64,64]{1,0:T(8,128)S(1)} custom-call(f32[64,64]{1,0:T(8,128)S(1)} %fusion.31), custom_call_target="Cholesky" | custom-call | tf_op jit(solution)/shard_map/jit(cholesky)/cholesky | solution.py:322
  260.7 4.9 %custom-call.14 = f32[1,64,64]{1,2,0:T(8,128)S(1)} custom-call(f32[1,64,64]{2,1,0:T(8,128)S(1)} %fusion.20), custom_call_target="InvertDiagBlocksLowerTriangular" | custom-call | tf_op jit(solution)/shard_map/jit(_cho_solve)/triangular_solve | solution.py:323
  267.9 16.8 %krylov_basis.9 = f32[5,512,128]{2,1,0:T(8,128)} custom-call(f32[512,128]{1,0:T(8,128)} %reshape_reshape.34.refs_0_, f32[6,32,128]{2,1,0:T(8,128)} %copy-done, f32[32,128]{1,0:T(8,128)} %bitcast.122), custom_call_target="tpu_custom_call" | custom-call | tf_op jit(solution)/shard_map/krylov_basis/pallas_call | solution.py:275
  284.7 1.5 reshape_reshape.35
  286.2 1.2 fusion.123
  288.0 22.5 %gram_allreduce.9 = f32[128,128]{1,0:T(8,128)} custom-call(f32[128,128]{1,0:T(8,128)} %pad.30.refs_0_), custom_call_target="tpu_custom_call" | custom-call | tf_op jit(solution)/shard_map/gram_allreduce/pallas_call | solution.py:154
  310.5 1.1 fusion.2
  312.1 5.8 %cholesky.133 = f32[64,64]{1,0:T(8,128)S(1)} custom-call(f32[64,64]{1,0:T(8,128)S(1)} %fusion.26), custom_call_target="Cholesky" | custom-call | tf_op jit(solution)/shard_map/jit(cholesky)/cholesky | solution.py:322
  319.3 4.9 %custom-call.15 = f32[1,64,64]{1,2,0:T(8,128)S(1)} custom-call(f32[1,64,64]{2,1,0:T(8,128)S(1)} %fusion.21), custom_call_target="InvertDiagBlocksLowerTriangular" | custom-call | tf_op jit(solution)/shard_map/jit(_cho_solve)/triangular_solve | solution.py:323
  (85 shorter events, 27.6 us)
Async XLA Ops:
  0.6 26.1 %copy-start.1 = (f32[4,8,128]{2,1,0:T(8,128)S(1)}, f32[4,8,128]{2,1,0:T(8,128)}, u32[]{:S(2)}) copy-start(f32[4,8,128]{2,1,0:T(8,128)} %param.7) | copy-start | bytes 49156
  1.5 6.0 %collective-permute-start.1 = (f32[4,1,128]{2,1,0:T(1,128)S(1)}, f32[4,1,128]{2,1,0:T(1,128)S(1)}, u32[]{:S(2)}, u32[]{:S(2)}) collective-permute-start(f32[4,1,128]{2,1,0:T(1,128)S(1)} %get-tuple-element.8), channel_id=1, source_target_pairs={{8,0},{16,8},{24,16},{32,24},{40,32},{48,40},{56,48},{64,56},{72,6... | collective-permute-start | bytes 6152 | tf_op jit(solution)/shard_map/ppermute | solution.py:22
  2.8 5.4 %collective-permute-start = (f32[4,1,128]{2,1,0:T(1,128)S(1)}, f32[4,1,128]{2,1,0:T(1,128)S(1)}, u32[]{:S(2)}, u32[]{:S(2)}) collective-permute-start(f32[4,1,128]{2,1,0:T(1,128)S(1)} %get-tuple-element.9), channel_id=1, source_target_pairs={{0,8},{8,16},{16,24},{24,32},{32,40},{40,48},{48,56},{56,64},{64,7... | collective-permute-start | bytes 6152 | tf_op jit(solution)/shard_map/ppermute | solution.py:21
  8.9 6.9 %collective-permute-start.2 = (f32[4,10,1]{2,1,0:T(8,128)S(1)}, f32[4,10,1]{2,1,0:T(8,128)S(1)}, u32[]{:S(2)}, u32[]{:S(2)}) collective-permute-start(f32[4,10,1]{2,1,0:T(8,128)S(1)} %get-tuple-element.6), channel_id=1, source_target_pairs={{0,1},{1,2},{2,3},{3,4},{4,5},{5,6},{6,7},{8,9},{9,10},{10,11},{11... | collective-permute-start | bytes 488 | tf_op jit(solution)/shard_map/ppermute | solution.py:21
  13.9 5.2 %collective-permute-start.3 = (f32[4,10,1]{2,1,0:T(8,128)S(1)}, f32[4,10,1]{2,1,0:T(8,128)S(1)}, u32[]{:S(2)}, u32[]{:S(2)}) collective-permute-start(f32[4,10,1]{2,1,0:T(8,128)S(1)} %get-tuple-element.7), channel_id=1, source_target_pairs={{1,0},{2,1},{3,2},{4,3},{5,4},{6,5},{7,6},{9,8},{10,9},{11,10},{12... | collective-permute-start | bytes 488 | tf_op jit(solution)/shard_map/ppermute | solution.py:22
  22.6 4.3 %copy-start.2 = (f32[4,8,128]{2,1,0:T(8,128)}, f32[4,8,128]{2,1,0:T(8,128)S(1)}, u32[]{:S(2)}) copy-start(f32[4,8,128]{2,1,0:T(8,128)S(1)} %add_add_fusion) | copy-start | bytes 49156
  26.8 0.6 copy-start

commit v6 on v5

--- a/solution.py
+++ b/solution.py
@@ -75,18 +75,6 @@
                   y_send, y_rs, y_ag, x_send, x_rs, x_ag):
     gx = lax.axis_index("gx")
     gy = lax.axis_index("gy")
-    barrier = pltpu.get_barrier_semaphore()
-    for j in range(nx):
-        @pl.when(j != gx)
-        def _():
-            pl.semaphore_signal(barrier, inc=1, device_id={"gx": j, "gy": gy},
-                                device_id_type=pl.DeviceIdType.MESH)
-    for j in range(ny):
-        @pl.when(j != gy)
-        def _():
-            pl.semaphore_signal(barrier, inc=1, device_id={"gx": gx, "gy": j},
-                                device_id_type=pl.DeviceIdType.MESH)
-    pl.semaphore_wait(barrier, nx + ny - 2)
     part = x_ref.shape[0] // ny
 
     def to_y(j, src, dst, slot, sem):
@@ -171,38 +159,27 @@
             pltpu.SemaphoreType.DMA((nx,)),
             pltpu.SemaphoreType.DMA((nx,)),
         ],
-        compiler_params=pltpu.CompilerParams(collective_id=4, has_side_effects=True),
+        compiler_params=pltpu.CompilerParams(has_side_effects=True),
         name="gram_allreduce",
     )(wide)
     return total[:size, :size]
 
 
 def krylov_kernel(nx, ny, bx, v0_ref, terms_ref, diag_ref, out_ref,
-                  halo_x, xsend, ysend, xr, yr, send_sem, recv_sem):
+                  halo_x, xsend, ysend, xr, yr, send_sem, recv_sem, ybuf):
     gx = lax.axis_index("gx")
     gy = lax.axis_index("gy")
     rhs = out_ref.shape[1] // terms_ref.shape[1]
     rows, lanes = terms_ref.shape[1], terms_ref.shape[2]
     cells = out_ref.shape[1]
     zero_x = jnp.zeros(xr.shape[2:], jnp.float32)
-    zero_y = jnp.zeros(yr.shape[2:], jnp.float32)
-    for k in range(xr.shape[0]):
-        for d in range(2):
-            xr[k, d] = zero_x
-            yr[k, d] = zero_y
+    zero_row = jnp.zeros((1, yr.shape[3]), jnp.float32)
     targets = (
         (gx < nx - 1, {"gx": gx + 1, "gy": gy}, gx > 0),
         (gx > 0, {"gx": gx - 1, "gy": gy}, gx < nx - 1),
         (gy < ny - 1, {"gx": gx, "gy": gy + 1}, gy > 0),
         (gy > 0, {"gx": gx, "gy": gy - 1}, gy < ny - 1),
     )
-    barrier = pltpu.get_barrier_semaphore()
-    for has_target, target, _ in targets:
-        @pl.when(has_target)
-        def _():
-            pl.semaphore_signal(barrier, inc=1, device_id=target, device_id_type=pl.DeviceIdType.MESH)
-    peers = (gx + nx - 1) // nx + (2 * nx - 2 - gx) // nx + (gy + ny - 1) // ny + (2 * ny - 2 - gy) // ny
-    pl.semaphore_wait(barrier, peers)
 
     row = lax.broadcasted_iota(jnp.int32, (rhs, rows, lanes), 1)
     lane = lax.broadcasted_iota(jnp.int32, (rhs, rows, lanes), 2)
@@ -247,10 +224,28 @@
             def _():
                 copy(d).wait_recv()
 
-        halo_x[pl.ds(0, cells // bx, stride=bx), :] = xr[k, 0]
-        halo_x[pl.ds(bx - 1, cells // bx, stride=bx), :] = xr[k, 1]
-        before = yr[k, 0][1:2]
-        after = yr[k, 1][0:1]
+        for side, start in ((0, 0), (1, bx - 1)):
+            has_x = targets[side][2]
+            has_y = targets[2 + side][2]
+
+            @pl.when(has_x)
+            def _():
+                halo_x[pl.ds(start, cells // bx, stride=bx), :] = xr[k, side]
+
+            @pl.when(jnp.logical_not(has_x))
+            def _():
+                halo_x[pl.ds(start, cells // bx, stride=bx), :] = zero_x
+
+            @pl.when(has_y)
+            def _():
+                ybuf[side:side + 1] = yr[k, side][1 - side:2 - side]
+
+            @pl.when(jnp.logical_not(has_y))
+            def _():
+                ybuf[side:side + 1] = zero_row
+
+        before = ybuf[0:1]
+        after = ybuf[1:2]
         ycols = jnp.where(trow == 0, before, jnp.where(trow == lanes - 1, after, 0.0)).T
         v = flat.reshape(rhs, rows, lanes)
         hx = halo_x[...].reshape(rhs, rows, lanes)
@@ -285,8 +280,9 @@
             pltpu.VMEM((S, 2, 8, cells), jnp.float32),
             pltpu.SemaphoreType.DMA((4,)),
             pltpu.SemaphoreType.DMA((S, 4)),
+            pltpu.VMEM((8, cells), jnp.float32),
         ],
-        compiler_params=pltpu.CompilerParams(collective_id=3, has_side_effects=True),
+        compiler_params=pltpu.CompilerParams(has_side_effects=True),
         name="krylov_basis",
     )(v0.reshape(cells, by), jnp.stack(terms).reshape(6, nz * bx, by), diagonal.reshape(nz * bx, by))
     return out.reshape(S + 1, rhs, nz, bx, by)

time: 329 us -> 388 us (1.18)
  Pallas kernels: 202 us -> 262 us
    pallas_call x5, Pallas kernels: 112 us -> 144 us  [gram_sum(): pl.pallas_call(lambda *refs: reduce_kernel(nx, ny, *refs), out_shape=jax....]
    pallas_call x5, Pallas kernels: 89.7 us -> 117 us  [krylov_basis(): pl.pallas_call(lambda *refs: krylov_kernel(nx, ny, bx, *refs), out_shape=...]
where the time goes in v6:
time: 388 us; the launch traced here: 387 us
  Pallas kernels  262 us (68%)
  other arithmetic  68.9 us (18%)
  matrix products  21 us (5%)
  local copies, waits for them, and re-layouts  17.2 us (4%)
  starting transfers between devices  12.8 us (3%)
  waiting for transfers between devices  4 us (1%)
    pallas_call x5, Pallas kernels, gram_sum(): pl.pallas_call(lambda *refs: reduce_kernel(nx, ny, *refs), out_shape=jax....  144 us
    pallas_call x5, Pallas kernels, krylov_basis(): pl.pallas_call(lambda *refs: krylov_kernel(nx, ny, bx, *refs), out_shape=...  117 us
    another operation x15, other arithmetic, small_solve(): lower = jnp.linalg.cholesky(normal)  32.6 us
    another operation x10, other arithmetic, small_solve(): y = jax.scipy.linalg.cho_solve((lower, True), right_side)  27.7 us
    ppermute x2, starting transfers between devices, padded_2(): before = lax.ppermute(last, axis, up)  9.62 us
  transfers between devices with their start and end apart: 4, of which 2 were waited for; matrix products, arithmetic and copies ran while one was open for 0% of the time, Pallas kernels for 0%

profile of v6, /device:TPU:1, one launch (start us, length us, event | category | flops | bytes accessed | tf_op | source)
XLA Modules:
  0.0 386.9 jit_solution(18111204738454387735)
XLA Ops:
  0.6 0.8 fusion.118
  1.5 1.3 collective-permute-start.1
  2.8 4.7 %collective-permute-start = (f32[4,1,128]{2,1,0:T(1,128)S(1)}, f32[4,1,128]{2,1,0:T(1,128)S(1)}, u32[]{:S(2)}, u32[]{:S(2)}) collective-permute-start(f32[4,1,128]{2,1,0:T(1,128)S(1)} %get-tuple-element.9), channel_id=1, source_target_pairs={{0,8},{8,16},{16,24},{24,32},{32,40},{40,48},{48,56},{56,64},{64,7... | collective-permute-start | bytes 6152 | tf_op jit(solution)/shard_map/ppermute | solution.py:21
  8.9 5.0 %collective-permute-start.2 = (f32[4,10,1]{2,1,0:T(8,128)S(1)}, f32[4,10,1]{2,1,0:T(8,128)S(1)}, u32[]{:S(2)}, u32[]{:S(2)}) collective-permute-start(f32[4,10,1]{2,1,0:T(8,128)S(1)} %get-tuple-element.6), channel_id=1, source_target_pairs={{0,1},{1,2},{2,3},{3,4},{4,5},{5,6},{6,7},{8,9},{9,10},{10,11},{11... | collective-permute-start | bytes 488 | tf_op jit(solution)/shard_map/ppermute | solution.py:21
  13.9 1.9 collective-permute-start.3
  15.9 3.3 collective-permute-done.3
  19.1 0.8 select_maximum_fusion
  20.0 0.8 bitcast_dynamic-update-slice_fusion.5
  21.6 1.0 add_add_fusion
  22.6 1.7 broadcast_divide_fusion
  24.3 0.8 bitcast_dynamic-update-slice_fusion.3
  25.1 0.8 bitcast_dynamic-update-slice_fusion.2
  25.9 0.9 bitcast_dynamic-update-slice_fusion.1
  27.5 28.8 %krylov_basis.5 = f32[5,512,128]{2,1,0:T(8,128)} custom-call(f32[512,128]{1,0:T(8,128)} %bitcast.117, f32[6,32,128]{2,1,0:T(8,128)} %copy-done, f32[32,128]{1,0:T(8,128)} %bitcast.118), custom_call_target="tpu_custom_call" | custom-call | tf_op jit(solution)/shard_map/krylov_basis/pallas_call | solution.py:270
  56.3 1.5 reshape_reshape.27
  57.8 1.2 fusion.119
  59.7 28.9 %gram_allreduce.5 = f32[128,128]{1,0:T(8,128)} custom-call(f32[128,128]{1,0:T(8,128)} %pad.26.refs_0_), custom_call_target="tpu_custom_call" | custom-call | tf_op jit(solution)/shard_map/gram_allreduce/pallas_call | solution.py:142
  88.6 1.1 fusion.10
  90.2 5.8 %cholesky.89 = f32[64,64]{1,0:T(8,128)S(1)} custom-call(f32[64,64]{1,0:T(8,128)S(1)} %fusion.46), custom_call_target="Cholesky" | custom-call | tf_op jit(solution)/shard_map/jit(cholesky)/cholesky | solution.py:318
  97.4 4.9 %custom-call.11 = f32[1,64,64]{1,2,0:T(8,128)S(1)} custom-call(f32[1,64,64]{2,1,0:T(8,128)S(1)} %fusion.17), custom_call_target="InvertDiagBlocksLowerTriangular" | custom-call | tf_op jit(solution)/shard_map/jit(_cho_solve)/triangular_solve | solution.py:319
  104.6 22.1 %krylov_basis.6 = f32[5,512,128]{2,1,0:T(8,128)} custom-call(f32[512,128]{1,0:T(8,128)} %reshape_reshape.28.refs_0_, f32[6,32,128]{2,1,0:T(8,128)} %copy-done, f32[32,128]{1,0:T(8,128)} %bitcast.119), custom_call_target="tpu_custom_call" | custom-call | tf_op jit(solution)/shard_map/krylov_basis/pallas_call | solution.py:270
  126.6 1.5 reshape_reshape.29
  128.2 1.2 fusion.120
  130.0 28.9 %gram_allreduce.6 = f32[128,128]{1,0:T(8,128)} custom-call(f32[128,128]{1,0:T(8,128)} %pad.27.refs_0_), custom_call_target="tpu_custom_call" | custom-call | tf_op jit(solution)/shard_map/gram_allreduce/pallas_call | solution.py:142
  158.9 1.1 fusion.8
  160.5 5.8 %cholesky.100 = f32[64,64]{1,0:T(8,128)S(1)} custom-call(f32[64,64]{1,0:T(8,128)S(1)} %fusion.41), custom_call_target="Cholesky" | custom-call | tf_op jit(solution)/shard_map/jit(cholesky)/cholesky | solution.py:318
  167.7 4.9 %custom-call.12 = f32[1,64,64]{1,2,0:T(8,128)S(1)} custom-call(f32[1,64,64]{2,1,0:T(8,128)S(1)} %fusion.18), custom_call_target="InvertDiagBlocksLowerTriangular" | custom-call | tf_op jit(solution)/shard_map/jit(_cho_solve)/triangular_solve | solution.py:319
  174.9 22.1 %krylov_basis.7 = f32[5,512,128]{2,1,0:T(8,128)} custom-call(f32[512,128]{1,0:T(8,128)} %reshape_reshape.30.refs_0_, f32[6,32,128]{2,1,0:T(8,128)} %copy-done, f32[32,128]{1,0:T(8,128)} %bitcast.120), custom_call_target="tpu_custom_call" | custom-call | tf_op jit(solution)/shard_map/krylov_basis/pallas_call | solution.py:270
  197.0 1.5 reshape_reshape.31
  198.5 1.2 fusion.121
  200.3 28.9 %gram_allreduce.7 = f32[128,128]{1,0:T(8,128)} custom-call(f32[128,128]{1,0:T(8,128)} %pad.28.refs_0_), custom_call_target="tpu_custom_call" | custom-call | tf_op jit(solution)/shard_map/gram_allreduce/pallas_call | solution.py:142
  229.2 1.1 fusion.6
  230.8 5.8 %cholesky.111 = f32[64,64]{1,0:T(8,128)S(1)} custom-call(f32[64,64]{1,0:T(8,128)S(1)} %fusion.36), custom_call_target="Cholesky" | custom-call | tf_op jit(solution)/shard_map/jit(cholesky)/cholesky | solution.py:318
  238.0 4.9 %custom-call.13 = f32[1,64,64]{1,2,0:T(8,128)S(1)} custom-call(f32[1,64,64]{2,1,0:T(8,128)S(1)} %fusion.19), custom_call_target="InvertDiagBlocksLowerTriangular" | custom-call | tf_op jit(solution)/shard_map/jit(_cho_solve)/triangular_solve | solution.py:319
  245.2 22.3 %krylov_basis.8 = f32[5,512,128]{2,1,0:T(8,128)} custom-call(f32[512,128]{1,0:T(8,128)} %reshape_reshape.32.refs_0_, f32[6,32,128]{2,1,0:T(8,128)} %copy-done, f32[32,128]{1,0:T(8,128)} %bitcast.121), custom_call_target="tpu_custom_call" | custom-call | tf_op jit(solution)/shard_map/krylov_basis/pallas_call | solution.py:270
  267.5 1.5 reshape_reshape.33
  269.0 1.2 fusion.122
  270.8 28.9 %gram_allreduce.8 = f32[128,128]{1,0:T(8,128)} custom-call(f32[128,128]{1,0:T(8,128)} %pad.29.refs_0_), custom_call_target="tpu_custom_call" | custom-call | tf_op jit(solution)/shard_map/gram_allreduce/pallas_call | solution.py:142
  299.7 1.1 fusion.4
  301.4 5.8 %cholesky.122 = f32[64,64]{1,0:T(8,128)S(1)} custom-call(f32[64,64]{1,0:T(8,128)S(1)} %fusion.31), custom_call_target="Cholesky" | custom-call | tf_op jit(solution)/shard_map/jit(cholesky)/cholesky | solution.py:318
  308.6 4.9 %custom-call.14 = f32[1,64,64]{1,2,0:T(8,128)S(1)} custom-call(f32[1,64,64]{2,1,0:T(8,128)S(1)} %fusion.20), custom_call_target="InvertDiagBlocksLowerTriangular" | custom-call | tf_op jit(solution)/shard_map/jit(_cho_solve)/triangular_solve | solution.py:319
  315.8 22.1 %krylov_basis.9 = f32[5,512,128]{2,1,0:T(8,128)} custom-call(f32[512,128]{1,0:T(8,128)} %reshape_reshape.34.refs_0_, f32[6,32,128]{2,1,0:T(8,128)} %copy-done, f32[32,128]{1,0:T(8,128)} %bitcast.122), custom_call_target="tpu_custom_call" | custom-call | tf_op jit(solution)/shard_map/krylov_basis/pallas_call | solution.py:270
  337.8 1.5 reshape_reshape.35
  339.3 1.2 fusion.123
  341.2 28.9 %gram_allreduce.9 = f32[128,128]{1,0:T(8,128)} custom-call(f32[128,128]{1,0:T(8,128)} %pad.30.refs_0_), custom_call_target="tpu_custom_call" | custom-call | tf_op jit(solution)/shard_map/gram_allreduce/pallas_call | solution.py:142
  370.1 1.1 fusion.2
  371.7 5.8 %cholesky.133 = f32[64,64]{1,0:T(8,128)S(1)} custom-call(f32[64,64]{1,0:T(8,128)S(1)} %fusion.26), custom_call_target="Cholesky" | custom-call | tf_op jit(solution)/shard_map/jit(cholesky)/cholesky | solution.py:318
  378.9 4.9 %custom-call.15 = f32[1,64,64]{1,2,0:T(8,128)S(1)} custom-call(f32[1,64,64]{2,1,0:T(8,128)S(1)} %fusion.21), custom_call_target="InvertDiagBlocksLowerTriangular" | custom-call | tf_op jit(solution)/shard_map/jit(_cho_solve)/triangular_solve | solution.py:319
  (85 shorter events, 27.6 us)
Async XLA Ops:
  0.6 26.1 %copy-start.1 = (f32[4,8,128]{2,1,0:T(8,128)S(1)}, f32[4,8,128]{2,1,0:T(8,128)}, u32[]{:S(2)}) copy-start(f32[4,8,128]{2,1,0:T(8,128)} %param.7) | copy-start | bytes 49156
  1.5 6.0 %collective-permute-start.1 = (f32[4,1,128]{2,1,0:T(1,128)S(1)}, f32[4,1,128]{2,1,0:T(1,128)S(1)}, u32[]{:S(2)}, u32[]{:S(2)}) collective-permute-start(f32[4,1,128]{2,1,0:T(1,128)S(1)} %get-tuple-element.8), channel_id=1, source_target_pairs={{8,0},{16,8},{24,16},{32,24},{40,32},{48,40},{56,48},{64,56},{72,6... | collective-permute-start | bytes 6152 | tf_op jit(solution)/shard_map/ppermute | solution.py:22
  2.8 5.4 %collective-permute-start = (f32[4,1,128]{2,1,0:T(1,128)S(1)}, f32[4,1,128]{2,1,0:T(1,128)S(1)}, u32[]{:S(2)}, u32[]{:S(2)}) collective-permute-start(f32[4,1,128]{2,1,0:T(1,128)S(1)} %get-tuple-element.9), channel_id=1, source_target_pairs={{0,8},{8,16},{16,24},{24,32},{32,40},{40,48},{48,56},{56,64},{64,7... | collective-permute-start | bytes 6152 | tf_op jit(solution)/shard_map/ppermute | solution.py:21
  8.9 6.9 %collective-permute-start.2 = (f32[4,10,1]{2,1,0:T(8,128)S(1)}, f32[4,10,1]{2,1,0:T(8,128)S(1)}, u32[]{:S(2)}, u32[]{:S(2)}) collective-permute-start(f32[4,10,1]{2,1,0:T(8,128)S(1)} %get-tuple-element.6), channel_id=1, source_target_pairs={{0,1},{1,2},{2,3},{3,4},{4,5},{5,6},{6,7},{8,9},{9,10},{10,11},{11... | collective-permute-start | bytes 488 | tf_op jit(solution)/shard_map/ppermute | solution.py:21
  13.9 5.2 %collective-permute-start.3 = (f32[4,10,1]{2,1,0:T(8,128)S(1)}, f32[4,10,1]{2,1,0:T(8,128)S(1)}, u32[]{:S(2)}, u32[]{:S(2)}) collective-permute-start(f32[4,10,1]{2,1,0:T(8,128)S(1)} %get-tuple-element.7), channel_id=1, source_target_pairs={{1,0},{2,1},{3,2},{4,3},{5,4},{6,5},{7,6},{9,8},{10,9},{11,10},{12... | collective-permute-start | bytes 488 | tf_op jit(solution)/shard_map/ppermute | solution.py:22
  22.6 4.3 %copy-start.2 = (f32[4,8,128]{2,1,0:T(8,128)}, f32[4,8,128]{2,1,0:T(8,128)S(1)}, u32[]{:S(2)}) copy-start(f32[4,8,128]{2,1,0:T(8,128)S(1)} %add_add_fusion) | copy-start | bytes 49156
  26.8 0.6 copy-start

commit v7 on v5

--- a/solution.py
+++ b/solution.py
@@ -319,8 +319,9 @@
     gram_shift = jnp.dot(gram_all, shift_matrix, precision=hp)
     normal = jnp.dot(shift_matrix.T, gram_shift, precision=hp)
     right_side = jnp.dot(gram_shift.T, first_block, precision=hp)
-    lower = jnp.linalg.cholesky(normal)
-    y = jax.scipy.linalg.cho_solve((lower, True), right_side)
+    lower = lax.linalg.cholesky(normal, symmetrize_input=False)
+    forward = lax.linalg.triangular_solve(lower, right_side, left_side=True, lower=True)
+    y = lax.linalg.triangular_solve(lower, forward, left_side=True, lower=True, transpose_a=True)
     coeffs = first_block - jnp.dot(shift_matrix, y, precision=hp)
     return (y, coeffs)
 

time: 329 us -> 328 us (level)
  no operation moved by 1% of the time
where the time goes in v7:
time: 328 us; the launch traced here: 327 us
  Pallas kernels  202 us (62%)
  other arithmetic  68.8 us (21%)
  matrix products  21 us (6%)
  local copies, waits for them, and re-layouts  16.9 us (5%)
  starting transfers between devices  12.8 us (4%)
  waiting for transfers between devices  4 us (1%)
    pallas_call x5, Pallas kernels, gram_sum(): pl.pallas_call(lambda *refs: reduce_kernel(nx, ny, *refs), out_shape=jax....  112 us
    pallas_call x5, Pallas kernels, krylov_basis(): pl.pallas_call(lambda *refs: krylov_kernel(nx, ny, bx, *refs), out_shape=...  89.7 us
    another operation x15, other arithmetic, small_solve(): lower = lax.linalg.cholesky(normal, symmetrize_input=False)  32.6 us
    another operation x10, other arithmetic, small_solve(): lax.linalg.triangular_solve(lower, forward, left_side=True, lower=True, t...  27.7 us
    ppermute x2, starting transfers between devices, padded_2(): before = lax.ppermute(last, axis, up)  9.62 us
    another operation x5, local copies, waits for them, and re-layouts, shards(): stacked = krylov_basis(residual, terms, diagonal).reshape(BASIS, -1)  7.57 us
  transfers between devices with their start and end apart: 4, of which 2 were waited for; matrix products, arithmetic and copies ran while one was open for 0% of the time, Pallas kernels for 0%

profile of v7, /device:TPU:1, one launch (start us, length us, event | category | flops | bytes accessed | tf_op | source)
XLA Modules:
  0.0 326.9 jit_solution(12626796865298724310)
XLA Ops:
  0.6 0.8 fusion.113
  1.5 1.3 collective-permute-start.1
  2.8 4.7 %collective-permute-start = (f32[4,1,128]{2,1,0:T(1,128)S(1)}, f32[4,1,128]{2,1,0:T(1,128)S(1)}, u32[]{:S(2)}, u32[]{:S(2)}) collective-permute-start(f32[4,1,128]{2,1,0:T(1,128)S(1)} %get-tuple-element.10), channel_id=1, source_target_pairs={{0,8},{8,16},{16,24},{24,32},{32,40},{40,48},{48,56},{56,64},{64,7... | collective-permute-start | bytes 6152 | tf_op jit(solution)/shard_map/ppermute | solution.py:21
  8.9 5.0 %collective-permute-start.2 = (f32[4,10,1]{2,1,0:T(8,128)S(1)}, f32[4,10,1]{2,1,0:T(8,128)S(1)}, u32[]{:S(2)}, u32[]{:S(2)}) collective-permute-start(f32[4,10,1]{2,1,0:T(8,128)S(1)} %get-tuple-element.7), channel_id=1, source_target_pairs={{0,1},{1,2},{2,3},{3,4},{4,5},{5,6},{6,7},{8,9},{9,10},{10,11},{11... | collective-permute-start | bytes 488 | tf_op jit(solution)/shard_map/ppermute | solution.py:21
  13.9 1.9 collective-permute-start.3
  15.9 3.3 %collective-permute-done.3 = f32[4,10,1]{2,1,0:T(8,128)S(1)} collective-permute-done((f32[4,10,1]{2,1,0:T(8,128)S(1)}, f32[4,10,1]{2,1,0:T(8,128)S(1)}, u32[]{:S(2)}, u32[]{:S(2)}) %collective-permute-start.3) | collective-permute-done | bytes 192 | tf_op jit(solution)/shard_map/ppermute | solution.py:22
  19.1 0.8 select_maximum_fusion
  20.0 0.8 bitcast_dynamic-update-slice_fusion.5
  21.6 1.0 add_add_fusion
  22.6 1.7 broadcast_divide_fusion
  24.3 0.8 bitcast_dynamic-update-slice_fusion.3
  25.1 0.8 bitcast_dynamic-update-slice_fusion.2
  25.9 0.9 bitcast_dynamic-update-slice_fusion.1
  27.5 22.5 %krylov_basis.5 = f32[5,512,128]{2,1,0:T(8,128)} custom-call(f32[512,128]{1,0:T(8,128)} %bitcast.107, f32[6,32,128]{2,1,0:T(8,128)} %copy-done, f32[32,128]{1,0:T(8,128)} %bitcast.108), custom_call_target="tpu_custom_call" | custom-call | tf_op jit(solution)/shard_map/krylov_basis/pallas_call | solution.py:275
  49.9 1.5 reshape_reshape.27
  51.5 1.2 fusion.114
  53.3 22.8 %gram_allreduce.5 = f32[128,128]{1,0:T(8,128)} custom-call(f32[128,128]{1,0:T(8,128)} %pad.26.refs_0_), custom_call_target="tpu_custom_call" | custom-call | tf_op jit(solution)/shard_map/gram_allreduce/pallas_call | solution.py:154
  76.0 1.1 fusion.10
  77.6 5.8 %custom-call.21 = f32[64,64]{1,0:T(8,128)S(1)} custom-call(f32[64,64]{1,0:T(8,128)S(1)} %fusion.16), custom_call_target="Cholesky" | custom-call | tf_op jit(solution)/shard_map/cholesky/custom-call.1 | solution.py:322
  84.8 4.9 %custom-call.23 = f32[1,64,64]{1,2,0:T(8,128)S(1)} custom-call(f32[1,64,64]{2,1,0:T(8,128)S(1)} %fusion.17), custom_call_target="InvertDiagBlocksLowerTriangular" | custom-call | tf_op jit(solution)/shard_map/triangular_solve/custom-call.2 | solution.py:324
  92.0 16.8 %krylov_basis.6 = f32[5,512,128]{2,1,0:T(8,128)} custom-call(f32[512,128]{1,0:T(8,128)} %reshape_reshape.28.refs_0_, f32[6,32,128]{2,1,0:T(8,128)} %copy-done, f32[32,128]{1,0:T(8,128)} %bitcast.109), custom_call_target="tpu_custom_call" | custom-call | tf_op jit(solution)/shard_map/krylov_basis/pallas_call | solution.py:275
  108.8 1.5 reshape_reshape.29
  110.3 1.2 fusion.115
  112.1 22.4 %gram_allreduce.6 = f32[128,128]{1,0:T(8,128)} custom-call(f32[128,128]{1,0:T(8,128)} %pad.27.refs_0_), custom_call_target="tpu_custom_call" | custom-call | tf_op jit(solution)/shard_map/gram_allreduce/pallas_call | solution.py:154
  134.5 1.1 fusion.8
  136.1 5.8 %custom-call.24 = f32[64,64]{1,0:T(8,128)S(1)} custom-call(f32[64,64]{1,0:T(8,128)S(1)} %fusion.15), custom_call_target="Cholesky" | custom-call | tf_op jit(solution)/shard_map/cholesky/custom-call.1 | solution.py:322
  143.2 4.9 %custom-call.26 = f32[1,64,64]{1,2,0:T(8,128)S(1)} custom-call(f32[1,64,64]{2,1,0:T(8,128)S(1)} %fusion.18), custom_call_target="InvertDiagBlocksLowerTriangular" | custom-call | tf_op jit(solution)/shard_map/triangular_solve/custom-call.2 | solution.py:324
  150.4 16.8 %krylov_basis.7 = f32[5,512,128]{2,1,0:T(8,128)} custom-call(f32[512,128]{1,0:T(8,128)} %reshape_reshape.30.refs_0_, f32[6,32,128]{2,1,0:T(8,128)} %copy-done, f32[32,128]{1,0:T(8,128)} %bitcast.110), custom_call_target="tpu_custom_call" | custom-call | tf_op jit(solution)/shard_map/krylov_basis/pallas_call | solution.py:275
  167.2 1.5 reshape_reshape.31
  168.8 1.2 fusion.116
  170.6 22.4 %gram_allreduce.7 = f32[128,128]{1,0:T(8,128)} custom-call(f32[128,128]{1,0:T(8,128)} %pad.28.refs_0_), custom_call_target="tpu_custom_call" | custom-call | tf_op jit(solution)/shard_map/gram_allreduce/pallas_call | solution.py:154
  193.0 1.1 fusion.6
  194.6 5.8 %custom-call.27 = f32[64,64]{1,0:T(8,128)S(1)} custom-call(f32[64,64]{1,0:T(8,128)S(1)} %fusion.14), custom_call_target="Cholesky" | custom-call | tf_op jit(solution)/shard_map/cholesky/custom-call.1 | solution.py:322
  201.8 4.9 %custom-call.29 = f32[1,64,64]{1,2,0:T(8,128)S(1)} custom-call(f32[1,64,64]{2,1,0:T(8,128)S(1)} %fusion.19), custom_call_target="InvertDiagBlocksLowerTriangular" | custom-call | tf_op jit(solution)/shard_map/triangular_solve/custom-call.2 | solution.py:324
  208.9 16.9 %krylov_basis.8 = f32[5,512,128]{2,1,0:T(8,128)} custom-call(f32[512,128]{1,0:T(8,128)} %reshape_reshape.32.refs_0_, f32[6,32,128]{2,1,0:T(8,128)} %copy-done, f32[32,128]{1,0:T(8,128)} %bitcast.111), custom_call_target="tpu_custom_call" | custom-call | tf_op jit(solution)/shard_map/krylov_basis/pallas_call | solution.py:275
  225.8 1.5 reshape_reshape.33
  227.3 1.2 fusion.117
  229.2 22.4 %gram_allreduce.8 = f32[128,128]{1,0:T(8,128)} custom-call(f32[128,128]{1,0:T(8,128)} %pad.29.refs_0_), custom_call_target="tpu_custom_call" | custom-call | tf_op jit(solution)/shard_map/gram_allreduce/pallas_call | solution.py:154
  251.6 1.1 fusion.4
  253.1 5.8 %custom-call.30 = f32[64,64]{1,0:T(8,128)S(1)} custom-call(f32[64,64]{1,0:T(8,128)S(1)} %fusion.13), custom_call_target="Cholesky" | custom-call | tf_op jit(solution)/shard_map/cholesky/custom-call.1 | solution.py:322
  260.3 4.9 %custom-call.32 = f32[1,64,64]{1,2,0:T(8,128)S(1)} custom-call(f32[1,64,64]{2,1,0:T(8,128)S(1)} %fusion.20), custom_call_target="InvertDiagBlocksLowerTriangular" | custom-call | tf_op jit(solution)/shard_map/triangular_solve/custom-call.2 | solution.py:324
  267.5 16.8 %krylov_basis.9 = f32[5,512,128]{2,1,0:T(8,128)} custom-call(f32[512,128]{1,0:T(8,128)} %reshape_reshape.34.refs_0_, f32[6,32,128]{2,1,0:T(8,128)} %copy-done, f32[32,128]{1,0:T(8,128)} %bitcast.112), custom_call_target="tpu_custom_call" | custom-call | tf_op jit(solution)/shard_map/krylov_basis/pallas_call | solution.py:275
  284.3 1.5 reshape_reshape.35
  285.8 1.2 fusion.118
  287.6 22.5 %gram_allreduce.9 = f32[128,128]{1,0:T(8,128)} custom-call(f32[128,128]{1,0:T(8,128)} %pad.30.refs_0_), custom_call_target="tpu_custom_call" | custom-call | tf_op jit(solution)/shard_map/gram_allreduce/pallas_call | solution.py:154
  310.1 1.1 fusion.2
  311.7 5.8 %custom-call.33 = f32[64,64]{1,0:T(8,128)S(1)} custom-call(f32[64,64]{1,0:T(8,128)S(1)} %fusion.12), custom_call_target="Cholesky" | custom-call | tf_op jit(solution)/shard_map/cholesky/custom-call.1 | solution.py:322
  318.9 4.9 %custom-call.35 = f32[1,64,64]{1,2,0:T(8,128)S(1)} custom-call(f32[1,64,64]{2,1,0:T(8,128)S(1)} %fusion.21), custom_call_target="InvertDiagBlocksLowerTriangular" | custom-call | tf_op jit(solution)/shard_map/triangular_solve/custom-call.2 | solution.py:324
  (75 shorter events, 27.2 us)
Async XLA Ops:
  0.6 26.1 %copy-start.1 = (f32[4,8,128]{2,1,0:T(8,128)S(1)}, f32[4,8,128]{2,1,0:T(8,128)}, u32[]{:S(2)}) copy-start(f32[4,8,128]{2,1,0:T(8,128)} %param.9) | copy-start | bytes 49156
  1.5 6.0 %collective-permute-start.1 = (f32[4,1,128]{2,1,0:T(1,128)S(1)}, f32[4,1,128]{2,1,0:T(1,128)S(1)}, u32[]{:S(2)}, u32[]{:S(2)}) collective-permute-start(f32[4,1,128]{2,1,0:T(1,128)S(1)} %get-tuple-element.9), channel_id=1, source_target_pairs={{8,0},{16,8},{24,16},{32,24},{40,32},{48,40},{56,48},{64,56},{72,6... | collective-permute-start | bytes 6152 | tf_op jit(solution)/shard_map/ppermute | solution.py:22
  2.8 5.4 %collective-permute-start = (f32[4,1,128]{2,1,0:T(1,128)S(1)}, f32[4,1,128]{2,1,0:T(1,128)S(1)}, u32[]{:S(2)}, u32[]{:S(2)}) collective-permute-start(f32[4,1,128]{2,1,0:T(1,128)S(1)} %get-tuple-element.10), channel_id=1, source_target_pairs={{0,8},{8,16},{16,24},{24,32},{32,40},{40,48},{48,56},{56,64},{64,7... | collective-permute-start | bytes 6152 | tf_op jit(solution)/shard_map/ppermute | solution.py:21
  8.9 6.9 %collective-permute-start.2 = (f32[4,10,1]{2,1,0:T(8,128)S(1)}, f32[4,10,1]{2,1,0:T(8,128)S(1)}, u32[]{:S(2)}, u32[]{:S(2)}) collective-permute-start(f32[4,10,1]{2,1,0:T(8,128)S(1)} %get-tuple-element.7), channel_id=1, source_target_pairs={{0,1},{1,2},{2,3},{3,4},{4,5},{5,6},{6,7},{8,9},{9,10},{10,11},{11... | collective-permute-start | bytes 488 | tf_op jit(solution)/shard_map/ppermute | solution.py:21
  13.9 5.2 %collective-permute-start.3 = (f32[4,10,1]{2,1,0:T(8,128)S(1)}, f32[4,10,1]{2,1,0:T(8,128)S(1)}, u32[]{:S(2)}, u32[]{:S(2)}) collective-permute-start(f32[4,10,1]{2,1,0:T(8,128)S(1)} %get-tuple-element.8), channel_id=1, source_target_pairs={{1,0},{2,1},{3,2},{4,3},{5,4},{6,5},{7,6},{9,8},{10,9},{11,10},{12... | collective-permute-start | bytes 488 | tf_op jit(solution)/shard_map/ppermute | solution.py:22
  22.6 4.3 %copy-start.2 = (f32[4,8,128]{2,1,0:T(8,128)}, f32[4,8,128]{2,1,0:T(8,128)S(1)}, u32[]{:S(2)}) copy-start(f32[4,8,128]{2,1,0:T(8,128)S(1)} %add_add_fusion) | copy-start | bytes 49156
  26.8 0.6 copy-start

commit v8 on v5

--- a/solution.py
+++ b/solution.py
@@ -239,10 +239,6 @@
             def _():
                 copy(d).start()
         for d in range(4):
-            @pl.when(targets[d][0])
-            def _():
-                copy(d).wait_send()
-
             @pl.when(targets[d][2])
             def _():
                 copy(d).wait_recv()
@@ -265,6 +261,10 @@
         total = total + t[2] * xm + t[3] * xp
         total = total + t[4] * ym + t[5] * yp
         out_ref[k + 1] = (-total / diag).reshape(cells, lanes)
+        for d in range(4):
+            @pl.when(targets[d][0])
+            def _():
+                copy(d).wait_send()
 
 
 def krylov_basis(v0, terms, diagonal):

time: 329 us -> 329 us (level)
  no operation moved by 1% of the time
where the time goes in v8:
time: 329 us; the launch traced here: 328 us
  Pallas kernels  202 us (61%)
  other arithmetic  68.9 us (21%)
  matrix products  21 us (6%)
  local copies, waits for them, and re-layouts  17.2 us (5%)
  starting transfers between devices  12.8 us (4%)
  waiting for transfers between devices  4 us (1%)
    pallas_call x5, Pallas kernels, gram_sum(): pl.pallas_call(lambda *refs: reduce_kernel(nx, ny, *refs), out_shape=jax....  112 us
    pallas_call x5, Pallas kernels, krylov_basis(): pl.pallas_call(lambda *refs: krylov_kernel(nx, ny, bx, *refs), out_shape=...  90 us
    another operation x15, other arithmetic, small_solve(): lower = jnp.linalg.cholesky(normal)  32.6 us
    another operation x10, other arithmetic, small_solve(): y = jax.scipy.linalg.cho_solve((lower, True), right_side)  27.7 us
    ppermute x2, starting transfers between devices, padded_2(): before = lax.ppermute(last, axis, up)  9.62 us
    another operation x5, local copies, waits for them, and re-layouts, shards(): stacked = krylov_basis(residual, terms, diagonal).reshape(BASIS, -1)  7.57 us
  transfers between devices with their start and end apart: 4, of which 2 were waited for; matrix products, arithmetic and copies ran while one was open for 0% of the time, Pallas kernels for 0%

profile of v8, /device:TPU:1, one launch (start us, length us, event | category | flops | bytes accessed | tf_op | source)
XLA Modules:
  0.0 327.6 jit_solution(4074163038987792153)
XLA Ops:
  0.6 0.8 fusion.118
  1.5 1.3 collective-permute-start.1
  2.8 4.7 %collective-permute-start = (f32[4,1,128]{2,1,0:T(1,128)S(1)}, f32[4,1,128]{2,1,0:T(1,128)S(1)}, u32[]{:S(2)}, u32[]{:S(2)}) collective-permute-start(f32[4,1,128]{2,1,0:T(1,128)S(1)} %get-tuple-element.9), channel_id=1, source_target_pairs={{0,8},{8,16},{16,24},{24,32},{32,40},{40,48},{48,56},{56,64},{64,7... | collective-permute-start | bytes 6152 | tf_op jit(solution)/shard_map/ppermute | solution.py:21
  8.9 5.0 %collective-permute-start.2 = (f32[4,10,1]{2,1,0:T(8,128)S(1)}, f32[4,10,1]{2,1,0:T(8,128)S(1)}, u32[]{:S(2)}, u32[]{:S(2)}) collective-permute-start(f32[4,10,1]{2,1,0:T(8,128)S(1)} %get-tuple-element.6), channel_id=1, source_target_pairs={{0,1},{1,2},{2,3},{3,4},{4,5},{5,6},{6,7},{8,9},{9,10},{10,11},{11... | collective-permute-start | bytes 488 | tf_op jit(solution)/shard_map/ppermute | solution.py:21
  13.9 1.9 collective-permute-start.3
  15.9 3.3 %collective-permute-done.3 = f32[4,10,1]{2,1,0:T(8,128)S(1)} collective-permute-done((f32[4,10,1]{2,1,0:T(8,128)S(1)}, f32[4,10,1]{2,1,0:T(8,128)S(1)}, u32[]{:S(2)}, u32[]{:S(2)}) %collective-permute-start.3) | collective-permute-done | bytes 192 | tf_op jit(solution)/shard_map/ppermute | solution.py:22
  19.1 0.8 select_maximum_fusion
  20.0 0.8 bitcast_dynamic-update-slice_fusion.5
  21.6 1.0 add_add_fusion
  22.6 1.7 broadcast_divide_fusion
  24.3 0.8 bitcast_dynamic-update-slice_fusion.3
  25.1 0.8 bitcast_dynamic-update-slice_fusion.2
  25.9 0.9 bitcast_dynamic-update-slice_fusion.1
  27.5 22.5 %krylov_basis.5 = f32[5,512,128]{2,1,0:T(8,128)} custom-call(f32[512,128]{1,0:T(8,128)} %bitcast.117, f32[6,32,128]{2,1,0:T(8,128)} %copy-done, f32[32,128]{1,0:T(8,128)} %bitcast.118), custom_call_target="tpu_custom_call" | custom-call | tf_op jit(solution)/shard_map/krylov_basis/pallas_call | solution.py:275
  50.0 1.5 reshape_reshape.27
  51.5 1.2 fusion.119
  53.3 22.7 %gram_allreduce.5 = f32[128,128]{1,0:T(8,128)} custom-call(f32[128,128]{1,0:T(8,128)} %pad.26.refs_0_), custom_call_target="tpu_custom_call" | custom-call | tf_op jit(solution)/shard_map/gram_allreduce/pallas_call | solution.py:154
  76.1 1.1 fusion.10
  77.8 5.8 %cholesky.89 = f32[64,64]{1,0:T(8,128)S(1)} custom-call(f32[64,64]{1,0:T(8,128)S(1)} %fusion.46), custom_call_target="Cholesky" | custom-call | tf_op jit(solution)/shard_map/jit(cholesky)/cholesky | solution.py:322
  84.9 4.9 %custom-call.11 = f32[1,64,64]{1,2,0:T(8,128)S(1)} custom-call(f32[1,64,64]{2,1,0:T(8,128)S(1)} %fusion.17), custom_call_target="InvertDiagBlocksLowerTriangular" | custom-call | tf_op jit(solution)/shard_map/jit(_cho_solve)/triangular_solve | solution.py:323
  92.1 16.9 %krylov_basis.6 = f32[5,512,128]{2,1,0:T(8,128)} custom-call(f32[512,128]{1,0:T(8,128)} %reshape_reshape.28.refs_0_, f32[6,32,128]{2,1,0:T(8,128)} %copy-done, f32[32,128]{1,0:T(8,128)} %bitcast.119), custom_call_target="tpu_custom_call" | custom-call | tf_op jit(solution)/shard_map/krylov_basis/pallas_call | solution.py:275
  109.0 1.5 reshape_reshape.29
  110.5 1.2 fusion.120
  112.3 22.4 %gram_allreduce.6 = f32[128,128]{1,0:T(8,128)} custom-call(f32[128,128]{1,0:T(8,128)} %pad.27.refs_0_), custom_call_target="tpu_custom_call" | custom-call | tf_op jit(solution)/shard_map/gram_allreduce/pallas_call | solution.py:154
  134.7 1.1 fusion.8
  136.4 5.8 %cholesky.100 = f32[64,64]{1,0:T(8,128)S(1)} custom-call(f32[64,64]{1,0:T(8,128)S(1)} %fusion.41), custom_call_target="Cholesky" | custom-call | tf_op jit(solution)/shard_map/jit(cholesky)/cholesky | solution.py:322
  143.6 4.9 %custom-call.12 = f32[1,64,64]{1,2,0:T(8,128)S(1)} custom-call(f32[1,64,64]{2,1,0:T(8,128)S(1)} %fusion.18), custom_call_target="InvertDiagBlocksLowerTriangular" | custom-call | tf_op jit(solution)/shard_map/jit(_cho_solve)/triangular_solve | solution.py:323
  150.7 16.9 %krylov_basis.7 = f32[5,512,128]{2,1,0:T(8,128)} custom-call(f32[512,128]{1,0:T(8,128)} %reshape_reshape.30.refs_0_, f32[6,32,128]{2,1,0:T(8,128)} %copy-done, f32[32,128]{1,0:T(8,128)} %bitcast.120), custom_call_target="tpu_custom_call" | custom-call | tf_op jit(solution)/shard_map/krylov_basis/pallas_call | solution.py:275
  167.6 1.5 reshape_reshape.31
  169.1 1.2 fusion.121
  171.0 22.4 %gram_allreduce.7 = f32[128,128]{1,0:T(8,128)} custom-call(f32[128,128]{1,0:T(8,128)} %pad.28.refs_0_), custom_call_target="tpu_custom_call" | custom-call | tf_op jit(solution)/shard_map/gram_allreduce/pallas_call | solution.py:154
  193.4 1.1 fusion.6
  195.1 5.8 %cholesky.111 = f32[64,64]{1,0:T(8,128)S(1)} custom-call(f32[64,64]{1,0:T(8,128)S(1)} %fusion.36), custom_call_target="Cholesky" | custom-call | tf_op jit(solution)/shard_map/jit(cholesky)/cholesky | solution.py:322
  202.2 4.9 %custom-call.13 = f32[1,64,64]{1,2,0:T(8,128)S(1)} custom-call(f32[1,64,64]{2,1,0:T(8,128)S(1)} %fusion.19), custom_call_target="InvertDiagBlocksLowerTriangular" | custom-call | tf_op jit(solution)/shard_map/jit(_cho_solve)/triangular_solve | solution.py:323
  209.4 16.9 %krylov_basis.8 = f32[5,512,128]{2,1,0:T(8,128)} custom-call(f32[512,128]{1,0:T(8,128)} %reshape_reshape.32.refs_0_, f32[6,32,128]{2,1,0:T(8,128)} %copy-done, f32[32,128]{1,0:T(8,128)} %bitcast.121), custom_call_target="tpu_custom_call" | custom-call | tf_op jit(solution)/shard_map/krylov_basis/pallas_call | solution.py:275
  226.4 1.5 reshape_reshape.33
  227.9 1.2 fusion.122
  229.7 22.4 %gram_allreduce.8 = f32[128,128]{1,0:T(8,128)} custom-call(f32[128,128]{1,0:T(8,128)} %pad.29.refs_0_), custom_call_target="tpu_custom_call" | custom-call | tf_op jit(solution)/shard_map/gram_allreduce/pallas_call | solution.py:154
  252.1 1.1 fusion.4
  253.8 5.8 %cholesky.122 = f32[64,64]{1,0:T(8,128)S(1)} custom-call(f32[64,64]{1,0:T(8,128)S(1)} %fusion.31), custom_call_target="Cholesky" | custom-call | tf_op jit(solution)/shard_map/jit(cholesky)/cholesky | solution.py:322
  261.0 4.9 %custom-call.14 = f32[1,64,64]{1,2,0:T(8,128)S(1)} custom-call(f32[1,64,64]{2,1,0:T(8,128)S(1)} %fusion.20), custom_call_target="InvertDiagBlocksLowerTriangular" | custom-call | tf_op jit(solution)/shard_map/jit(_cho_solve)/triangular_solve | solution.py:323
  268.1 16.8 %krylov_basis.9 = f32[5,512,128]{2,1,0:T(8,128)} custom-call(f32[512,128]{1,0:T(8,128)} %reshape_reshape.34.refs_0_, f32[6,32,128]{2,1,0:T(8,128)} %copy-done, f32[32,128]{1,0:T(8,128)} %bitcast.122), custom_call_target="tpu_custom_call" | custom-call | tf_op jit(solution)/shard_map/krylov_basis/pallas_call | solution.py:275
  285.0 1.5 reshape_reshape.35
  286.5 1.2 fusion.123
  288.3 22.5 %gram_allreduce.9 = f32[128,128]{1,0:T(8,128)} custom-call(f32[128,128]{1,0:T(8,128)} %pad.30.refs_0_), custom_call_target="tpu_custom_call" | custom-call | tf_op jit(solution)/shard_map/gram_allreduce/pallas_call | solution.py:154
  310.8 1.1 fusion.2
  312.5 5.8 %cholesky.133 = f32[64,64]{1,0:T(8,128)S(1)} custom-call(f32[64,64]{1,0:T(8,128)S(1)} %fusion.26), custom_call_target="Cholesky" | custom-call | tf_op jit(solution)/shard_map/jit(cholesky)/cholesky | solution.py:322
  319.6 4.9 %custom-call.15 = f32[1,64,64]{1,2,0:T(8,128)S(1)} custom-call(f32[1,64,64]{2,1,0:T(8,128)S(1)} %fusion.21), custom_call_target="InvertDiagBlocksLowerTriangular" | custom-call | tf_op jit(solution)/shard_map/jit(_cho_solve)/triangular_solve | solution.py:323
  (85 shorter events, 27.6 us)
Async XLA Ops:
  0.6 26.1 %copy-start.1 = (f32[4,8,128]{2,1,0:T(8,128)S(1)}, f32[4,8,128]{2,1,0:T(8,128)}, u32[]{:S(2)}) copy-start(f32[4,8,128]{2,1,0:T(8,128)} %param.7) | copy-start | bytes 49156
  1.5 6.0 %collective-permute-start.1 = (f32[4,1,128]{2,1,0:T(1,128)S(1)}, f32[4,1,128]{2,1,0:T(1,128)S(1)}, u32[]{:S(2)}, u32[]{:S(2)}) collective-permute-start(f32[4,1,128]{2,1,0:T(1,128)S(1)} %get-tuple-element.8), channel_id=1, source_target_pairs={{8,0},{16,8},{24,16},{32,24},{40,32},{48,40},{56,48},{64,56},{72,6... | collective-permute-start | bytes 6152 | tf_op jit(solution)/shard_map/ppermute | solution.py:22
  2.8 5.4 %collective-permute-start = (f32[4,1,128]{2,1,0:T(1,128)S(1)}, f32[4,1,128]{2,1,0:T(1,128)S(1)}, u32[]{:S(2)}, u32[]{:S(2)}) collective-permute-start(f32[4,1,128]{2,1,0:T(1,128)S(1)} %get-tuple-element.9), channel_id=1, source_target_pairs={{0,8},{8,16},{16,24},{24,32},{32,40},{40,48},{48,56},{56,64},{64,7... | collective-permute-start | bytes 6152 | tf_op jit(solution)/shard_map/ppermute | solution.py:21
  8.9 6.9 %collective-permute-start.2 = (f32[4,10,1]{2,1,0:T(8,128)S(1)}, f32[4,10,1]{2,1,0:T(8,128)S(1)}, u32[]{:S(2)}, u32[]{:S(2)}) collective-permute-start(f32[4,10,1]{2,1,0:T(8,128)S(1)} %get-tuple-element.6), channel_id=1, source_target_pairs={{0,1},{1,2},{2,3},{3,4},{4,5},{5,6},{6,7},{8,9},{9,10},{10,11},{11... | collective-permute-start | bytes 488 | tf_op jit(solution)/shard_map/ppermute | solution.py:21
  13.9 5.2 %collective-permute-start.3 = (f32[4,10,1]{2,1,0:T(8,128)S(1)}, f32[4,10,1]{2,1,0:T(8,128)S(1)}, u32[]{:S(2)}, u32[]{:S(2)}) collective-permute-start(f32[4,10,1]{2,1,0:T(8,128)S(1)} %get-tuple-element.7), channel_id=1, source_target_pairs={{1,0},{2,1},{3,2},{4,3},{5,4},{6,5},{7,6},{9,8},{10,9},{11,10},{12... | collective-permute-start | bytes 488 | tf_op jit(solution)/shard_map/ppermute | solution.py:22
  22.6 4.3 %copy-start.2 = (f32[4,8,128]{2,1,0:T(8,128)}, f32[4,8,128]{2,1,0:T(8,128)S(1)}, u32[]{:S(2)}) copy-start(f32[4,8,128]{2,1,0:T(8,128)S(1)} %add_add_fusion) | copy-start | bytes 49156
  26.8 0.6 copy-start

commit v9 on v5

--- a/solution.py
+++ b/solution.py
@@ -22,6 +22,21 @@
         after = lax.ppermute(leading, axis, down)
         array = jnp.concatenate([before, array, after], axis=dim)
     return array
+
+
+def halo_faces(array, xdim, ydim):
+    out = {}
+    for axis, dim in (("gx", xdim), ("gy", ydim)):
+        devices, length = (lax.axis_size(axis), array.shape[dim])
+        up = [(i, (i + 1) % devices) for i in range(devices - 1)]
+        down = [(j, i) for i, j in up]
+        last = lax.slice_in_dim(array, length - 1, length, axis=dim)
+        leading = lax.slice_in_dim(array, 0, 1, axis=dim)
+        out[axis] = (lax.ppermute(last, axis, up), lax.ppermute(leading, axis, down))
+    rows = jnp.concatenate([out["gx"][0], array, out["gx"][1]], axis=xdim)
+    widths = [(0, 0)] * array.ndim
+    widths[xdim] = (1, 1)
+    return jnp.concatenate([jnp.pad(out["gy"][0], widths), rows, jnp.pad(out["gy"][1], widths)], axis=ydim)
 
 
 def exchange_reduce(axis, other_axis, n, src, mine, rs, ag, full, send_sem, rs_sem, ag_sem):
@@ -328,7 +343,7 @@
 def shards(pumping, conductivity, capacity):
     hp = lax.Precision.HIGHEST
     shape = pumping.shape
-    cond_halo = padded_2(conductivity, (("gx", 1), ("gy", 2)), 1)
+    cond_halo = halo_faces(conductivity, 1, 2)
     cond_pad = jnp.pad(cond_halo, ((1, 1), (0, 0), (0, 0)))
     terms, diagonal = face_terms(cond_pad, capacity)
     solution = jnp.zeros(shape, jnp.float32)

time: 329 us -> 326 us (level)
  transfers between devices with their start and end apart: 4 -> 4, of which waited for: 2 -> 1; matrix products, arithmetic and copies ran while one was open for 0% -> 0% of each run, Pallas kernels for 0% -> 0%
where the time goes in v9:
time: 326 us; the launch traced here: 324 us
  Pallas kernels  200 us (61%)
  other arithmetic  68.9 us (21%)
  matrix products  21 us (6%)
  local copies, waits for them, and re-layouts  18 us (6%)
  starting transfers between devices  12.2 us (4%)
    pallas_call x5, Pallas kernels, gram_sum(): pl.pallas_call(lambda *refs: reduce_kernel(nx, ny, *refs), out_shape=jax....  113 us
    pallas_call x5, Pallas kernels, krylov_basis(): pl.pallas_call(lambda *refs: krylov_kernel(nx, ny, bx, *refs), out_shape=...  86.8 us
    another operation x15, other arithmetic, small_solve(): lower = jnp.linalg.cholesky(normal)  32.6 us
    another operation x10, other arithmetic, small_solve(): y = jax.scipy.linalg.cho_solve((lower, True), right_side)  27.7 us
    ppermute x2, starting transfers between devices, halo_faces(): lax.ppermute(last, axis, up)  9.05 us
    another operation x5, local copies, waits for them, and re-layouts, shards(): stacked = krylov_basis(residual, terms, diagonal).reshape(BASIS, -1)  7.57 us
  transfers between devices with their start and end apart: 4, of which 1 were waited for; matrix products, arithmetic and copies ran while one was open for 0% of the time, Pallas kernels for 0%

profile of v9, /device:TPU:1, one launch (start us, length us, event | category | flops | bytes accessed | tf_op | source)
XLA Modules:
  0.0 324.4 jit_solution(2970340828266186835)
XLA Ops:
  1.4 1.3 collective-permute-start.2
  2.7 4.7 %collective-permute-start.1 = (f32[4,1,128]{2,1,0:T(1,128)S(1)}, f32[4,1,128]{2,1,0:T(1,128)S(1)}, u32[]{:S(2)}, u32[]{:S(2)}) collective-permute-start(f32[4,1,128]{2,1,0:T(1,128)S(1)} %get-tuple-element.9), channel_id=1, source_target_pairs={{0,8},{8,16},{16,24},{24,32},{32,40},{40,48},{48,56},{56,64},{64,7... | collective-permute-start | bytes 6152 | tf_op jit(solution)/shard_map/ppermute | solution.py:35
  7.4 0.9 fusion.117
  8.2 4.4 %collective-permute-start = (f32[4,8,1]{2,1,0:T(8,128)S(1)}, f32[4,8,1]{2,1,0:T(8,128)S(1)}, u32[]{:S(2)}, u32[]{:S(2)}) collective-permute-start(f32[4,8,1]{2,1,0:T(8,128)S(1)} %get-tuple-element.6), channel_id=1, source_target_pairs={{0,1},{1,2},{2,3},{3,4},{4,5},{5,6},{6,7},{8,9},{9,10},{10,11},{11... | collective-permute-start | bytes 392 | tf_op jit(solution)/shard_map/ppermute | solution.py:35
  12.6 1.9 collective-permute-start.3
  14.6 3.1 collective-permute-done.3
  17.7 0.8 select_maximum_fusion
  20.1 1.0 add_add_fusion
  21.2 1.7 broadcast_divide_fusion
  22.9 0.8 bitcast_dynamic-update-slice_fusion.3
  23.7 0.8 bitcast_dynamic-update-slice_fusion.2
  24.5 0.9 bitcast_dynamic-update-slice_fusion.1
  25.3 0.9 bitcast_dynamic-update-slice_fusion.refs_1_
  26.8 19.7 %krylov_basis.5 = f32[5,512,128]{2,1,0:T(8,128)} custom-call(f32[512,128]{1,0:T(8,128)} %bitcast.117, f32[6,32,128]{2,1,0:T(8,128)} %copy-done, f32[32,128]{1,0:T(8,128)} %bitcast.118), custom_call_target="tpu_custom_call" | custom-call | tf_op jit(solution)/shard_map/krylov_basis/pallas_call | solution.py:290
  46.6 1.5 reshape_reshape.27
  48.1 1.2 fusion.119
  49.9 23.2 %gram_allreduce.5 = f32[128,128]{1,0:T(8,128)} custom-call(f32[128,128]{1,0:T(8,128)} %pad.35.refs_0_), custom_call_target="tpu_custom_call" | custom-call | tf_op jit(solution)/shard_map/gram_allreduce/pallas_call | solution.py:169
  73.1 1.1 fusion.10
  74.8 5.8 %cholesky.89 = f32[64,64]{1,0:T(8,128)S(1)} custom-call(f32[64,64]{1,0:T(8,128)S(1)} %fusion.46), custom_call_target="Cholesky" | custom-call | tf_op jit(solution)/shard_map/jit(cholesky)/cholesky | solution.py:337
  81.9 4.9 %custom-call.11 = f32[1,64,64]{1,2,0:T(8,128)S(1)} custom-call(f32[1,64,64]{2,1,0:T(8,128)S(1)} %fusion.17), custom_call_target="InvertDiagBlocksLowerTriangular" | custom-call | tf_op jit(solution)/shard_map/jit(_cho_solve)/triangular_solve | solution.py:338
  89.1 16.8 %krylov_basis.6 = f32[5,512,128]{2,1,0:T(8,128)} custom-call(f32[512,128]{1,0:T(8,128)} %reshape_reshape.28.refs_0_, f32[6,32,128]{2,1,0:T(8,128)} %copy-done, f32[32,128]{1,0:T(8,128)} %bitcast.119), custom_call_target="tpu_custom_call" | custom-call | tf_op jit(solution)/shard_map/krylov_basis/pallas_call | solution.py:290
  105.9 1.5 reshape_reshape.29
  107.4 1.2 fusion.120
  109.3 22.5 %gram_allreduce.6 = f32[128,128]{1,0:T(8,128)} custom-call(f32[128,128]{1,0:T(8,128)} %pad.36.refs_0_), custom_call_target="tpu_custom_call" | custom-call | tf_op jit(solution)/shard_map/gram_allreduce/pallas_call | solution.py:169
  131.8 1.1 fusion.8
  133.4 5.8 %cholesky.100 = f32[64,64]{1,0:T(8,128)S(1)} custom-call(f32[64,64]{1,0:T(8,128)S(1)} %fusion.41), custom_call_target="Cholesky" | custom-call | tf_op jit(solution)/shard_map/jit(cholesky)/cholesky | solution.py:337
  140.6 4.9 %custom-call.12 = f32[1,64,64]{1,2,0:T(8,128)S(1)} custom-call(f32[1,64,64]{2,1,0:T(8,128)S(1)} %fusion.18), custom_call_target="InvertDiagBlocksLowerTriangular" | custom-call | tf_op jit(solution)/shard_map/jit(_cho_solve)/triangular_solve | solution.py:338
  147.8 16.7 %krylov_basis.7 = f32[5,512,128]{2,1,0:T(8,128)} custom-call(f32[512,128]{1,0:T(8,128)} %reshape_reshape.30.refs_0_, f32[6,32,128]{2,1,0:T(8,128)} %copy-done, f32[32,128]{1,0:T(8,128)} %bitcast.120), custom_call_target="tpu_custom_call" | custom-call | tf_op jit(solution)/shard_map/krylov_basis/pallas_call | solution.py:290
  164.6 1.5 reshape_reshape.31
  166.1 1.2 fusion.121
  167.9 22.5 %gram_allreduce.7 = f32[128,128]{1,0:T(8,128)} custom-call(f32[128,128]{1,0:T(8,128)} %pad.37.refs_0_), custom_call_target="tpu_custom_call" | custom-call | tf_op jit(solution)/shard_map/gram_allreduce/pallas_call | solution.py:169
  190.4 1.1 fusion.6
  192.0 5.8 %cholesky.111 = f32[64,64]{1,0:T(8,128)S(1)} custom-call(f32[64,64]{1,0:T(8,128)S(1)} %fusion.36), custom_call_target="Cholesky" | custom-call | tf_op jit(solution)/shard_map/jit(cholesky)/cholesky | solution.py:337
  199.2 4.9 %custom-call.13 = f32[1,64,64]{1,2,0:T(8,128)S(1)} custom-call(f32[1,64,64]{2,1,0:T(8,128)S(1)} %fusion.19), custom_call_target="InvertDiagBlocksLowerTriangular" | custom-call | tf_op jit(solution)/shard_map/jit(_cho_solve)/triangular_solve | solution.py:338
  206.4 16.8 %krylov_basis.8 = f32[5,512,128]{2,1,0:T(8,128)} custom-call(f32[512,128]{1,0:T(8,128)} %reshape_reshape.32.refs_0_, f32[6,32,128]{2,1,0:T(8,128)} %copy-done, f32[32,128]{1,0:T(8,128)} %bitcast.121), custom_call_target="tpu_custom_call" | custom-call | tf_op jit(solution)/shard_map/krylov_basis/pallas_call | solution.py:290
  223.2 1.5 reshape_reshape.33
  224.7 1.2 fusion.122
  226.5 22.5 %gram_allreduce.8 = f32[128,128]{1,0:T(8,128)} custom-call(f32[128,128]{1,0:T(8,128)} %pad.38.refs_0_), custom_call_target="tpu_custom_call" | custom-call | tf_op jit(solution)/shard_map/gram_allreduce/pallas_call | solution.py:169
  249.0 1.1 fusion.4
  250.7 5.8 %cholesky.122 = f32[64,64]{1,0:T(8,128)S(1)} custom-call(f32[64,64]{1,0:T(8,128)S(1)} %fusion.31), custom_call_target="Cholesky" | custom-call | tf_op jit(solution)/shard_map/jit(cholesky)/cholesky | solution.py:337
  257.8 4.9 %custom-call.14 = f32[1,64,64]{1,2,0:T(8,128)S(1)} custom-call(f32[1,64,64]{2,1,0:T(8,128)S(1)} %fusion.20), custom_call_target="InvertDiagBlocksLowerTriangular" | custom-call | tf_op jit(solution)/shard_map/jit(_cho_solve)/triangular_solve | solution.py:338
  265.0 16.8 %krylov_basis.9 = f32[5,512,128]{2,1,0:T(8,128)} custom-call(f32[512,128]{1,0:T(8,128)} %reshape_reshape.34.refs_0_, f32[6,32,128]{2,1,0:T(8,128)} %copy-done, f32[32,128]{1,0:T(8,128)} %bitcast.122), custom_call_target="tpu_custom_call" | custom-call | tf_op jit(solution)/shard_map/krylov_basis/pallas_call | solution.py:290
  281.8 1.5 reshape_reshape.35
  283.3 1.2 fusion.123
  285.1 22.4 %gram_allreduce.9 = f32[128,128]{1,0:T(8,128)} custom-call(f32[128,128]{1,0:T(8,128)} %pad.39.refs_0_), custom_call_target="tpu_custom_call" | custom-call | tf_op jit(solution)/shard_map/gram_allreduce/pallas_call | solution.py:169
  307.6 1.1 fusion.2
  309.2 5.8 %cholesky.133 = f32[64,64]{1,0:T(8,128)S(1)} custom-call(f32[64,64]{1,0:T(8,128)S(1)} %fusion.26), custom_call_target="Cholesky" | custom-call | tf_op jit(solution)/shard_map/jit(cholesky)/cholesky | solution.py:337
  316.4 4.9 %custom-call.15 = f32[1,64,64]{1,2,0:T(8,128)S(1)} custom-call(f32[1,64,64]{2,1,0:T(8,128)S(1)} %fusion.21), custom_call_target="InvertDiagBlocksLowerTriangular" | custom-call | tf_op jit(solution)/shard_map/jit(_cho_solve)/triangular_solve | solution.py:338
  (84 shorter events, 27.6 us)
Async XLA Ops:
  1.4 16.3 %collective-permute-start.2 = (f32[4,1,128]{2,1,0:T(1,128)S(1)}, f32[4,1,128]{2,1,0:T(1,128)S(1)}, u32[]{:S(2)}, u32[]{:S(2)}) collective-permute-start(f32[4,1,128]{2,1,0:T(1,128)S(1)} %get-tuple-element.8), channel_id=1, source_target_pairs={{8,0},{16,8},{24,16},{32,24},{40,32},{48,40},{56,48},{64,56},{72,6... | collective-permute-start | bytes 6152 | tf_op jit(solution)/shard_map/ppermute | solution.py:35
  2.7 15.0 %collective-permute-start.1 = (f32[4,1,128]{2,1,0:T(1,128)S(1)}, f32[4,1,128]{2,1,0:T(1,128)S(1)}, u32[]{:S(2)}, u32[]{:S(2)}) collective-permute-start(f32[4,1,128]{2,1,0:T(1,128)S(1)} %get-tuple-element.9), channel_id=1, source_target_pairs={{0,8},{8,16},{16,24},{24,32},{32,40},{40,48},{48,56},{56,64},{64,7... | collective-permute-start | bytes 6152 | tf_op jit(solution)/shard_map/ppermute | solution.py:35
  8.2 6.3 %collective-permute-start = (f32[4,8,1]{2,1,0:T(8,128)S(1)}, f32[4,8,1]{2,1,0:T(8,128)S(1)}, u32[]{:S(2)}, u32[]{:S(2)}) collective-permute-start(f32[4,8,1]{2,1,0:T(8,128)S(1)} %get-tuple-element.6), channel_id=1, source_target_pairs={{0,1},{1,2},{2,3},{3,4},{4,5},{5,6},{6,7},{8,9},{9,10},{10,11},{11... | collective-permute-start | bytes 392 | tf_op jit(solution)/shard_map/ppermute | solution.py:35
  12.6 5.1 %collective-permute-start.3 = (f32[4,8,1]{2,1,0:T(8,128)S(1)}, f32[4,8,1]{2,1,0:T(8,128)S(1)}, u32[]{:S(2)}, u32[]{:S(2)}) collective-permute-start(f32[4,8,1]{2,1,0:T(8,128)S(1)} %get-tuple-element.7), channel_id=1, source_target_pairs={{1,0},{2,1},{3,2},{4,3},{5,4},{6,5},{7,6},{9,8},{10,9},{11,10},{12... | collective-permute-start | bytes 392 | tf_op jit(solution)/shard_map/ppermute | solution.py:35
  21.2 5.1 %copy-start.1 = (f32[4,8,128]{2,1,0:T(8,128)}, f32[4,8,128]{2,1,0:T(8,128)S(1)}, u32[]{:S(2)}) copy-start(f32[4,8,128]{2,1,0:T(8,128)S(1)} %add_add_fusion) | copy-start | bytes 49156
  26.2 0.6 copy-start

commit v10 on v9

--- a/solution.py
+++ b/solution.py
@@ -192,7 +192,7 @@
     return total[:size, :size]
 
 
-def krylov_kernel(nx, ny, bx, v0_ref, terms_ref, diag_ref, out_ref,
+def krylov_kernel(nx, ny, bx, v0_ref, terms_ref, diag_ref, tiled_ref, out_ref,
                   halo_x, xsend, ysend, xr, yr, send_sem, recv_sem):
     gx = lax.axis_index("gx")
     gy = lax.axis_index("gy")
@@ -281,6 +281,16 @@
         total = total + t[4] * ym + t[5] * yp
         out_ref[k + 1] = (-total / diag).reshape(cells, lanes)
 
+    groups = rhs // 8
+
+    def to_tiled(zx, carry):
+        for k in range(out_ref.shape[0]):
+            for b in range(groups):
+                tiled_ref[k * groups + b, zx] = out_ref[k, pl.ds(b * 8 * rows + zx, 8, stride=rows), :]
+        return carry
+
+    lax.fori_loop(0, rows, to_tiled, 0)
+
 
 def krylov_basis(v0, terms, diagonal):
     rhs, nz, bx, by = v0.shape
@@ -289,10 +299,11 @@
     vmem = pl.BlockSpec(memory_space=pltpu.VMEM)
     out = pl.pallas_call(
         lambda *refs: krylov_kernel(nx, ny, bx, *refs),
-        out_shape=jax.ShapeDtypeStruct((S + 1, cells, by), jnp.float32),
+        out_shape=jax.ShapeDtypeStruct(((S + 1) * rhs // 8, nz * bx, 8, by), jnp.float32),
         in_specs=[vmem] * 3,
         out_specs=vmem,
         scratch_shapes=[
+            pltpu.VMEM((S + 1, cells, by), jnp.float32),
             pltpu.VMEM((cells, by), jnp.float32),
             pltpu.VMEM((2, cells // bx, by), jnp.float32),
             pltpu.VMEM((8, cells), jnp.float32),
@@ -304,7 +315,7 @@
         compiler_params=pltpu.CompilerParams(collective_id=3, has_side_effects=True),
         name="krylov_basis",
     )(v0.reshape(cells, by), jnp.stack(terms).reshape(6, nz * bx, by), diagonal.reshape(nz * bx, by))
-    return out.reshape(S + 1, rhs, nz, bx, by)
+    return out.transpose(0, 2, 1, 3).reshape(BASIS, -1)
 
 
 def face_terms(padded, storage):
@@ -349,7 +360,7 @@
     solution = jnp.zeros(shape, jnp.float32)
     residual = pumping / diagonal
     for restart in range(CYCLES):
-        stacked = krylov_basis(residual, terms, diagonal).reshape(BASIS, -1)
+        stacked = krylov_basis(residual, terms, diagonal)
         local_gram = jnp.dot(stacked, stacked.T, precision=hp)
         gram_all = gram_sum(local_gram)
         y, coeffs = small_solve(gram_all)

time: 326 us -> 335 us (1.028)
  matrix products: 21 us -> 30 us
  local copies, waits for them, and re-layouts: 18 us -> 10.6 us
  Pallas kernels: 200 us -> 207 us
    dot_general x5, matrix products: 5.86 us -> 15 us  [shards(): local_gram = jnp.dot(stacked, stacked.T, precision=hp)]
    pallas_call x5, Pallas kernels: 86.8 us -> 94.4 us  [krylov_basis(): pl.pallas_call(lambda *refs: krylov_kernel(nx, ny, bx, *refs), out_shape=...]
    another operation x5 -> x0, local copies, waits for them, and re-layouts: 7.57 us -> none  [shards(): stacked = krylov_basis(residual, terms, diagonal).reshape(BASIS, -1)]
where the time goes in v10:
time: 335 us; the launch traced here: 334 us
  Pallas kernels  207 us (62%)
  other arithmetic  68.9 us (21%)
  matrix products  30 us (9%)
  starting transfers between devices  12.2 us (4%)
  local copies, waits for them, and re-layouts  10.6 us (3%)
    pallas_call x5, Pallas kernels, gram_sum(): pl.pallas_call(lambda *refs: reduce_kernel(nx, ny, *refs), out_shape=jax....  113 us
    pallas_call x5, Pallas kernels, krylov_basis(): pl.pallas_call(lambda *refs: krylov_kernel(nx, ny, bx, *refs), out_shape=...  94.4 us
    another operation x15, other arithmetic, small_solve(): lower = jnp.linalg.cholesky(normal)  32.6 us
    another operation x10, other arithmetic, small_solve(): y = jax.scipy.linalg.cho_solve((lower, True), right_side)  27.7 us
    dot_general x5, matrix products, shards(): local_gram = jnp.dot(stacked, stacked.T, precision=hp)  15 us
    ppermute x2, starting transfers between devices, halo_faces(): lax.ppermute(last, axis, up)  9.05 us
  transfers between devices with their start and end apart: 4, of which 1 were waited for; matrix products, arithmetic and copies ran while one was open for 0% of the time, Pallas kernels for 0%

profile of v10, /device:TPU:1, one launch (start us, length us, event | category | flops | bytes accessed | tf_op | source)
XLA Modules:
  0.0 333.6 jit_solution(11957528528032204999)
XLA Ops:
  0.6 0.8 fusion.133
  1.4 1.3 collective-permute-start.2
  2.7 4.7 %collective-permute-start.1 = (f32[4,1,128]{2,1,0:T(1,128)S(1)}, f32[4,1,128]{2,1,0:T(1,128)S(1)}, u32[]{:S(2)}, u32[]{:S(2)}) collective-permute-start(f32[4,1,128]{2,1,0:T(1,128)S(1)} %get-tuple-element.9), channel_id=1, source_target_pairs={{0,8},{8,16},{16,24},{24,32},{32,40},{40,48},{48,56},{56,64},{64,7... | collective-permute-start | bytes 6152 | tf_op jit(solution)/shard_map/ppermute | solution.py:35
  7.4 0.9 fusion.132
  8.2 4.4 %collective-permute-start = (f32[4,8,1]{2,1,0:T(8,128)S(1)}, f32[4,8,1]{2,1,0:T(8,128)S(1)}, u32[]{:S(2)}, u32[]{:S(2)}) collective-permute-start(f32[4,8,1]{2,1,0:T(8,128)S(1)} %get-tuple-element.6), channel_id=1, source_target_pairs={{0,1},{1,2},{2,3},{3,4},{4,5},{5,6},{6,7},{8,9},{9,10},{10,11},{11... | collective-permute-start | bytes 392 | tf_op jit(solution)/shard_map/ppermute | solution.py:35
  12.6 1.9 collective-permute-start.3
  14.6 3.1 collective-permute-done.3
  17.7 0.8 select_maximum_fusion
  18.6 0.8 bitcast_dynamic-update-slice_fusion.5
  19.4 0.8 bitcast_dynamic-update-slice_fusion.4
  20.1 1.0 add_add_fusion
  21.2 1.7 broadcast_divide_fusion
  22.9 0.8 bitcast_dynamic-update-slice_fusion.3
  23.7 0.8 bitcast_dynamic-update-slice_fusion.2
  24.5 0.9 bitcast_dynamic-update-slice_fusion.1
  25.3 0.9 bitcast_dynamic-update-slice_fusion.refs_1_
  26.8 21.2 %krylov_basis.5 = f32[10,32,8,128]{3,2,1,0:T(8,128)} custom-call(f32[512,128]{1,0:T(8,128)} %bitcast.137, f32[6,32,128]{2,1,0:T(8,128)} %copy-done.5, f32[32,128]{1,0:T(8,128)} %bitcast.138), custom_call_target="tpu_custom_call" | custom-call | tf_op jit(solution)/shard_map/krylov_basis/pallas_call | solution.py:300
  48.1 3.0 fusion.18
  51.7 23.2 %gram_allreduce.5 = f32[128,128]{1,0:T(8,128)} custom-call(f32[128,128]{1,0:T(8,128)} %pad.35.refs_0_), custom_call_target="tpu_custom_call" | custom-call | tf_op jit(solution)/shard_map/gram_allreduce/pallas_call | solution.py:169
  74.9 1.1 fusion.30
  76.6 5.8 %cholesky.89 = f32[64,64]{1,0:T(8,128)S(1)} custom-call(f32[64,64]{1,0:T(8,128)S(1)} %fusion.66), custom_call_target="Cholesky" | custom-call | tf_op jit(solution)/shard_map/jit(cholesky)/cholesky | solution.py:348
  83.8 4.9 %custom-call.11 = f32[1,64,64]{1,2,0:T(8,128)S(1)} custom-call(f32[1,64,64]{2,1,0:T(8,128)S(1)} %fusion.37), custom_call_target="InvertDiagBlocksLowerTriangular" | custom-call | tf_op jit(solution)/shard_map/jit(_cho_solve)/triangular_solve | solution.py:349
  89.4 0.8 fusion.16
  91.0 18.3 %krylov_basis.6 = f32[10,32,8,128]{3,2,1,0:T(8,128)} custom-call(f32[512,128]{1,0:T(8,128)} %reshape_reshape.12.refs_0_, f32[6,32,128]{2,1,0:T(8,128)} %copy-done.5, f32[32,128]{1,0:T(8,128)} %bitcast.139), custom_call_target="tpu_custom_call" | custom-call | tf_op jit(solution)/shard_map/krylov_basis/pallas_call | solution.py:300
  109.3 3.0 fusion.14
  112.9 22.5 %gram_allreduce.6 = f32[128,128]{1,0:T(8,128)} custom-call(f32[128,128]{1,0:T(8,128)} %pad.36.refs_0_), custom_call_target="tpu_custom_call" | custom-call | tf_op jit(solution)/shard_map/gram_allreduce/pallas_call | solution.py:169
  135.5 1.1 fusion.28
  137.1 5.8 %cholesky.100 = f32[64,64]{1,0:T(8,128)S(1)} custom-call(f32[64,64]{1,0:T(8,128)S(1)} %fusion.61), custom_call_target="Cholesky" | custom-call | tf_op jit(solution)/shard_map/jit(cholesky)/cholesky | solution.py:348
  144.3 4.9 %custom-call.12 = f32[1,64,64]{1,2,0:T(8,128)S(1)} custom-call(f32[1,64,64]{2,1,0:T(8,128)S(1)} %fusion.38), custom_call_target="InvertDiagBlocksLowerTriangular" | custom-call | tf_op jit(solution)/shard_map/jit(_cho_solve)/triangular_solve | solution.py:349
  151.5 18.3 %krylov_basis.7 = f32[10,32,8,128]{3,2,1,0:T(8,128)} custom-call(f32[512,128]{1,0:T(8,128)} %reshape_reshape.13.refs_0_, f32[6,32,128]{2,1,0:T(8,128)} %copy-done.5, f32[32,128]{1,0:T(8,128)} %bitcast.140), custom_call_target="tpu_custom_call" | custom-call | tf_op jit(solution)/shard_map/krylov_basis/pallas_call | solution.py:300
  169.8 3.0 fusion.10
  173.4 22.4 %gram_allreduce.7 = f32[128,128]{1,0:T(8,128)} custom-call(f32[128,128]{1,0:T(8,128)} %pad.37.refs_0_), custom_call_target="tpu_custom_call" | custom-call | tf_op jit(solution)/shard_map/gram_allreduce/pallas_call | solution.py:169
  195.9 1.1 fusion.26
  197.5 5.8 %cholesky.111 = f32[64,64]{1,0:T(8,128)S(1)} custom-call(f32[64,64]{1,0:T(8,128)S(1)} %fusion.56), custom_call_target="Cholesky" | custom-call | tf_op jit(solution)/shard_map/jit(cholesky)/cholesky | solution.py:348
  204.7 4.9 %custom-call.13 = f32[1,64,64]{1,2,0:T(8,128)S(1)} custom-call(f32[1,64,64]{2,1,0:T(8,128)S(1)} %fusion.39), custom_call_target="InvertDiagBlocksLowerTriangular" | custom-call | tf_op jit(solution)/shard_map/jit(_cho_solve)/triangular_solve | solution.py:349
  211.9 18.3 %krylov_basis.8 = f32[10,32,8,128]{3,2,1,0:T(8,128)} custom-call(f32[512,128]{1,0:T(8,128)} %reshape_reshape.14.refs_0_, f32[6,32,128]{2,1,0:T(8,128)} %copy-done.5, f32[32,128]{1,0:T(8,128)} %bitcast.141), custom_call_target="tpu_custom_call" | custom-call | tf_op jit(solution)/shard_map/krylov_basis/pallas_call | solution.py:300
  230.2 3.0 fusion.6
  233.9 22.5 %gram_allreduce.8 = f32[128,128]{1,0:T(8,128)} custom-call(f32[128,128]{1,0:T(8,128)} %pad.38.refs_0_), custom_call_target="tpu_custom_call" | custom-call | tf_op jit(solution)/shard_map/gram_allreduce/pallas_call | solution.py:169
  256.4 1.1 fusion.24
  258.0 5.8 %cholesky.122 = f32[64,64]{1,0:T(8,128)S(1)} custom-call(f32[64,64]{1,0:T(8,128)S(1)} %fusion.51), custom_call_target="Cholesky" | custom-call | tf_op jit(solution)/shard_map/jit(cholesky)/cholesky | solution.py:348
  265.2 4.9 %custom-call.14 = f32[1,64,64]{1,2,0:T(8,128)S(1)} custom-call(f32[1,64,64]{2,1,0:T(8,128)S(1)} %fusion.40), custom_call_target="InvertDiagBlocksLowerTriangular" | custom-call | tf_op jit(solution)/shard_map/jit(_cho_solve)/triangular_solve | solution.py:349
  272.4 18.3 %krylov_basis.9 = f32[10,32,8,128]{3,2,1,0:T(8,128)} custom-call(f32[512,128]{1,0:T(8,128)} %reshape_reshape.15.refs_0_, f32[6,32,128]{2,1,0:T(8,128)} %copy-done.5, f32[32,128]{1,0:T(8,128)} %bitcast.142), custom_call_target="tpu_custom_call" | custom-call | tf_op jit(solution)/shard_map/krylov_basis/pallas_call | solution.py:300
  290.7 3.0 fusion.2
  294.4 22.4 %gram_allreduce.9 = f32[128,128]{1,0:T(8,128)} custom-call(f32[128,128]{1,0:T(8,128)} %pad.39.refs_0_), custom_call_target="tpu_custom_call" | custom-call | tf_op jit(solution)/shard_map/gram_allreduce/pallas_call | solution.py:169
  316.8 1.1 fusion.22
  318.4 5.8 %cholesky.133 = f32[64,64]{1,0:T(8,128)S(1)} custom-call(f32[64,64]{1,0:T(8,128)S(1)} %fusion.46), custom_call_target="Cholesky" | custom-call | tf_op jit(solution)/shard_map/jit(cholesky)/cholesky | solution.py:348
  325.6 4.9 %custom-call.15 = f32[1,64,64]{1,2,0:T(8,128)S(1)} custom-call(f32[1,64,64]{2,1,0:T(8,128)S(1)} %fusion.41), custom_call_target="InvertDiagBlocksLowerTriangular" | custom-call | tf_op jit(solution)/shard_map/jit(_cho_solve)/triangular_solve | solution.py:349
  332.1 0.8 copy.11
  (89 shorter events, 23.7 us)
Async XLA Ops:
  1.4 16.3 %collective-permute-start.2 = (f32[4,1,128]{2,1,0:T(1,128)S(1)}, f32[4,1,128]{2,1,0:T(1,128)S(1)}, u32[]{:S(2)}, u32[]{:S(2)}) collective-permute-start(f32[4,1,128]{2,1,0:T(1,128)S(1)} %get-tuple-element.8), channel_id=1, source_target_pairs={{8,0},{16,8},{24,16},{32,24},{40,32},{48,40},{56,48},{64,56},{72,6... | collective-permute-start | bytes 6152 | tf_op jit(solution)/shard_map/ppermute | solution.py:35
  2.7 15.0 %collective-permute-start.1 = (f32[4,1,128]{2,1,0:T(1,128)S(1)}, f32[4,1,128]{2,1,0:T(1,128)S(1)}, u32[]{:S(2)}, u32[]{:S(2)}) collective-permute-start(f32[4,1,128]{2,1,0:T(1,128)S(1)} %get-tuple-element.9), channel_id=1, source_target_pairs={{0,8},{8,16},{16,24},{24,32},{32,40},{40,48},{48,56},{56,64},{64,7... | collective-permute-start | bytes 6152 | tf_op jit(solution)/shard_map/ppermute | solution.py:35
  8.2 6.3 %collective-permute-start = (f32[4,8,1]{2,1,0:T(8,128)S(1)}, f32[4,8,1]{2,1,0:T(8,128)S(1)}, u32[]{:S(2)}, u32[]{:S(2)}) collective-permute-start(f32[4,8,1]{2,1,0:T(8,128)S(1)} %get-tuple-element.6), channel_id=1, source_target_pairs={{0,1},{1,2},{2,3},{3,4},{4,5},{5,6},{6,7},{8,9},{9,10},{10,11},{11... | collective-permute-start | bytes 392 | tf_op jit(solution)/shard_map/ppermute | solution.py:35
  12.6 5.1 %collective-permute-start.3 = (f32[4,8,1]{2,1,0:T(8,128)S(1)}, f32[4,8,1]{2,1,0:T(8,128)S(1)}, u32[]{:S(2)}, u32[]{:S(2)}) collective-permute-start(f32[4,8,1]{2,1,0:T(8,128)S(1)} %get-tuple-element.7), channel_id=1, source_target_pairs={{1,0},{2,1},{3,2},{4,3},{5,4},{6,5},{7,6},{9,8},{10,9},{11,10},{12... | collective-permute-start | bytes 392 | tf_op jit(solution)/shard_map/ppermute | solution.py:35
  21.2 5.1 %copy-start.6 = (f32[4,8,128]{2,1,0:T(8,128)}, f32[4,8,128]{2,1,0:T(8,128)S(1)}, u32[]{:S(2)}) copy-start(f32[4,8,128]{2,1,0:T(8,128)S(1)} %add_add_fusion) | copy-start | bytes 49156
  26.2 0.6 copy-start.5
  48.1 41.3 %copy-start.1 = (f32[10,32,8,128]{3,2,1,0:T(8,128)S(1)}, f32[10,32,8,128]{3,2,1,0:T(8,128)}, u32[]{:S(2)}) copy-start(f32[10,32,8,128]{3,2,1,0:T(8,128)} %krylov_basis.5) | copy-start | bytes 3932164
  109.3 40.7 %copy-start.2 = (f32[10,32,8,128]{3,2,1,0:T(8,128)S(1)}, f32[10,32,8,128]{3,2,1,0:T(8,128)}, u32[]{:S(2)}) copy-start(f32[10,32,8,128]{3,2,1,0:T(8,128)} %krylov_basis.6) | copy-start | bytes 3932164
  169.8 40.6 %copy-start.3 = (f32[10,32,8,128]{3,2,1,0:T(8,128)S(1)}, f32[10,32,8,128]{3,2,1,0:T(8,128)}, u32[]{:S(2)}) copy-start(f32[10,32,8,128]{3,2,1,0:T(8,128)} %krylov_basis.7) | copy-start | bytes 3932164
  230.2 40.6 %copy-start.4 = (f32[10,32,8,128]{3,2,1,0:T(8,128)S(1)}, f32[10,32,8,128]{3,2,1,0:T(8,128)}, u32[]{:S(2)}) copy-start(f32[10,32,8,128]{3,2,1,0:T(8,128)} %krylov_basis.8) | copy-start | bytes 3932164
  290.7 40.6 %copy-start = (f32[10,32,8,128]{3,2,1,0:T(8,128)S(1)}, f32[10,32,8,128]{3,2,1,0:T(8,128)}, u32[]{:S(2)}) copy-start(f32[10,32,8,128]{3,2,1,0:T(8,128)} %krylov_basis.9) | copy-start | bytes 3932164

commit v11 on v9

--- a/solution.py
+++ b/solution.py
@@ -164,7 +164,7 @@
     pad = 128
     py, px = pad // ny, pad // nx
     f32 = jnp.float32
-    wide = jnp.pad(local_gram, ((0, pad - size), (0, pad - size)))
+    wide = jnp.zeros((pad, pad), f32).at[:size, :size].set(local_gram)
     vmem = pl.BlockSpec(memory_space=pltpu.VMEM)
     total = pl.pallas_call(
         lambda *refs: reduce_kernel(nx, ny, *refs),

time: 326 us -> 326 us (level)
  no operation moved by 1% of the time
where the time goes in v11:
time: 326 us; the launch traced here: 324 us
  Pallas kernels  200 us (61%)
  other arithmetic  68.9 us (21%)
  matrix products  21 us (6%)
  local copies, waits for them, and re-layouts  18 us (6%)
  starting transfers between devices  12.2 us (4%)
    pallas_call x5, Pallas kernels, gram_sum(): pl.pallas_call(lambda *refs: reduce_kernel(nx, ny, *refs), out_shape=jax....  113 us
    pallas_call x5, Pallas kernels, krylov_basis(): pl.pallas_call(lambda *refs: krylov_kernel(nx, ny, bx, *refs), out_shape=...  86.8 us
    another operation x15, other arithmetic, small_solve(): lower = jnp.linalg.cholesky(normal)  32.6 us
    another operation x10, other arithmetic, small_solve(): y = jax.scipy.linalg.cho_solve((lower, True), right_side)  27.7 us
    ppermute x2, starting transfers between devices, halo_faces(): lax.ppermute(last, axis, up)  9.05 us
    another operation x5, local copies, waits for them, and re-layouts, shards(): stacked = krylov_basis(residual, terms, diagonal).reshape(BASIS, -1)  7.57 us
  transfers between devices with their start and end apart: 4, of which 1 were waited for; matrix products, arithmetic and copies ran while one was open for 0% of the time, Pallas kernels for 0%

profile of v11, /device:TPU:1, one launch (start us, length us, event | category | flops | bytes accessed | tf_op | source)
XLA Modules:
  0.0 324.4 jit_solution(2970340828266186835)
XLA Ops:
  1.4 1.3 collective-permute-start.2
  2.7 4.7 %collective-permute-start.1 = (f32[4,1,128]{2,1,0:T(1,128)S(1)}, f32[4,1,128]{2,1,0:T(1,128)S(1)}, u32[]{:S(2)}, u32[]{:S(2)}) collective-permute-start(f32[4,1,128]{2,1,0:T(1,128)S(1)} %get-tuple-element.69), channel_id=1, source_target_pairs={{0,8},{8,16},{16,24},{24,32},{32,40},{40,48},{48,56},{56,64},{64,7... | collective-permute-start | bytes 6152 | tf_op jit(solution)/shard_map/ppermute | solution.py:35
  7.4 0.9 fusion.117
  8.2 4.4 %collective-permute-start = (f32[4,8,1]{2,1,0:T(8,128)S(1)}, f32[4,8,1]{2,1,0:T(8,128)S(1)}, u32[]{:S(2)}, u32[]{:S(2)}) collective-permute-start(f32[4,8,1]{2,1,0:T(8,128)S(1)} %get-tuple-element.66), channel_id=1, source_target_pairs={{0,1},{1,2},{2,3},{3,4},{4,5},{5,6},{6,7},{8,9},{9,10},{10,11},{11... | collective-permute-start | bytes 392 | tf_op jit(solution)/shard_map/ppermute | solution.py:35
  12.6 1.9 collective-permute-start.3
  14.6 3.1 collective-permute-done.3
  17.7 0.8 select_maximum_fusion
  20.1 1.0 add_add_fusion
  21.2 1.7 broadcast_divide_fusion
  22.9 0.8 bitcast_dynamic-update-slice_fusion.3
  23.7 0.8 bitcast_dynamic-update-slice_fusion.2
  24.5 0.9 bitcast_dynamic-update-slice_fusion.1
  25.3 0.9 bitcast_dynamic-update-slice_fusion.refs_1_
  26.8 19.7 %krylov_basis.5 = f32[5,512,128]{2,1,0:T(8,128)} custom-call(f32[512,128]{1,0:T(8,128)} %bitcast.117, f32[6,32,128]{2,1,0:T(8,128)} %copy-done, f32[32,128]{1,0:T(8,128)} %bitcast.118), custom_call_target="tpu_custom_call" | custom-call | tf_op jit(solution)/shard_map/krylov_basis/pallas_call | solution.py:290
  46.6 1.5 reshape_reshape.27
  48.1 1.2 fusion.119
  49.9 23.2 %gram_allreduce.5 = f32[128,128]{1,0:T(8,128)} custom-call(f32[128,128]{1,0:T(8,128)} %scatter.16.refs_0_), custom_call_target="tpu_custom_call" | custom-call | tf_op jit(solution)/shard_map/gram_allreduce/pallas_call | solution.py:169
  73.1 1.1 fusion.10
  74.8 5.8 %cholesky.89 = f32[64,64]{1,0:T(8,128)S(1)} custom-call(f32[64,64]{1,0:T(8,128)S(1)} %fusion.46), custom_call_target="Cholesky" | custom-call | tf_op jit(solution)/shard_map/jit(cholesky)/cholesky | solution.py:337
  81.9 4.9 %custom-call.11 = f32[1,64,64]{1,2,0:T(8,128)S(1)} custom-call(f32[1,64,64]{2,1,0:T(8,128)S(1)} %fusion.17), custom_call_target="InvertDiagBlocksLowerTriangular" | custom-call | tf_op jit(solution)/shard_map/jit(_cho_solve)/triangular_solve | solution.py:338
  89.1 16.8 %krylov_basis.6 = f32[5,512,128]{2,1,0:T(8,128)} custom-call(f32[512,128]{1,0:T(8,128)} %reshape_reshape.28.refs_0_, f32[6,32,128]{2,1,0:T(8,128)} %copy-done, f32[32,128]{1,0:T(8,128)} %bitcast.119), custom_call_target="tpu_custom_call" | custom-call | tf_op jit(solution)/shard_map/krylov_basis/pallas_call | solution.py:290
  105.9 1.5 reshape_reshape.29
  107.4 1.2 fusion.120
  109.3 22.5 %gram_allreduce.6 = f32[128,128]{1,0:T(8,128)} custom-call(f32[128,128]{1,0:T(8,128)} %scatter.19.refs_0_), custom_call_target="tpu_custom_call" | custom-call | tf_op jit(solution)/shard_map/gram_allreduce/pallas_call | solution.py:169
  131.8 1.1 fusion.8
  133.4 5.8 %cholesky.100 = f32[64,64]{1,0:T(8,128)S(1)} custom-call(f32[64,64]{1,0:T(8,128)S(1)} %fusion.41), custom_call_target="Cholesky" | custom-call | tf_op jit(solution)/shard_map/jit(cholesky)/cholesky | solution.py:337
  140.6 4.9 %custom-call.12 = f32[1,64,64]{1,2,0:T(8,128)S(1)} custom-call(f32[1,64,64]{2,1,0:T(8,128)S(1)} %fusion.18), custom_call_target="InvertDiagBlocksLowerTriangular" | custom-call | tf_op jit(solution)/shard_map/jit(_cho_solve)/triangular_solve | solution.py:338
  147.8 16.7 %krylov_basis.7 = f32[5,512,128]{2,1,0:T(8,128)} custom-call(f32[512,128]{1,0:T(8,128)} %reshape_reshape.30.refs_0_, f32[6,32,128]{2,1,0:T(8,128)} %copy-done, f32[32,128]{1,0:T(8,128)} %bitcast.120), custom_call_target="tpu_custom_call" | custom-call | tf_op jit(solution)/shard_map/krylov_basis/pallas_call | solution.py:290
  164.6 1.5 reshape_reshape.31
  166.1 1.2 fusion.121
  167.9 22.5 %gram_allreduce.7 = f32[128,128]{1,0:T(8,128)} custom-call(f32[128,128]{1,0:T(8,128)} %scatter.20.refs_0_), custom_call_target="tpu_custom_call" | custom-call | tf_op jit(solution)/shard_map/gram_allreduce/pallas_call | solution.py:169
  190.4 1.1 fusion.6
  192.0 5.8 %cholesky.111 = f32[64,64]{1,0:T(8,128)S(1)} custom-call(f32[64,64]{1,0:T(8,128)S(1)} %fusion.36), custom_call_target="Cholesky" | custom-call | tf_op jit(solution)/shard_map/jit(cholesky)/cholesky | solution.py:337
  199.2 4.9 %custom-call.13 = f32[1,64,64]{1,2,0:T(8,128)S(1)} custom-call(f32[1,64,64]{2,1,0:T(8,128)S(1)} %fusion.19), custom_call_target="InvertDiagBlocksLowerTriangular" | custom-call | tf_op jit(solution)/shard_map/jit(_cho_solve)/triangular_solve | solution.py:338
  206.4 16.8 %krylov_basis.8 = f32[5,512,128]{2,1,0:T(8,128)} custom-call(f32[512,128]{1,0:T(8,128)} %reshape_reshape.32.refs_0_, f32[6,32,128]{2,1,0:T(8,128)} %copy-done, f32[32,128]{1,0:T(8,128)} %bitcast.121), custom_call_target="tpu_custom_call" | custom-call | tf_op jit(solution)/shard_map/krylov_basis/pallas_call | solution.py:290
  223.2 1.5 reshape_reshape.33
  224.7 1.2 fusion.122
  226.5 22.5 %gram_allreduce.8 = f32[128,128]{1,0:T(8,128)} custom-call(f32[128,128]{1,0:T(8,128)} %scatter.21.refs_0_), custom_call_target="tpu_custom_call" | custom-call | tf_op jit(solution)/shard_map/gram_allreduce/pallas_call | solution.py:169
  249.0 1.1 fusion.4
  250.7 5.8 %cholesky.122 = f32[64,64]{1,0:T(8,128)S(1)} custom-call(f32[64,64]{1,0:T(8,128)S(1)} %fusion.31), custom_call_target="Cholesky" | custom-call | tf_op jit(solution)/shard_map/jit(cholesky)/cholesky | solution.py:337
  257.8 4.9 %custom-call.14 = f32[1,64,64]{1,2,0:T(8,128)S(1)} custom-call(f32[1,64,64]{2,1,0:T(8,128)S(1)} %fusion.20), custom_call_target="InvertDiagBlocksLowerTriangular" | custom-call | tf_op jit(solution)/shard_map/jit(_cho_solve)/triangular_solve | solution.py:338
  265.0 16.8 %krylov_basis.9 = f32[5,512,128]{2,1,0:T(8,128)} custom-call(f32[512,128]{1,0:T(8,128)} %reshape_reshape.34.refs_0_, f32[6,32,128]{2,1,0:T(8,128)} %copy-done, f32[32,128]{1,0:T(8,128)} %bitcast.122), custom_call_target="tpu_custom_call" | custom-call | tf_op jit(solution)/shard_map/krylov_basis/pallas_call | solution.py:290
  281.8 1.5 reshape_reshape.35
  283.3 1.2 fusion.123
  285.1 22.4 %gram_allreduce.9 = f32[128,128]{1,0:T(8,128)} custom-call(f32[128,128]{1,0:T(8,128)} %scatter.24.refs_0_), custom_call_target="tpu_custom_call" | custom-call | tf_op jit(solution)/shard_map/gram_allreduce/pallas_call | solution.py:169
  307.6 1.1 fusion.2
  309.2 5.8 %cholesky.133 = f32[64,64]{1,0:T(8,128)S(1)} custom-call(f32[64,64]{1,0:T(8,128)S(1)} %fusion.26), custom_call_target="Cholesky" | custom-call | tf_op jit(solution)/shard_map/jit(cholesky)/cholesky | solution.py:337
  316.4 4.9 %custom-call.15 = f32[1,64,64]{1,2,0:T(8,128)S(1)} custom-call(f32[1,64,64]{2,1,0:T(8,128)S(1)} %fusion.21), custom_call_target="InvertDiagBlocksLowerTriangular" | custom-call | tf_op jit(solution)/shard_map/jit(_cho_solve)/triangular_solve | solution.py:338
  (84 shorter events, 27.6 us)
Async XLA Ops:
  1.4 16.3 %collective-permute-start.2 = (f32[4,1,128]{2,1,0:T(1,128)S(1)}, f32[4,1,128]{2,1,0:T(1,128)S(1)}, u32[]{:S(2)}, u32[]{:S(2)}) collective-permute-start(f32[4,1,128]{2,1,0:T(1,128)S(1)} %get-tuple-element.68), channel_id=1, source_target_pairs={{8,0},{16,8},{24,16},{32,24},{40,32},{48,40},{56,48},{64,56},{72,6... | collective-permute-start | bytes 6152 | tf_op jit(solution)/shard_map/ppermute | solution.py:35
  2.7 15.0 %collective-permute-start.1 = (f32[4,1,128]{2,1,0:T(1,128)S(1)}, f32[4,1,128]{2,1,0:T(1,128)S(1)}, u32[]{:S(2)}, u32[]{:S(2)}) collective-permute-start(f32[4,1,128]{2,1,0:T(1,128)S(1)} %get-tuple-element.69), channel_id=1, source_target_pairs={{0,8},{8,16},{16,24},{24,32},{32,40},{40,48},{48,56},{56,64},{64,7... | collective-permute-start | bytes 6152 | tf_op jit(solution)/shard_map/ppermute | solution.py:35
  8.2 6.3 %collective-permute-start = (f32[4,8,1]{2,1,0:T(8,128)S(1)}, f32[4,8,1]{2,1,0:T(8,128)S(1)}, u32[]{:S(2)}, u32[]{:S(2)}) collective-permute-start(f32[4,8,1]{2,1,0:T(8,128)S(1)} %get-tuple-element.66), channel_id=1, source_target_pairs={{0,1},{1,2},{2,3},{3,4},{4,5},{5,6},{6,7},{8,9},{9,10},{10,11},{11... | collective-permute-start | bytes 392 | tf_op jit(solution)/shard_map/ppermute | solution.py:35
  12.6 5.1 %collective-permute-start.3 = (f32[4,8,1]{2,1,0:T(8,128)S(1)}, f32[4,8,1]{2,1,0:T(8,128)S(1)}, u32[]{:S(2)}, u32[]{:S(2)}) collective-permute-start(f32[4,8,1]{2,1,0:T(8,128)S(1)} %get-tuple-element.67), channel_id=1, source_target_pairs={{1,0},{2,1},{3,2},{4,3},{5,4},{6,5},{7,6},{9,8},{10,9},{11,10},{12... | collective-permute-start | bytes 392 | tf_op jit(solution)/shard_map/ppermute | solution.py:35
  21.2 5.1 %copy-start.1 = (f32[4,8,128]{2,1,0:T(8,128)}, f32[4,8,128]{2,1,0:T(8,128)S(1)}, u32[]{:S(2)}) copy-start(f32[4,8,128]{2,1,0:T(8,128)S(1)} %add_add_fusion) | copy-start | bytes 49156
  26.2 0.6 copy-start
